TPU v7x, 32 devices: a whole 2x2x4 slice. The times are simulated.
32 devices in a mesh: gx: 4 (over z), gy: 4 (over y, x), gz: 2 (over core).
Axes of the slice: x: 2, y: 2, z: 4, core: 2. Of those that a mesh axis runs over, the one named last changes fastest.
Arguments:
- e_field: float32 [3, 8, 128, 512], P(None, 'gz', 'gx', 'gy'), may hold values from -6 to 6
- h_field: float32 [3, 8, 128, 512], P(None, 'gz', 'gx', 'gy'), may hold values from -6 to 6
- pole_current: float32 [3, 8, 128, 512], P(None, 'gz', 'gx', 'gy'), may hold values from -6 to 6
- material: int32 [8, 128, 512], P('gz', 'gx', 'gy'), may hold values from 0 to 3
- pole_table: float32 [3, 4], replicated, may hold values from 0.2 to 0.9
- cotangent: float32 [16, 8, 4096], P(None, None, ('gx', 'gy', 'gz')), may hold values from -6 to 6
- cosines: float32 [2, 4096], P(None, ('gx', 'gy', 'gz')), may hold values from -0.7 to 0.7
- wavenumber: float32 [16], replicated, may hold values from 0.6 to 0.8
- time_phase: float32 [16], replicated, may hold values from -3.140625 to 3.140625
Outputs:
- e_next: float32 [3, 8, 128, 512], P(None, 'gz', 'gx', 'gy')
- h_next: float32 [3, 8, 128, 512], P(None, 'gz', 'gx', 'gy')
- pole_next: float32 [3, 8, 128, 512], P(None, 'gz', 'gx', 'gy')
All inputs are finite; a program needn't handle non-finite values.
Results may differ from a plain program's by a relative error of at most 0.0003.
Values sent between devices are 32-bit elements; how exact they have to be, the bound alone decides.
No kernel may reach another device: no remote copies, remote signals or barrier semaphores. Data moves between devices by JAX's collectives and lax.ppermute only.
A program may use at most 64 MiB of HBM per device.

v0:
```python
import math

import jax
import jax.numpy as jnp
from jax import lax
from jax.sharding import PartitionSpec as P

FREQS = 16
DIRS = 4096
NPOLE = 4


courant = 0.5


def from_behind(array, axis, by):
    size = lax.axis_size(axis)
    pairs = [(i, i + by) for i in range(size) if 0 <= i + by < size]
    return lax.ppermute(array, axis, pairs)


def surface_source(cotangent, cosines, wavenumber, time_phase, xs, ys):
    count = cotangent.shape[2]
    rows_x = xs.shape[0]
    rows_y = ys.shape[0]

    def one_freq(total, freq):
        wave = wavenumber[freq]
        along_x = wave * cosines[0]
        along_y = wave * cosines[1]
        phase_x = xs[:, None] * along_x[None, :] - time_phase[freq]
        phase_y = ys[:, None] * along_y[None, :]
        cos_x = jnp.cos(phase_x)[None]
        sin_x = jnp.sin(phase_x)[None]
        weights = cotangent[freq]
        real_part = weights[0::2][:, None, :]
        imag_part = weights[1::2][:, None, :]
        first = real_part * cos_x - imag_part * sin_x
        second = -(real_part * sin_x + imag_part * cos_x)
        left = jnp.concatenate([first, second], axis=2).reshape(4 * rows_x, 2 * count)
        right = jnp.concatenate([jnp.cos(phase_y), jnp.sin(phase_y)], axis=1).T
        part = jnp.dot(
            left, right, preferred_element_type=jnp.float32, precision=lax.Precision.HIGHEST
        )
        return (total + part.reshape(4, rows_x, rows_y), None)

    start = jnp.zeros((4, rows_x, rows_y), jnp.float32)
    total, _ = lax.scan(one_freq, start, jnp.arange(cotangent.shape[0], dtype=jnp.int32))
    return total


def ahead(value, nearby, axis):
    rest = lax.slice_in_dim(value, 1, value.shape[axis], axis=axis)
    return jnp.concatenate([rest, nearby], axis) - value


def behind(value, nearby, axis):
    rest = lax.slice_in_dim(value, 0, value.shape[axis] - 1, axis=axis)
    return value - jnp.concatenate([nearby, rest], axis)


def local(
    e_field, h_field, pole_current, material, pole_table, cotangent, cosines, wavenumber, time_phase
):
    depth, width_x, width_y = material.shape
    scale = 1.0 / math.sqrt(DIRS * FREQS)
    anchor_x = (lax.axis_index("gx") * width_x).astype(jnp.float32)
    anchor_y = (lax.axis_index("gy") * width_y).astype(jnp.float32)
    ys = anchor_y + jnp.arange(width_y).astype(jnp.float32)
    first_cot, first_cos = (
        lax.all_gather(cotangent, "gx", axis=2, tiled=True),
        lax.all_gather(cosines, "gx", axis=1, tiled=True),
    )
    band_cot, band_cos = (
        lax.all_gather(first_cot, "gy", axis=2, tiled=True),
        lax.all_gather(first_cos, "gy", axis=1, tiled=True),
    )
    xs = anchor_x + jnp.arange(width_x).astype(jnp.float32)
    partial_value = surface_source(band_cot, band_cos, wavenumber, time_phase, xs, ys)
    source = lax.psum(partial_value, "gz") * scale
    is_top = lax.axis_index("gz") == lax.axis_size("gz") - 1
    top = ((jnp.arange(depth) == depth - 1) & is_top).astype(jnp.float32)[:, None, None]
    next_x = from_behind(e_field[1:3, :, :1, :], "gx", -1)
    next_y = from_behind(e_field[0::2, :, :, :1], "gy", -1)
    next_z = from_behind(e_field[0:2, :1], "gz", -1)
    ex, ey, ez = (e_field[0], e_field[1], e_field[2])
    curl_x = ahead(ez, next_y[1], 2) - ahead(ey, next_z[1], 0)
    curl_y = ahead(ex, next_z[0], 0) - ahead(ez, next_x[1], 1)
    curl_z = ahead(ey, next_x[0], 1) - ahead(ex, next_y[0], 2)
    hx = h_field[0] - courant * curl_x - courant * top * source[2][None]
    hy = h_field[1] - courant * curl_y - courant * top * source[3][None]
    hz = h_field[2] - courant * curl_z
    h_next = jnp.stack([hx, hy, hz])
    prev_x = from_behind(h_next[1:3, :, -1:, :], "gx", 1)
    prev_y = from_behind(h_next[0::2, :, :, -1:], "gy", 1)
    prev_z = from_behind(h_next[0:2, -1:], "gz", 1)
    chosen = (material[None] == jnp.arange(NPOLE, dtype=jnp.int32)[:, None, None, None]).astype(
        jnp.float32
    )
    decay = jnp.sum(chosen * pole_table[0][:, None, None, None], axis=0)
    drive = jnp.sum(chosen * pole_table[1][:, None, None, None], axis=0)
    coef = jnp.sum(chosen * pole_table[2][:, None, None, None], axis=0)
    pole_next = decay[None] * pole_current + drive[None] * e_field
    side_x = behind(hz, prev_y[1], 2) - behind(hy, prev_z[1], 0)
    side_y = behind(hx, prev_z[0], 0) - behind(hz, prev_x[1], 1)
    side_z = behind(hy, prev_x[0], 1) - behind(hx, prev_y[0], 2)
    curl_h = jnp.stack([side_x, side_y, side_z])
    inject = jnp.stack([top * source[0][None], top * source[1][None], jnp.zeros_like(ex)])
    e_next = (
        e_field + coef[None] * (curl_h - 0.5 * (pole_next + pole_current)) - coef[None] * inject
    )
    return (e_next, h_next, pole_next)


def solution(mesh):
    in_specs = (
        P(None, "gz", "gx", "gy"),
        P(None, "gz", "gx", "gy"),
        P(None, "gz", "gx", "gy"),
        P("gz", "gx", "gy"),
        P(),
        P(None, None, ("gx", "gy", "gz")),
        P(None, ("gx", "gy", "gz")),
        P(),
        P(),
    )
    out_specs = (P(None, "gz", "gx", "gy"), P(None, "gz", "gx", "gy"), P(None, "gz", "gx", "gy"))
    return jax.shard_map(local, mesh=mesh, in_specs=in_specs, out_specs=out_specs, check_vma=False)
```

profile of v0, /device:TPU:1, one launch (start us, length us, event | category | flops | bytes accessed | tf_op | source)
XLA Modules:
  0.0 364.8 jit_solution(2642953224590001199)
XLA Ops:
  7.2 14.6 %all_gather.12 = f32[16,8,512]{2,1,0:T(8,128)} all-gather(f32[16,8,128]{2,1,0:T(8,128)} %param.16), channel_id=1, replica_groups=mesh['gx'=4,'gy'=4,'gz'=2] {'gx'}, dimensions={2}, use_global_device_ids=true | all-gather | bytes 327680 | tf_op jit(solution)/shard_map/all_gather | solution.py:71
  25.5 5.5 %collective-permute-start.2 = (f32[2,1,32,128]{3,2,1,0:T(8,128)}, f32[2,1,32,128]{3,2,1,0:T(8,128)}, u32[]{:S(2)}, u32[]{:S(2)}) collective-permute-start(f32[2,1,32,128]{3,2,1,0:T(8,128)} %slice.166), channel_id=1, source_target_pairs={{1,0},{3,2},{5,4},{7,6},{9,8},{11,10},{13,12},{15,14},{17,16},{19,... | collective-permute-start | bytes 98312 | tf_op jit(solution)/shard_map/ppermute | solution.py:19
  33.1 8.2 %all_gather.14 = f32[2,512]{1,0:T(2,128)S(1)} all-gather(f32[2,128]{1,0:T(2,128)} %param.17), channel_id=1, replica_groups=mesh['gx'=4,'gy'=4,'gz'=2] {'gx'}, dimensions={1}, use_global_device_ids=true | all-gather | bytes 5120 | tf_op jit(solution)/shard_map/all_gather | solution.py:72
  41.3 9.4 %all_gather.15 = f32[2,2048]{1,0:T(2,128)S(1)} all-gather(f32[2,512]{1,0:T(2,128)S(1)} %all_gather.14), channel_id=1, replica_groups=mesh['gx'=4,'gy'=4,'gz'=2] {'gy'}, dimensions={1}, use_global_device_ids=true | all-gather | bytes 20480 | tf_op jit(solution)/shard_map/all_gather | solution.py:76
  58.2 268.2 %while.11 = (s32[]{:T(128)}, f32[4,32,128]{2,1,0:T(8,128)S(1)}, s32[16]{0:T(128)S(1)}, f32[16,8,2048]{2,1,0:T(8,128)}, f32[16]{0:T(128)}, /*index=5*/f32[2,2048]...) while((s32[]{:T(128)}, f32[4,32,128]{2,1,0:T(8,128)S(1)}, ...), condition=%wide.region_2.3_spmd.clone, body=%wide.region_1.2_spmd.clone.sunk | while | flops 808620352 | bytes 9947153 | solution.py:48
  68.2 3.7 %multiply_cosine_fusion.2 = (f32[128,2048]{1,0:T(8,128)S(1)}, f32[128,2048]{1,0:T(8,128)S(1)}) fusion(f32[2048]{0:T(1024)S(1)} %bitcast.105, f32[128]{0:T(128)S(1)} %convert_add_fusion.4), kind=kLoop, calls=%fused_computation.10.clone.1 | loop fusion | flops 262144 | bytes 2105856 | tf_op jit(solution)/shard_map/while/body/eval_jaxpr/cos | solution.py:41
  71.9 3.1 fusion.57
  84.9 3.7 %multiply_cosine_fusion.2 = (f32[128,2048]{1,0:T(8,128)S(1)}, f32[128,2048]{1,0:T(8,128)S(1)}) fusion(f32[2048]{0:T(1024)S(1)} %bitcast.105, f32[128]{0:T(128)S(1)} %convert_add_fusion.4), kind=kLoop, calls=%fused_computation.10.clone.1 | loop fusion | flops 262144 | bytes 2105856 | tf_op jit(solution)/shard_map/while/body/eval_jaxpr/cos | solution.py:41
  88.6 3.1 fusion.57
  101.7 3.7 %multiply_cosine_fusion.2 = (f32[128,2048]{1,0:T(8,128)S(1)}, f32[128,2048]{1,0:T(8,128)S(1)}) fusion(f32[2048]{0:T(1024)S(1)} %bitcast.105, f32[128]{0:T(128)S(1)} %convert_add_fusion.4), kind=kLoop, calls=%fused_computation.10.clone.1 | loop fusion | flops 262144 | bytes 2105856 | tf_op jit(solution)/shard_map/while/body/eval_jaxpr/cos | solution.py:41
  105.4 3.1 fusion.57
  114.6 1.7 fusion.56
  118.5 3.7 %multiply_cosine_fusion.2 = (f32[128,2048]{1,0:T(8,128)S(1)}, f32[128,2048]{1,0:T(8,128)S(1)}) fusion(f32[2048]{0:T(1024)S(1)} %bitcast.105, f32[128]{0:T(128)S(1)} %convert_add_fusion.4), kind=kLoop, calls=%fused_computation.10.clone.1 | loop fusion | flops 262144 | bytes 2105856 | tf_op jit(solution)/shard_map/while/body/eval_jaxpr/cos | solution.py:41
  122.2 3.1 fusion.57
  131.4 1.7 fusion.56
  135.2 3.7 %multiply_cosine_fusion.2 = (f32[128,2048]{1,0:T(8,128)S(1)}, f32[128,2048]{1,0:T(8,128)S(1)}) fusion(f32[2048]{0:T(1024)S(1)} %bitcast.105, f32[128]{0:T(128)S(1)} %convert_add_fusion.4), kind=kLoop, calls=%fused_computation.10.clone.1 | loop fusion | flops 262144 | bytes 2105856 | tf_op jit(solution)/shard_map/while/body/eval_jaxpr/cos | solution.py:41
  138.9 3.1 fusion.57
  148.2 1.7 fusion.56
  152.0 3.7 %multiply_cosine_fusion.2 = (f32[128,2048]{1,0:T(8,128)S(1)}, f32[128,2048]{1,0:T(8,128)S(1)}) fusion(f32[2048]{0:T(1024)S(1)} %bitcast.105, f32[128]{0:T(128)S(1)} %convert_add_fusion.4), kind=kLoop, calls=%fused_computation.10.clone.1 | loop fusion | flops 262144 | bytes 2105856 | tf_op jit(solution)/shard_map/while/body/eval_jaxpr/cos | solution.py:41
  155.7 3.1 fusion.57
  164.9 1.7 fusion.56
  168.8 3.7 %multiply_cosine_fusion.2 = (f32[128,2048]{1,0:T(8,128)S(1)}, f32[128,2048]{1,0:T(8,128)S(1)}) fusion(f32[2048]{0:T(1024)S(1)} %bitcast.105, f32[128]{0:T(128)S(1)} %convert_add_fusion.4), kind=kLoop, calls=%fused_computation.10.clone.1 | loop fusion | flops 262144 | bytes 2105856 | tf_op jit(solution)/shard_map/while/body/eval_jaxpr/cos | solution.py:41
  172.5 3.1 fusion.57
  185.5 3.7 %multiply_cosine_fusion.2 = (f32[128,2048]{1,0:T(8,128)S(1)}, f32[128,2048]{1,0:T(8,128)S(1)}) fusion(f32[2048]{0:T(1024)S(1)} %bitcast.105, f32[128]{0:T(128)S(1)} %convert_add_fusion.4), kind=kLoop, calls=%fused_computation.10.clone.1 | loop fusion | flops 262144 | bytes 2105856 | tf_op jit(solution)/shard_map/while/body/eval_jaxpr/cos | solution.py:41
  189.2 3.1 fusion.57
  202.3 3.7 %multiply_cosine_fusion.2 = (f32[128,2048]{1,0:T(8,128)S(1)}, f32[128,2048]{1,0:T(8,128)S(1)}) fusion(f32[2048]{0:T(1024)S(1)} %bitcast.105, f32[128]{0:T(128)S(1)} %convert_add_fusion.4), kind=kLoop, calls=%fused_computation.10.clone.1 | loop fusion | flops 262144 | bytes 2105856 | tf_op jit(solution)/shard_map/while/body/eval_jaxpr/cos | solution.py:41
  206.0 3.1 fusion.57
  215.2 1.7 fusion.56
  219.1 3.7 %multiply_cosine_fusion.2 = (f32[128,2048]{1,0:T(8,128)S(1)}, f32[128,2048]{1,0:T(8,128)S(1)}) fusion(f32[2048]{0:T(1024)S(1)} %bitcast.105, f32[128]{0:T(128)S(1)} %convert_add_fusion.4), kind=kLoop, calls=%fused_computation.10.clone.1 | loop fusion | flops 262144 | bytes 2105856 | tf_op jit(solution)/shard_map/while/body/eval_jaxpr/cos | solution.py:41
  222.8 3.1 fusion.57
  232.0 1.7 fusion.56
  235.8 3.7 %multiply_cosine_fusion.2 = (f32[128,2048]{1,0:T(8,128)S(1)}, f32[128,2048]{1,0:T(8,128)S(1)}) fusion(f32[2048]{0:T(1024)S(1)} %bitcast.105, f32[128]{0:T(128)S(1)} %convert_add_fusion.4), kind=kLoop, calls=%fused_computation.10.clone.1 | loop fusion | flops 262144 | bytes 2105856 | tf_op jit(solution)/shard_map/while/body/eval_jaxpr/cos | solution.py:41
  239.5 3.1 fusion.57
  248.8 1.7 fusion.56
  252.6 3.7 %multiply_cosine_fusion.2 = (f32[128,2048]{1,0:T(8,128)S(1)}, f32[128,2048]{1,0:T(8,128)S(1)}) fusion(f32[2048]{0:T(1024)S(1)} %bitcast.105, f32[128]{0:T(128)S(1)} %convert_add_fusion.4), kind=kLoop, calls=%fused_computation.10.clone.1 | loop fusion | flops 262144 | bytes 2105856 | tf_op jit(solution)/shard_map/while/body/eval_jaxpr/cos | solution.py:41
  256.3 3.1 fusion.57
  265.5 1.7 fusion.56
  269.4 3.7 %multiply_cosine_fusion.2 = (f32[128,2048]{1,0:T(8,128)S(1)}, f32[128,2048]{1,0:T(8,128)S(1)}) fusion(f32[2048]{0:T(1024)S(1)} %bitcast.105, f32[128]{0:T(128)S(1)} %convert_add_fusion.4), kind=kLoop, calls=%fused_computation.10.clone.1 | loop fusion | flops 262144 | bytes 2105856 | tf_op jit(solution)/shard_map/while/body/eval_jaxpr/cos | solution.py:41
  273.1 3.1 fusion.57
  286.1 3.7 %multiply_cosine_fusion.2 = (f32[128,2048]{1,0:T(8,128)S(1)}, f32[128,2048]{1,0:T(8,128)S(1)}) fusion(f32[2048]{0:T(1024)S(1)} %bitcast.105, f32[128]{0:T(128)S(1)} %convert_add_fusion.4), kind=kLoop, calls=%fused_computation.10.clone.1 | loop fusion | flops 262144 | bytes 2105856 | tf_op jit(solution)/shard_map/while/body/eval_jaxpr/cos | solution.py:41
  289.8 3.1 fusion.57
  302.9 3.7 %multiply_cosine_fusion.2 = (f32[128,2048]{1,0:T(8,128)S(1)}, f32[128,2048]{1,0:T(8,128)S(1)}) fusion(f32[2048]{0:T(1024)S(1)} %bitcast.105, f32[128]{0:T(128)S(1)} %convert_add_fusion.4), kind=kLoop, calls=%fused_computation.10.clone.1 | loop fusion | flops 262144 | bytes 2105856 | tf_op jit(solution)/shard_map/while/body/eval_jaxpr/cos | solution.py:41
  306.6 3.1 fusion.57
  319.7 3.7 %multiply_cosine_fusion.2 = (f32[128,2048]{1,0:T(8,128)S(1)}, f32[128,2048]{1,0:T(8,128)S(1)}) fusion(f32[2048]{0:T(1024)S(1)} %bitcast.105, f32[128]{0:T(128)S(1)} %convert_add_fusion.4), kind=kLoop, calls=%fused_computation.10.clone.1 | loop fusion | flops 262144 | bytes 2105856 | tf_op jit(solution)/shard_map/while/body/eval_jaxpr/cos | solution.py:41
  323.4 3.1 fusion.57
  327.9 16.2 %all-reduce.2.cloned.1.call-done = f32[4,32,128]{2,1,0:T(8,128)} async-done(((f32[4,32,128]{2,1,0:T(8,128)}), f32[4,32,128]{2,1,0:T(8,128)}) %all-reduce.2.cloned.1.call-update) | async-done | bytes 65552 | tf_op jit(solution)/shard_map/psum | solution.py:80
  347.4 3.4 collective-permute-start.3
  350.8 3.1 collective-permute-start.5
  (322 shorter events, 133.7 us)
Async XLA Ops:
  7.2 47.1 %copy-start = (f32[3,4,32,128]{3,2,1,0:T(8,128)S(1)}, f32[3,4,32,128]{3,2,1,0:T(8,128)}, u32[]{:S(2)}) copy-start(f32[3,4,32,128]{3,2,1,0:T(8,128)} %param.11) | copy-start | bytes 589828
  7.2 51.1 %all-gather.2.cloned.1.call-start = ((), (), s32[]{:S(2)}) async-start(), calls=%async_computation | async-start | bytes 1310720 | tf_op jit(solution)/shard_map/all_gather | solution.py:75
  21.9 322.3 %all-reduce.2.cloned.1.call-start = ((), (), s32[]{:S(2)}) async-start(), calls=%async_computation.1 | async-start | bytes 131072 | tf_op jit(solution)/shard_map/psum | solution.py:80
  22.8 34.1 %collective-permute-start.1 = (f32[2,4,32,1]{3,2,1,0:T(8,128)S(1)}, f32[2,4,32,1]{3,2,1,0:T(8,128)S(1)}, u32[]{:S(2)}, u32[]{:S(2)}) collective-permute-start(f32[2,4,32,1]{3,2,1,0:T(8,128)S(1)} %slice.159), channel_id=1, source_target_pairs={{2,0},{4,2},{6,4},{3,1},{5,3},{7,5},{10,8},{12,10},{14,12},{11,9},... | collective-permute-start | bytes 3080 | tf_op jit(solution)/shard_map/ppermute | solution.py:19
  25.5 301.6 %collective-permute-start.2 = (f32[2,1,32,128]{3,2,1,0:T(8,128)}, f32[2,1,32,128]{3,2,1,0:T(8,128)}, u32[]{:S(2)}, u32[]{:S(2)}) collective-permute-start(f32[2,1,32,128]{3,2,1,0:T(8,128)} %slice.166), channel_id=1, source_target_pairs={{1,0},{3,2},{5,4},{7,6},{9,8},{11,10},{13,12},{15,14},{17,16},{19,... | collective-permute-start | bytes 98312 | tf_op jit(solution)/shard_map/ppermute | solution.py:19
  31.8 25.8 %collective-permute-start = (f32[2,4,1,128]{3,2,1,0:T(1,128)S(1)}, f32[2,4,1,128]{3,2,1,0:T(1,128)S(1)}, u32[]{:S(2)}, u32[]{:S(2)}) collective-permute-start(f32[2,4,1,128]{3,2,1,0:T(1,128)S(1)} %slice.155), channel_id=1, source_target_pairs={{8,0},{16,8},{24,16},{9,1},{17,9},{25,17},{10,2},{18,10},{26,18},{... | collective-permute-start | bytes 12296 | tf_op jit(solution)/shard_map/ppermute | solution.py:19
  58.2 4.0 %copy-start.19 = (s32[16]{0:T(128)}, s32[16]{0:T(128)S(1)}, u32[]{:S(2)}) copy-start(s32[16]{0:T(128)S(1)} %get-tuple-element.269) | copy-start | bytes 196 | tf_op jit(solution)/shard_map/while
  71.9 3.1 copy-start.20
  75.0 4.1 %copy-start.19 = (s32[16]{0:T(128)}, s32[16]{0:T(128)S(1)}, u32[]{:S(2)}) copy-start(s32[16]{0:T(128)S(1)} %get-tuple-element.269) | copy-start | bytes 196 | tf_op jit(solution)/shard_map/while
  88.6 3.1 copy-start.20
  91.8 4.1 %copy-start.19 = (s32[16]{0:T(128)}, s32[16]{0:T(128)S(1)}, u32[]{:S(2)}) copy-start(s32[16]{0:T(128)S(1)} %get-tuple-element.269) | copy-start | bytes 196 | tf_op jit(solution)/shard_map/while
  105.4 3.1 copy-start.20
  108.5 4.1 %copy-start.19 = (s32[16]{0:T(128)}, s32[16]{0:T(128)S(1)}, u32[]{:S(2)}) copy-start(s32[16]{0:T(128)S(1)} %get-tuple-element.269) | copy-start | bytes 196 | tf_op jit(solution)/shard_map/while
  122.2 3.1 copy-start.20
  125.3 4.1 %copy-start.19 = (s32[16]{0:T(128)}, s32[16]{0:T(128)S(1)}, u32[]{:S(2)}) copy-start(s32[16]{0:T(128)S(1)} %get-tuple-element.269) | copy-start | bytes 196 | tf_op jit(solution)/shard_map/while
  138.9 3.1 copy-start.20
  142.1 4.1 %copy-start.19 = (s32[16]{0:T(128)}, s32[16]{0:T(128)S(1)}, u32[]{:S(2)}) copy-start(s32[16]{0:T(128)S(1)} %get-tuple-element.269) | copy-start | bytes 196 | tf_op jit(solution)/shard_map/while
  155.7 3.1 copy-start.20
  158.8 4.1 %copy-start.19 = (s32[16]{0:T(128)}, s32[16]{0:T(128)S(1)}, u32[]{:S(2)}) copy-start(s32[16]{0:T(128)S(1)} %get-tuple-element.269) | copy-start | bytes 196 | tf_op jit(solution)/shard_map/while
  172.5 3.1 copy-start.20
  175.6 4.1 %copy-start.19 = (s32[16]{0:T(128)}, s32[16]{0:T(128)S(1)}, u32[]{:S(2)}) copy-start(s32[16]{0:T(128)S(1)} %get-tuple-element.269) | copy-start | bytes 196 | tf_op jit(solution)/shard_map/while
  189.2 3.1 copy-start.20
  192.4 4.1 %copy-start.19 = (s32[16]{0:T(128)}, s32[16]{0:T(128)S(1)}, u32[]{:S(2)}) copy-start(s32[16]{0:T(128)S(1)} %get-tuple-element.269) | copy-start | bytes 196 | tf_op jit(solution)/shard_map/while
  206.0 3.1 copy-start.20
  209.1 4.1 %copy-start.19 = (s32[16]{0:T(128)}, s32[16]{0:T(128)S(1)}, u32[]{:S(2)}) copy-start(s32[16]{0:T(128)S(1)} %get-tuple-element.269) | copy-start | bytes 196 | tf_op jit(solution)/shard_map/while
  222.8 3.1 copy-start.20
  225.9 4.1 %copy-start.19 = (s32[16]{0:T(128)}, s32[16]{0:T(128)S(1)}, u32[]{:S(2)}) copy-start(s32[16]{0:T(128)S(1)} %get-tuple-element.269) | copy-start | bytes 196 | tf_op jit(solution)/shard_map/while
  239.5 3.1 copy-start.20
  242.7 4.1 %copy-start.19 = (s32[16]{0:T(128)}, s32[16]{0:T(128)S(1)}, u32[]{:S(2)}) copy-start(s32[16]{0:T(128)S(1)} %get-tuple-element.269) | copy-start | bytes 196 | tf_op jit(solution)/shard_map/while
  256.3 3.1 copy-start.20
  259.4 4.1 %copy-start.19 = (s32[16]{0:T(128)}, s32[16]{0:T(128)S(1)}, u32[]{:S(2)}) copy-start(s32[16]{0:T(128)S(1)} %get-tuple-element.269) | copy-start | bytes 196 | tf_op jit(solution)/shard_map/while
  276.2 4.1 %copy-start.19 = (s32[16]{0:T(128)}, s32[16]{0:T(128)S(1)}, u32[]{:S(2)}) copy-start(s32[16]{0:T(128)S(1)} %get-tuple-element.269) | copy-start | bytes 196 | tf_op jit(solution)/shard_map/while
  289.8 3.1 copy-start.20
  293.0 4.1 %copy-start.19 = (s32[16]{0:T(128)}, s32[16]{0:T(128)S(1)}, u32[]{:S(2)}) copy-start(s32[16]{0:T(128)S(1)} %get-tuple-element.269) | copy-start | bytes 196 | tf_op jit(solution)/shard_map/while
  309.7 4.1 %copy-start.19 = (s32[16]{0:T(128)}, s32[16]{0:T(128)S(1)}, u32[]{:S(2)}) copy-start(s32[16]{0:T(128)S(1)} %get-tuple-element.269) | copy-start | bytes 196 | tf_op jit(solution)/shard_map/while
  323.4 3.1 copy-start.20
  326.5 19.8 %copy-start.2 = (f32[3,4,32,128]{3,2,1,0:T(8,128)S(1)}, f32[3,4,32,128]{3,2,1,0:T(8,128)}, u32[]{:S(2)}) copy-start(f32[3,4,32,128]{3,2,1,0:T(8,128)} %param.12) | copy-start | bytes 589828
  326.5 19.8 %copy-start.8 = (f32[1,4,32,1]{3,2,1,0:T(8,128)S(1)}, f32[1,4,32,1]{3,2,1,0:T(8,128)}, u32[]{:S(2)}) copy-start(f32[1,4,32,1]{3,2,1,0:T(8,128)} %get-tuple-element.133) | copy-start | bytes 1540
  326.5 19.8 %copy-start.15 = (f32[1,4,1,128]{3,2,1,0:T(1,128)S(1)}, f32[1,4,1,128]{3,2,1,0:T(1,128)}, u32[]{:S(2)}) copy-start(f32[1,4,1,128]{3,2,1,0:T(1,128)} %get-tuple-element.160) | copy-start | bytes 6148
  346.5 8.7 %copy-start.18 = (f32[4]{0:T(128)S(1)}, f32[4]{0:T(128)}, u32[]{:S(2)}) copy-start(f32[4]{0:T(128)} %fusion.44) | copy-start | bytes 52
  347.2 9.9 %copy-start.4 = (f32[4,32,128]{2,1,0:T(8,128)S(1)}, f32[4,32,128]{2,1,0:T(8,128)}, u32[]{:S(2)}) copy-start(f32[4,32,128]{2,1,0:T(8,128)} %get-tuple-element.87) | copy-start | bytes 196612
  347.2 9.9 %copy-start.5 = (f32[4,32,128]{2,1,0:T(8,128)S(1)}, f32[4,32,128]{2,1,0:T(8,128)}, u32[]{:S(2)}) copy-start(f32[4,32,128]{2,1,0:T(8,128)} %get-tuple-element.88) | copy-start | bytes 196612
  347.2 9.9 %copy-start.6 = (f32[4,32,128]{2,1,0:T(8,128)S(1)}, f32[4,32,128]{2,1,0:T(8,128)}, u32[]{:S(2)}) copy-start(f32[4,32,128]{2,1,0:T(8,128)} %get-tuple-element.89) | copy-start | bytes 196612
  347.2 9.9 %copy-start.12 = (f32[3,4,32,128]{3,2,1,0:T(8,128)S(1)}, f32[3,4,32,128]{3,2,1,0:T(8,128)}, u32[]{:S(2)}) copy-start(f32[3,4,32,128]{3,2,1,0:T(8,128)} %param.13) | copy-start | bytes 589828
  347.2 9.9 %copy-start.17 = (f32[3]{0:T(128)S(1)}, f32[3]{0:T(128)}, u32[]{:S(2)}) copy-start(f32[3]{0:T(128)} %pad.6.clone) | copy-start | bytes 40
  347.4 7.9 %collective-permute-start.3 = (f32[2,4,32,1]{3,2,1,0:T(8,128)S(1)}, f32[2,4,32,1]{3,2,1,0:T(8,128)S(1)}, u32[]{:S(2)}, u32[]{:S(2)}) collective-permute-start(f32[2,4,32,1]{3,2,1,0:T(8,128)S(1)} %slice.175), channel_id=1, source_target_pairs={{0,2},{2,4},{4,6},{1,3},{3,5},{5,7},{8,10},{10,12},{12,14},{9,11},... | collective-permute-start | bytes 3080 | tf_op jit(solution)/shard_map/ppermute | solution.py:19
  350.8 4.5 %collective-permute-start.5 = (f32[2,4,1,128]{3,2,1,0:T(1,128)S(1)}, f32[2,4,1,128]{3,2,1,0:T(1,128)S(1)}, u32[]{:S(2)}, u32[]{:S(2)}) collective-permute-start(f32[2,4,1,128]{3,2,1,0:T(1,128)S(1)} %pad_maximum_fusion.2), channel_id=1, source_target_pairs={{0,8},{8,16},{16,24},{1,9},{9,17},{17,25},{2,10},{10,18},{18,26},{... | collective-permute-start | bytes 12296 | tf_op jit(solution)/shard_map/ppermute | solution.py:19
  353.9 3.1 collective-permute-start.4
  (11 other events, 14.4 us)
Sparse Core Ops, SparseCore 0:
  22.0 28.8 all-gather.1
  327.3 16.8 all-reduce.1
where the time goes:
time: 368 us; the launch traced here: 365 us
  other arithmetic  123 us (33%)
  local copies, waits for them, and re-layouts  77.2 us (21%)
  matrix products  49.4 us (13%)
  loops' own time  34.3 us (9%)
  blocking collectives  32.2 us (9%)
  waiting for transfers between devices  17.9 us (5%)
  starting transfers between devices  16 us (4%)
  between operations  14.5 us (4%)
    cos x16, other arithmetic, one_freq(): right = jnp.concatenate([jnp.cos(phase_y), jnp.sin(phase_y)], axis=1).T  59 us
    dot_general x16, matrix products, one_freq(): jnp.dot(left, right, preferred_element_type=jnp.float32, precision=lax.Pr...  49.4 us
    another operation x1, loops' own time, surface_source(): lax.scan(one_freq, start, jnp.arange(cotangent.shape[0], dtype=jnp.int32))  34.3 us
    cos x16, other arithmetic, one_freq(): cos_x = jnp.cos(phase_x)[None]  26.9 us
    dynamic_slice x16, local copies, waits for them, and re-layouts, one_freq(): phase_x = xs[:, None] * along_x[None, :] - time_phase[freq]  21.1 us
    dynamic_slice x16, local copies, waits for them, and re-layouts, one_freq(): wave = wavenumber[freq]  21.1 us
    sub x16, other arithmetic, one_freq(): first = real_part * cos_x - imag_part * sin_x  20 us
    psum x1, waiting for transfers between devices, local(): source = lax.psum(partial_value, 'gz') * scale  16.2 us
  transfers between devices with their start and end apart: 8, of which 2 were waited for; matrix products, arithmetic and copies ran while one was open for 67% of the time, Pallas kernels for 0%

commit v1 on v0

--- a/solution.py
+++ b/solution.py
@@ -3,11 +3,12 @@
 import jax
 import jax.numpy as jnp
 from jax import lax
+from jax.experimental import pallas as pl
+from jax.experimental.pallas import tpu as pltpu
 from jax.sharding import PartitionSpec as P
 
-FREQS = 16
-DIRS = 4096
 NPOLE = 4
+LANES = 128
 
 
 courant = 0.5
@@ -19,34 +20,229 @@
     return lax.ppermute(array, axis, pairs)
 
 
-def surface_source(cotangent, cosines, wavenumber, time_phase, xs, ys):
-    count = cotangent.shape[2]
-    rows_x = xs.shape[0]
-    rows_y = ys.shape[0]
-
-    def one_freq(total, freq):
-        wave = wavenumber[freq]
-        along_x = wave * cosines[0]
-        along_y = wave * cosines[1]
-        phase_x = xs[:, None] * along_x[None, :] - time_phase[freq]
-        phase_y = ys[:, None] * along_y[None, :]
-        cos_x = jnp.cos(phase_x)[None]
-        sin_x = jnp.sin(phase_x)[None]
-        weights = cotangent[freq]
-        real_part = weights[0::2][:, None, :]
-        imag_part = weights[1::2][:, None, :]
-        first = real_part * cos_x - imag_part * sin_x
-        second = -(real_part * sin_x + imag_part * cos_x)
-        left = jnp.concatenate([first, second], axis=2).reshape(4 * rows_x, 2 * count)
-        right = jnp.concatenate([jnp.cos(phase_y), jnp.sin(phase_y)], axis=1).T
-        part = jnp.dot(
-            left, right, preferred_element_type=jnp.float32, precision=lax.Precision.HIGHEST
-        )
-        return (total + part.reshape(4, rows_x, rows_y), None)
-
-    start = jnp.zeros((4, rows_x, rows_y), jnp.float32)
-    total, _ = lax.scan(one_freq, start, jnp.arange(cotangent.shape[0], dtype=jnp.int32))
-    return total
+def exchange(array, axis, mask):
+    return lax.ppermute(array, axis, [(i, i ^ mask) for i in range(lax.axis_size(axis))])
+
+
+def gray(index):
+    return index ^ (index >> 1)
+
+
+def ungray(code, bits):
+    index = code
+    for step in range(1, bits):
+        index = index ^ (code >> step)
+    return index
+
+
+def bits_of(size):
+    return size.bit_length() - 1
+
+
+def cmul(a, b):
+    return (a[0] * b[0] - a[1] * b[1], a[0] * b[1] + a[1] * b[0])
+
+
+def small_turn(angle):
+    q = angle * angle
+    c = 1.0 + q * (-1 / 2 + q * (1 / 24 + q * (-1 / 720 + q * (1 / 40320))))
+    s = angle * (1.0 + q * (-1 / 6 + q * (1 / 120 + q * (-1 / 5040 + q * (1 / 362880)))))
+    return c, s
+
+
+def doubled(turn):
+    c, s = turn
+    return (c - s) * (c + s), 2.0 * (c * s)
+
+
+def rotations(base, powers, rows):
+    sub = lax.broadcasted_iota(jnp.int32, (8, base[0].shape[-1]), 0)
+    value = tuple(jnp.broadcast_to(part, sub.shape) for part in base)
+    for k in range(3):
+        picked = (sub & (1 << k)) != 0
+        value = cmul(value, (jnp.where(picked, powers[k][0], 1.0), jnp.where(picked, powers[k][1], 0.0)))
+    blocks = [value]
+    k = 3
+    while len(blocks) * 8 < rows:
+        blocks = blocks + [cmul(block, powers[k]) for block in blocks]
+        k += 1
+    return tuple(jnp.concatenate([block[i] for block in blocks], axis=0)[:rows] for i in (0, 1))
+
+
+def split(value):
+    high = value.astype(jnp.bfloat16)
+    return high, (value - high.astype(jnp.float32)).astype(jnp.bfloat16)
+
+
+def dot_nt(a, b):
+    return lax.dot_general(a, b, (((1,), (1,)), ((), ())), preferred_element_type=jnp.float32)
+
+
+def source_kernel(freqs, wx, half, tiles_y, zslots, xslots, scale, chunks):
+    xbits = max(3, (wx - 1).bit_length())
+    ybits = max(3, (half - 1).bit_length())
+    per = 4 // zslots
+
+    def body(*refs):
+        ints, wave_ref, phase_ref = refs[:3]
+        cots = refs[3 : 3 + chunks]
+        coss = refs[3 + chunks : 3 + 2 * chunks]
+        out = refs[3 + 2 * chunks]
+        xbase, xpow, ypow, acc_even, acc_odd = refs[4 + 2 * chunks :]
+        center = (2 * half - 1) / 2.0
+        for n in range(chunks):
+            along_x = wave_ref[...] * coss[n][0:1, :]
+            along_y = wave_ref[...] * coss[n][1:2, :]
+            origin = along_y * center - phase_ref[...]
+            for xr in range(xslots):
+                angle = along_x * ints[xr].astype(jnp.float32) + origin
+                xbase[n, xr, 0] = jnp.cos(angle)
+                xbase[n, xr, 1] = jnp.sin(angle)
+            turn = doubled(small_turn(0.5 * along_x))
+            for k in range(xbits):
+                xpow[n, k, 0], xpow[n, k, 1] = turn
+                turn = doubled(turn)
+            turn = small_turn(0.5 * along_y)
+            for k in range(ybits + 1):
+                ypow[n, k, 0], ypow[n, k, 1] = turn
+                turn = doubled(turn)
+        acc_even[...] = jnp.zeros_like(acc_even)
+        acc_odd[...] = jnp.zeros_like(acc_odd)
+        zcode = ints[xslots]
+
+        def one(f, carry):
+            firsts, seconds, coses, sines = [], [], [], []
+            for n in range(chunks):
+                def row(ref, *where):
+                    return tuple(ref[(n, *where, i, pl.ds(f, 1), slice(None))] for i in (0, 1))
+
+                powers = [row(ypow, k) for k in range(ybits + 1)]
+                cy, sy = rotations(powers[0], powers[1:], half)
+                coses.append(cy)
+                sines.append(sy)
+                powers = [row(xpow, k) for k in range(xbits)]
+                turns = [rotations(row(xbase, xr), powers, wx) for xr in range(xslots)]
+                first, second = [], []
+                for zr in range(zslots):
+                    for xr in range(xslots):
+                        cx, sx = turns[xr]
+                        for c2 in range(per):
+                            at = 2 * ((zcode ^ zr) * per + c2)
+                            p = cots[n][f, pl.ds(at, 1), :]
+                            q = cots[n][f, pl.ds(at + 1, 1), :]
+                            first.append(p * cx - q * sx)
+                            second.append(p * sx + q * cx)
+                firsts.append(jnp.concatenate(first, axis=0))
+                seconds.append(jnp.concatenate(second, axis=0))
+
+            def product(lefts, rights):
+                lh, ll = split(jnp.concatenate(lefts, axis=1))
+                rh, rl = split(jnp.concatenate(rights, axis=1))
+                return dot_nt(lh, rh) + dot_nt(lh, rl) + dot_nt(ll, rh)
+
+            acc_even[...] += product(firsts, coses)
+            acc_odd[...] += product(seconds, sines)
+            return carry
+
+        lax.fori_loop(0, freqs, one, 0)
+        ycode = ints[xslots + 1]
+        ybit = bits_of(tiles_y)
+
+        def slot(tile):
+            code = gray(tile) ^ ycode
+            place = 0
+            for k in range(ybit):
+                place = place * 2 + ((code >> k) & 1)
+            return place
+
+        for j in range(tiles_y // 2):
+            lanes = slice(j * LANES, (j + 1) * LANES)
+            up = slot(tiles_y // 2 + j)
+            down = slot(tiles_y // 2 - 1 - j)
+            at = 0
+            for zr in range(zslots):
+                for xr in range(xslots):
+                    for c2 in range(per):
+                        rows = slice(at * wx, (at + 1) * wx)
+                        even = acc_even[rows, lanes] * scale
+                        odd = acc_odd[rows, lanes] * scale
+                        out[zr, up, xr, c2] = even - odd
+                        out[zr, down, xr, c2] = even + odd
+                        at += 1
+
+    return body
+
+
+def surface_source(cotangent, cosines, wavenumber, time_phase, wx, wy):
+    sx, sy, sz = (lax.axis_size(name) for name in ("gx", "gy", "gz"))
+    ix, iy, iz = (lax.axis_index(name) for name in ("gx", "gy", "gz"))
+    freqs, _, count = cotangent.shape
+    scale = 1.0 / math.sqrt(freqs * count * sx * sy * sz)
+    assert wy == LANES and sx > 1 and sy > 1
+    pad = -count % LANES
+    if pad:
+        cotangent = jnp.pad(cotangent, ((0, 0), (0, 0), (0, pad)))
+        cosines = jnp.pad(cosines, ((0, 0), (0, pad)))
+    cots = [cotangent, exchange(cotangent, "gx", 1)]
+    coss = [cosines, exchange(cosines, "gx", 1)]
+    chunks = 2
+    xslots = sx // 2
+    zslots = min(sz, 4)
+    xbit, ybit, zbit = bits_of(sx), bits_of(sy), bits_of(zslots)
+    codes = []
+    for slot in range(xslots):
+        code = gray(ix)
+        for k in range(1, xbit):
+            code = code ^ (((slot >> (xbit - 1 - k)) & 1) << k)
+        codes.append(ungray(code, xbit) * wx)
+    zcode = 0
+    for k in range(zbit):
+        zcode = zcode * 2 + ((gray(iz) >> k) & 1)
+    ints = jnp.stack([*codes, jnp.asarray(zcode, jnp.int32), gray(iy)]).astype(jnp.int32)
+    half = sy * wy // 2
+    rows = 4 * xslots * wx
+    per = 4 // zslots
+    xlevels = max(3, (wx - 1).bit_length())
+    ylevels = max(3, (half - 1).bit_length()) + 1
+    width = count + pad
+    smem = pl.BlockSpec(memory_space=pltpu.SMEM)
+    vmem = pl.BlockSpec(memory_space=pltpu.VMEM)
+    f32 = jnp.float32
+    part = pl.pallas_call(
+        source_kernel(freqs, wx, half, sy, zslots, xslots, scale, chunks),
+        out_shape=jax.ShapeDtypeStruct((zslots, sy, xslots, per, wx, wy), f32),
+        in_specs=[smem] + [vmem] * (2 + 2 * chunks),
+        out_specs=vmem,
+        scratch_shapes=[
+            pltpu.VMEM((chunks, xslots, 2, freqs, width), f32),
+            pltpu.VMEM((chunks, xlevels, 2, freqs, width), f32),
+            pltpu.VMEM((chunks, ylevels, 2, freqs, width), f32),
+            pltpu.VMEM((rows, half), f32),
+            pltpu.VMEM((rows, half), f32),
+        ],
+        name="source",
+    )(ints, wavenumber[:, None], time_phase[:, None], *cots, *coss)
+    for k in range(bits_of(sz)):
+        mask = (2 << k) - 1
+        if k < zbit:
+            half_z = part.shape[0] // 2
+            part = part[:half_z] + exchange(part[half_z:], "gz", mask)
+        else:
+            part = part + exchange(part, "gz", mask)
+    part = part[0]
+    for k in range(ybit):
+        half_y = part.shape[0] // 2
+        part = part[:half_y] + exchange(part[half_y:], "gy", (2 << k) - 1)
+    part = part[0]
+    for k in range(1, xbit):
+        half_x = part.shape[0] // 2
+        part = part[:half_x] + exchange(part[half_x:], "gx", (2 << k) - 1)
+    part = part[0]
+    top = gray(sz - 1)
+    for k in reversed(range(zbit)):
+        other = exchange(part, "gz", (2 << k) - 1)
+        part = jnp.concatenate([other, part] if (top >> k) & 1 else [part, other], axis=0)
+    return part
 
 
 def ahead(value, nearby, axis):
@@ -63,21 +259,9 @@
     e_field, h_field, pole_current, material, pole_table, cotangent, cosines, wavenumber, time_phase
 ):
     depth, width_x, width_y = material.shape
-    scale = 1.0 / math.sqrt(DIRS * FREQS)
-    anchor_x = (lax.axis_index("gx") * width_x).astype(jnp.float32)
-    anchor_y = (lax.axis_index("gy") * width_y).astype(jnp.float32)
-    ys = anchor_y + jnp.arange(width_y).astype(jnp.float32)
-    first_cot, first_cos = (
-        lax.all_gather(cotangent, "gx", axis=2, tiled=True),
-        lax.all_gather(cosines, "gx", axis=1, tiled=True),
-    )
-    band_cot, band_cos = (
-        lax.all_gather(first_cot, "gy", axis=2, tiled=True),
-        lax.all_gather(first_cos, "gy", axis=1, tiled=True),
-    )
-    xs = anchor_x + jnp.arange(width_x).astype(jnp.float32)
-    partial_value = surface_source(band_cot, band_cos, wavenumber, time_phase, xs, ys)
-    source = lax.psum(partial_value, "gz") * scale
+    source = surface_source(cotangent, cosines, wavenumber, time_phase, width_x, width_y)
+    flipped = lax.axis_index("gy") < lax.axis_size("gy") // 2
+    source = jnp.where(flipped, source[..., ::-1], source)
     is_top = lax.axis_index("gz") == lax.axis_size("gz") - 1
     top = ((jnp.arange(depth) == depth - 1) & is_top).astype(jnp.float32)[:, None, None]
     next_x = from_behind(e_field[1:3, :, :1, :], "gx", -1)

time: 368 us -> 64.2 us (0.17)
  the two profiles are of different devices: /device:TPU:1 before, /device:TPU:20 now
where the time goes in v1:
time: 64.2 us; the launch traced here: 63.7 us
  starting transfers between devices  21.3 us (33%)
  waiting for transfers between devices  20.4 us (32%)
  Pallas kernels  9.77 us (15%)
  local copies, waits for them, and re-layouts  8.85 us (14%)
  other arithmetic  2.29 us (4%)
  between operations  1.06 us (2%)
    ppermute x6, starting transfers between devices, from_behind(): return lax.ppermute(array, axis, pairs)  16.6 us
    ppermute x7, waiting for transfers between devices, exchange(): lax.ppermute(array, axis, [(i, i ^ mask) for i in range(lax.axis_size(axi...  15.3 us
    pallas_call x1, Pallas kernels, surface_source(): pl.pallas_call(source_kernel(freqs, wx, half, sy, zslots, xslots, scale,...  9.77 us
    ppermute x6, waiting for transfers between devices, from_behind(): return lax.ppermute(array, axis, pairs)  5.17 us
    unnamed x22, local copies, waits for them, and re-layouts  4.97 us
    ppermute x7, starting transfers between devices, exchange(): lax.ppermute(array, axis, [(i, i ^ mask) for i in range(lax.axis_size(axi...  4.78 us
  transfers between devices with their start and end apart: 13, of which 6 were waited for; matrix products, arithmetic and copies ran while one was open for 7% of the time, Pallas kernels for 15%

profile of v1, /device:TPU:20, one launch (start us, length us, event | category | flops | bytes accessed | tf_op | source)
XLA Modules:
  0.0 63.7 jit_solution(15712008065094524635)
XLA Ops:
  0.6 1.6 %collective-permute-start.3 = (f32[16,8,128]{2,1,0:T(8,128)}, f32[16,8,128]{2,1,0:T(8,128)S(1)}, u32[]{:S(2)}, u32[]{:S(2)}) collective-permute-start(f32[16,8,128]{2,1,0:T(8,128)} %refs_3_.1), channel_id=1, source_target_pairs={{0,8},{8,0},{16,24},{24,16},{1,9},{9,1},{17,25},{25,17},{2,10},{10... | collective-permute-start | bytes 196616 | tf_op jit(solution)/shard_map/ppermute | solution.py:24
  2.3 0.4 collective-permute-start.4
  2.7 0.9 %slice.183 = f32[2,4,32,1]{3,2,1,0:T(8,128)S(1)} slice(f32[3,4,32,128]{3,2,1,0:T(8,128)} %param.9), slice={[0:3:2], [0:4:1], [0:32:1], [0:1:1]} | slice | bytes 2048 | tf_op jit(solution)/shard_map/slice | solution.py:268
  3.6 3.3 %collective-permute-start.1 = (f32[2,4,32,1]{3,2,1,0:T(8,128)S(1)}, f32[2,4,32,1]{3,2,1,0:T(8,128)S(1)}, u32[]{:S(2)}, u32[]{:S(2)}) collective-permute-start(f32[2,4,32,1]{3,2,1,0:T(8,128)S(1)} %slice.183), channel_id=1, source_target_pairs={{2,0},{4,2},{6,4},{3,1},{5,3},{7,5},{10,8},{12,10},{14,12},{11,9},... | collective-permute-start | bytes 3080 | tf_op jit(solution)/shard_map/ppermute | solution.py:20
  7.0 1.3 %collective-permute-start.2 = (f32[2,1,32,128]{3,2,1,0:T(8,128)S(1)}, f32[2,1,32,128]{3,2,1,0:T(8,128)S(1)}, u32[]{:S(2)}, u32[]{:S(2)}) collective-permute-start(f32[2,1,32,128]{3,2,1,0:T(8,128)S(1)} %slice.190), channel_id=1, source_target_pairs={{1,0},{3,2},{5,4},{7,6},{9,8},{11,10},{13,12},{15,14},{17,16},{19,... | collective-permute-start | bytes 98312 | tf_op jit(solution)/shard_map/ppermute | solution.py:20
  8.3 2.4 %collective-permute-start = (f32[2,4,1,128]{3,2,1,0:T(1,128)S(1)}, f32[2,4,1,128]{3,2,1,0:T(1,128)S(1)}, u32[]{:S(2)}, u32[]{:S(2)}) collective-permute-start(f32[2,4,1,128]{3,2,1,0:T(1,128)S(1)} %slice.179), channel_id=1, source_target_pairs={{8,0},{16,8},{24,16},{9,1},{17,9},{25,17},{10,2},{18,10},{26,18},{... | collective-permute-start | bytes 12296 | tf_op jit(solution)/shard_map/ppermute | solution.py:20
  10.7 0.1 fusion.35
  10.8 0.0 copy-start.7
  10.9 0.7 %copy-done.7 = f32[3,4]{1,0:T(4,128)S(1)} copy-done((f32[3,4]{1,0:T(4,128)S(1)}, f32[3,4]{1,0:T(4,128)}, u32[]{:S(2)}) %copy-start.7) | copy-done | bytes 72
  11.5 0.6 pad_add_fusion.refs_0_
  12.1 0.7 %copy-done.9 = f32[16]{0:T(128)S(1)} copy-done((f32[16]{0:T(128)S(1)}, f32[16]{0:T(128)}, u32[]{:S(2)}) %copy-start.9) | copy-done | bytes 88
  12.8 0.7 %copy.24.refs_1_ = f32[16,1]{1,0:T(8,128)} copy(f32[16,1]{0,1:T(1,128)S(1)} %bitcast.101) | data formatting | bytes 128 | tf_op jit(solution)/shard_map/broadcast_in_dim | solution.py:224
  13.5 0.7 %copy-done.10 = f32[16]{0:T(128)S(1)} copy-done((f32[16]{0:T(128)S(1)}, f32[16]{0:T(128)}, u32[]{:S(2)}) %copy-start.10) | copy-done | bytes 88
  14.1 0.7 %copy.25.refs_2_ = f32[16,1]{1,0:T(8,128)} copy(f32[16,1]{0,1:T(1,128)S(1)} %bitcast.102) | data formatting | bytes 128 | tf_op jit(solution)/shard_map/broadcast_in_dim | solution.py:224
  14.8 0.6 copy-done.8
  15.4 0.6 copy-done.5
  16.0 9.8 %source.1 = f32[2,4,2,2,32,128]{5,4,3,2,1,0:T(8,128)} custom-call(s32[4]{0:T(128)} %pad_add_fusion.refs_0_, f32[16,1]{1,0:T(8,128)} %copy.24.refs_1_, f32[16,1]{1,0:T(8,128)} %copy.25.refs_2_, f32[16,8,128]{2,1,0:T(8,128)} %refs_3_.1, f32[16,8,128]{2,1,0:T(8,128)} %copy-done.5, f32[2,128]{1,0:T(2,128)} %refs_5_.1, f32[2,128]{1,0:T(2,128)} %copy-done.8), custom_call_target="tpu_custom_call" | custom-call | tf_op jit(solution)/shard_map/source/pallas_call | solution.py:211
  25.8 1.0 %slice.240 = f32[1,4,2,2,32,128]{5,4,3,2,1,0:T(8,128)S(1)} slice(f32[2,4,2,2,32,128]{5,4,3,2,1,0:T(8,128)} %source.1), slice={[1:2], [0:4], [0:2], [0:2], [0:32], [0:128]} | slice | bytes 524288 | tf_op jit(solution)/shard_map/slice | solution.py:229
  26.8 0.9 %collective-permute-start.5 = (f32[1,4,2,2,32,128]{5,4,3,2,1,0:T(8,128)S(1)}, f32[1,4,2,2,32,128]{5,4,3,2,1,0:T(8,128)S(1)}, u32[]{:S(2)}, u32[]{:S(2)}) collective-permute-start(f32[1,4,2,2,32,128]{5,4,3,2,1,0:T(8,128)S(1)} %slice.240), channel_id=1, source_target_pairs={{0,1},{1,0},{2,3},{3,2},{4,5},{5,4},{6,7},{7,6},{8,9},{9,8},{10,11... | collective-permute-start | bytes 786440 | tf_op jit(solution)/shard_map/ppermute | solution.py:24
  27.8 1.1 %collective-permute-done.5 = f32[1,4,2,2,32,128]{5,4,3,2,1,0:T(8,128)S(1)} collective-permute-done((f32[1,4,2,2,32,128]{5,4,3,2,1,0:T(8,128)S(1)}, f32[1,4,2,2,32,128]{5,4,3,2,1,0:T(8,128)S(1)}, u32[]{:S(2)}, u32[]{:S(2)}) %collective-permute-start.5) | collective-permute-done | bytes 262176 | tf_op jit(solution)/shard_map/ppermute | solution.py:24
  29.0 0.7 %collective-permute-start.6 = (f32[2,2,2,32,128]{4,3,2,1,0:T(8,128)S(1)}, f32[2,2,2,32,128]{4,3,2,1,0:T(8,128)S(1)}, u32[]{:S(2)}, u32[]{:S(2)}) collective-permute-start(f32[2,2,2,32,128]{4,3,2,1,0:T(8,128)S(1)} %slice_bitcast_fusion), channel_id=1, source_target_pairs={{0,2},{2,0},{4,6},{6,4},{1,3},{3,1},{5,7},{7,5},{8,10},{10,8},{12,... | collective-permute-start | bytes 393224 | tf_op jit(solution)/shard_map/ppermute | solution.py:24
  29.6 0.1 pad.2.clone
  29.7 0.1 copy-done.6
  29.8 0.1 select_reduce_fusion.2
  29.9 4.9 %collective-permute-done.6 = f32[2,2,2,32,128]{4,3,2,1,0:T(8,128)S(1)} collective-permute-done((f32[2,2,2,32,128]{4,3,2,1,0:T(8,128)S(1)}, f32[2,2,2,32,128]{4,3,2,1,0:T(8,128)S(1)}, u32[]{:S(2)}, u32[]{:S(2)}) %collective-permute-start.6) | collective-permute-done | bytes 131104 | tf_op jit(solution)/shard_map/ppermute | solution.py:24
  34.9 0.6 collective-permute-start.7
  35.5 4.6 %collective-permute-done.7 = f32[1,2,2,32,128]{4,3,2,1,0:T(8,128)S(1)} collective-permute-done((f32[1,2,2,32,128]{4,3,2,1,0:T(8,128)S(1)}, f32[1,2,2,32,128]{4,3,2,1,0:T(8,128)S(1)}, u32[]{:S(2)}, u32[]{:S(2)}) %collective-permute-start.7) | collective-permute-done | bytes 65568 | tf_op jit(solution)/shard_map/ppermute | solution.py:24
  40.1 0.5 collective-permute-start.8
  40.6 3.4 %collective-permute-done.8 = f32[1,2,32,128]{3,2,1,0:T(8,128)S(1)} collective-permute-done((f32[1,2,32,128]{3,2,1,0:T(8,128)S(1)}, f32[1,2,32,128]{3,2,1,0:T(8,128)S(1)}, u32[]{:S(2)}, u32[]{:S(2)}) %collective-permute-start.8) | collective-permute-done | bytes 32800 | tf_op jit(solution)/shard_map/ppermute | solution.py:24
  44.1 1.2 %collective-permute-done.9 = f32[2,32,128]{2,1,0:T(8,128)S(1)} collective-permute-done((f32[2,32,128]{2,1,0:T(8,128)S(1)}, f32[2,32,128]{2,1,0:T(8,128)S(1)}, u32[]{:S(2)}, u32[]{:S(2)}) %collective-permute-start.9) | collective-permute-done | bytes 32800 | tf_op jit(solution)/shard_map/ppermute | solution.py:24
  45.3 0.1 rev.3
  45.4 0.9 %copy-done.2 = f32[3,4,32,128]{3,2,1,0:T(8,128)S(1)} copy-done((f32[3,4,32,128]{3,2,1,0:T(8,128)S(1)}, f32[3,4,32,128]{3,2,1,0:T(8,128)}, u32[]{:S(2)}) %copy-start.2) | copy-done | bytes 196632
  46.3 0.1 fusion.10
  46.4 0.1 fusion.33
  46.6 0.1 fusion.6
  46.7 0.0 copy-start.3
  46.7 0.1 fusion.17
  46.8 0.1 fusion.26
  47.0 5.3 %collective-permute-start.12 = (f32[2,4,1,128]{3,2,1,0:T(1,128)S(1)}, f32[2,4,1,128]{3,2,1,0:T(1,128)S(1)}, u32[]{:S(2)}, u32[]{:S(2)}) collective-permute-start(f32[2,4,1,128]{3,2,1,0:T(1,128)S(1)} %pad_maximum_fusion.3), channel_id=1, source_target_pairs={{0,8},{8,16},{16,24},{1,9},{9,17},{17,25},{2,10},{10,18},{18,26},{... | collective-permute-start | bytes 12296 | tf_op jit(solution)/shard_map/ppermute | solution.py:20
  52.3 1.8 %collective-permute-start.11 = (f32[2,1,32,128]{3,2,1,0:T(8,128)S(1)}, f32[2,1,32,128]{3,2,1,0:T(8,128)S(1)}, u32[]{:S(2)}, u32[]{:S(2)}) collective-permute-start(f32[2,1,32,128]{3,2,1,0:T(8,128)S(1)} %pad_maximum_fusion.2), channel_id=1, source_target_pairs={{0,1},{2,3},{4,5},{6,7},{8,9},{10,11},{12,13},{14,15},{16,17},{18,... | collective-permute-start | bytes 98312 | tf_op jit(solution)/shard_map/ppermute | solution.py:20
  54.1 0.1 slice.211
  54.2 2.5 %collective-permute-start.10 = (f32[2,4,32,1]{3,2,1,0:T(8,128)S(1)}, f32[2,4,32,1]{3,2,1,0:T(8,128)S(1)}, u32[]{:S(2)}, u32[]{:S(2)}) collective-permute-start(f32[2,4,32,1]{3,2,1,0:T(8,128)S(1)} %slice.211), channel_id=1, source_target_pairs={{0,2},{2,4},{4,6},{1,3},{3,5},{5,7},{8,10},{10,12},{12,14},{9,11},... | collective-permute-start | bytes 3080 | tf_op jit(solution)/shard_map/ppermute | solution.py:20
  56.7 0.1 broadcast_multiply_fusion.1
  56.8 5.2 %collective-permute-done.10 = f32[2,4,32,1]{3,2,1,0:T(8,128)S(1)} collective-permute-done((f32[2,4,32,1]{3,2,1,0:T(8,128)S(1)}, f32[2,4,32,1]{3,2,1,0:T(8,128)S(1)}, u32[]{:S(2)}, u32[]{:S(2)}) %collective-permute-start.10) | collective-permute-done | bytes 1056 | tf_op jit(solution)/shard_map/ppermute | solution.py:20
  62.0 0.0 copy-start.4
  62.0 0.1 fusion.18
  62.1 0.8 %copy-done.4 = f32[3,4,32,128]{3,2,1,0:T(8,128)S(1)} copy-done((f32[3,4,32,128]{3,2,1,0:T(8,128)S(1)}, f32[3,4,32,128]{3,2,1,0:T(8,128)}, u32[]{:S(2)}) %copy-start.4) | copy-done | bytes 196632
  62.9 0.8 %fusion.2 = (f32[3,4,32,128]{3,2,1,0:T(8,128)}, f32[3,4,32,128]{3,2,1,0:T(8,128)}) fusion(f32[3,4,32,128]{3,2,1,0:T(8,128)S(1)} %copy-done, f32[1,4,32,128]{3,2,1,0:T(8,128)S(1)} %get-tuple-element.29, f32[1,4,32,128]{3,2,1,0:T(8,128)S(1)} %get-tuple-element.30, f32[1,4,32,128]{3,2,1,0:T(8,128)S(1)} %get-tuple-element.28, ...), kind=kLoop, calls=%fused_computation.9 | loop fusion | flops 688128 | bytes 1310732 | tf_op jit(solution)/shard_map/sub | solution.py:294
  (50 shorter events, 0.3 us)
Async XLA Ops:
  0.6 6.4 %copy-start = (f32[3,4,32,128]{3,2,1,0:T(8,128)S(1)}, f32[3,4,32,128]{3,2,1,0:T(8,128)}, u32[]{:S(2)}) copy-start(f32[3,4,32,128]{3,2,1,0:T(8,128)} %param.9) | copy-start | bytes 589828
  0.6 14.2 %collective-permute-start.3 = (f32[16,8,128]{2,1,0:T(8,128)}, f32[16,8,128]{2,1,0:T(8,128)S(1)}, u32[]{:S(2)}, u32[]{:S(2)}) collective-permute-start(f32[16,8,128]{2,1,0:T(8,128)} %refs_3_.1), channel_id=1, source_target_pairs={{0,8},{8,0},{16,24},{24,16},{1,9},{9,1},{17,25},{25,17},{2,10},{10... | collective-permute-start | bytes 196616 | tf_op jit(solution)/shard_map/ppermute | solution.py:24
  2.3 12.5 %collective-permute-start.4 = (f32[2,128]{1,0:T(2,128)}, f32[2,128]{1,0:T(2,128)S(1)}, u32[]{:S(2)}, u32[]{:S(2)}) collective-permute-start(f32[2,128]{1,0:T(2,128)} %refs_5_.1), channel_id=1, source_target_pairs={{0,8},{8,0},{16,24},{24,16},{1,9},{9,1},{17,25},{25,17},{2,10},{10... | collective-permute-start | bytes 3080 | tf_op jit(solution)/shard_map/ppermute | solution.py:24
  3.6 31.8 %collective-permute-start.1 = (f32[2,4,32,1]{3,2,1,0:T(8,128)S(1)}, f32[2,4,32,1]{3,2,1,0:T(8,128)S(1)}, u32[]{:S(2)}, u32[]{:S(2)}) collective-permute-start(f32[2,4,32,1]{3,2,1,0:T(8,128)S(1)} %slice.183), channel_id=1, source_target_pairs={{2,0},{4,2},{6,4},{3,1},{5,3},{7,5},{10,8},{12,10},{14,12},{11,9},... | collective-permute-start | bytes 3080 | tf_op jit(solution)/shard_map/ppermute | solution.py:20
  7.0 37.1 %collective-permute-start.2 = (f32[2,1,32,128]{3,2,1,0:T(8,128)S(1)}, f32[2,1,32,128]{3,2,1,0:T(8,128)S(1)}, u32[]{:S(2)}, u32[]{:S(2)}) collective-permute-start(f32[2,1,32,128]{3,2,1,0:T(8,128)S(1)} %slice.190), channel_id=1, source_target_pairs={{1,0},{3,2},{5,4},{7,6},{9,8},{11,10},{13,12},{15,14},{17,16},{19,... | collective-permute-start | bytes 98312 | tf_op jit(solution)/shard_map/ppermute | solution.py:20
  8.3 32.3 %collective-permute-start = (f32[2,4,1,128]{3,2,1,0:T(1,128)S(1)}, f32[2,4,1,128]{3,2,1,0:T(1,128)S(1)}, u32[]{:S(2)}, u32[]{:S(2)}) collective-permute-start(f32[2,4,1,128]{3,2,1,0:T(1,128)S(1)} %slice.179), channel_id=1, source_target_pairs={{8,0},{16,8},{24,16},{9,1},{17,9},{25,17},{10,2},{18,10},{26,18},{... | collective-permute-start | bytes 12296 | tf_op jit(solution)/shard_map/ppermute | solution.py:20
  10.8 0.7 %copy-start.7 = (f32[3,4]{1,0:T(4,128)S(1)}, f32[3,4]{1,0:T(4,128)}, u32[]{:S(2)}) copy-start(f32[3,4]{1,0:T(4,128)} %param.13) | copy-start | bytes 148
  12.1 0.7 %copy-start.9 = (f32[16]{0:T(128)S(1)}, f32[16]{0:T(128)}, u32[]{:S(2)}) copy-start(f32[16]{0:T(128)} %param.16) | copy-start | bytes 196
  13.5 0.7 %copy-start.10 = (f32[16]{0:T(128)S(1)}, f32[16]{0:T(128)}, u32[]{:S(2)}) copy-start(f32[16]{0:T(128)} %param.17) | copy-start | bytes 196
  14.8 0.6 copy-start.8
  15.4 0.6 copy-start.5
  25.8 3.1 %copy-start.1 = (f32[2,4,2,2,32,128]{5,4,3,2,1,0:T(8,128)S(1)}, f32[2,4,2,2,32,128]{5,4,3,2,1,0:T(8,128)}, u32[]{:S(2)}) copy-start(f32[2,4,2,2,32,128]{5,4,3,2,1,0:T(8,128)} %source.1) | copy-start | bytes 1572868
  26.8 2.1 %collective-permute-start.5 = (f32[1,4,2,2,32,128]{5,4,3,2,1,0:T(8,128)S(1)}, f32[1,4,2,2,32,128]{5,4,3,2,1,0:T(8,128)S(1)}, u32[]{:S(2)}, u32[]{:S(2)}) collective-permute-start(f32[1,4,2,2,32,128]{5,4,3,2,1,0:T(8,128)S(1)} %slice.240), channel_id=1, source_target_pairs={{0,1},{1,0},{2,3},{3,2},{4,5},{5,4},{6,7},{7,6},{8,9},{9,8},{10,11... | collective-permute-start | bytes 786440 | tf_op jit(solution)/shard_map/ppermute | solution.py:24
  28.9 0.8 %copy-start.6 = (s32[4,32,128]{2,1,0:T(8,128)S(1)}, s32[4,32,128]{2,1,0:T(8,128)}, u32[]{:S(2)}) copy-start(s32[4,32,128]{2,1,0:T(8,128)} %param.12) | copy-start | bytes 196612
  29.0 5.8 %collective-permute-start.6 = (f32[2,2,2,32,128]{4,3,2,1,0:T(8,128)S(1)}, f32[2,2,2,32,128]{4,3,2,1,0:T(8,128)S(1)}, u32[]{:S(2)}, u32[]{:S(2)}) collective-permute-start(f32[2,2,2,32,128]{4,3,2,1,0:T(8,128)S(1)} %slice_bitcast_fusion), channel_id=1, source_target_pairs={{0,2},{2,0},{4,6},{6,4},{1,3},{3,1},{5,7},{7,5},{8,10},{10,8},{12,... | collective-permute-start | bytes 393224 | tf_op jit(solution)/shard_map/ppermute | solution.py:24
  34.9 5.2 %collective-permute-start.7 = (f32[1,2,2,32,128]{4,3,2,1,0:T(8,128)S(1)}, f32[1,2,2,32,128]{4,3,2,1,0:T(8,128)S(1)}, u32[]{:S(2)}, u32[]{:S(2)}) collective-permute-start(f32[1,2,2,32,128]{4,3,2,1,0:T(8,128)S(1)} %slice.244), channel_id=1, source_target_pairs={{0,6},{2,4},{4,2},{6,0},{1,7},{3,5},{5,3},{7,1},{8,14},{10,12},{12... | collective-permute-start | bytes 196616 | tf_op jit(solution)/shard_map/ppermute | solution.py:24
  40.1 4.0 %collective-permute-start.8 = (f32[1,2,32,128]{3,2,1,0:T(8,128)S(1)}, f32[1,2,32,128]{3,2,1,0:T(8,128)S(1)}, u32[]{:S(2)}, u32[]{:S(2)}) collective-permute-start(f32[1,2,32,128]{3,2,1,0:T(8,128)S(1)} %slice_bitcast_fusion.11), channel_id=1, source_target_pairs={{0,24},{8,16},{16,8},{24,0},{1,25},{9,17},{17,9},{25,1},{2,26},{10... | collective-permute-start | bytes 98312 | tf_op jit(solution)/shard_map/ppermute | solution.py:24
  44.1 1.2 %collective-permute-start.9 = (f32[2,32,128]{2,1,0:T(8,128)S(1)}, f32[2,32,128]{2,1,0:T(8,128)S(1)}, u32[]{:S(2)}, u32[]{:S(2)}) collective-permute-start(f32[2,32,128]{2,1,0:T(8,128)S(1)} %fusion.30), channel_id=1, source_target_pairs={{0,1},{1,0},{2,3},{3,2},{4,5},{5,4},{6,7},{7,6},{8,9},{9,8},{10,11... | collective-permute-start | bytes 98312 | tf_op jit(solution)/shard_map/ppermute | solution.py:24
  45.4 0.9 %copy-start.2 = (f32[3,4,32,128]{3,2,1,0:T(8,128)S(1)}, f32[3,4,32,128]{3,2,1,0:T(8,128)}, u32[]{:S(2)}) copy-start(f32[3,4,32,128]{3,2,1,0:T(8,128)} %param.10) | copy-start | bytes 589828
  46.7 7.4 %copy-start.3 = (f32[3,4,32,128]{3,2,1,0:T(8,128)}, f32[3,4,32,128]{3,2,1,0:T(8,128)S(1)}, u32[]{:S(2)}) copy-start(f32[3,4,32,128]{3,2,1,0:T(8,128)S(1)} %pad_maximum_fusion) | copy-start | bytes 589828
  47.0 15.0 %collective-permute-start.12 = (f32[2,4,1,128]{3,2,1,0:T(1,128)S(1)}, f32[2,4,1,128]{3,2,1,0:T(1,128)S(1)}, u32[]{:S(2)}, u32[]{:S(2)}) collective-permute-start(f32[2,4,1,128]{3,2,1,0:T(1,128)S(1)} %pad_maximum_fusion.3), channel_id=1, source_target_pairs={{0,8},{8,16},{16,24},{1,9},{9,17},{17,25},{2,10},{10,18},{18,26},{... | collective-permute-start | bytes 12296 | tf_op jit(solution)/shard_map/ppermute | solution.py:20
  52.3 9.7 %collective-permute-start.11 = (f32[2,1,32,128]{3,2,1,0:T(8,128)S(1)}, f32[2,1,32,128]{3,2,1,0:T(8,128)S(1)}, u32[]{:S(2)}, u32[]{:S(2)}) collective-permute-start(f32[2,1,32,128]{3,2,1,0:T(8,128)S(1)} %pad_maximum_fusion.2), channel_id=1, source_target_pairs={{0,1},{2,3},{4,5},{6,7},{8,9},{10,11},{12,13},{14,15},{16,17},{18,... | collective-permute-start | bytes 98312 | tf_op jit(solution)/shard_map/ppermute | solution.py:20
  54.2 7.8 %collective-permute-start.10 = (f32[2,4,32,1]{3,2,1,0:T(8,128)S(1)}, f32[2,4,32,1]{3,2,1,0:T(8,128)S(1)}, u32[]{:S(2)}, u32[]{:S(2)}) collective-permute-start(f32[2,4,32,1]{3,2,1,0:T(8,128)S(1)} %slice.211), channel_id=1, source_target_pairs={{0,2},{2,4},{4,6},{1,3},{3,5},{5,7},{8,10},{10,12},{12,14},{9,11},... | collective-permute-start | bytes 3080 | tf_op jit(solution)/shard_map/ppermute | solution.py:20
  62.0 0.9 %copy-start.4 = (f32[3,4,32,128]{3,2,1,0:T(8,128)S(1)}, f32[3,4,32,128]{3,2,1,0:T(8,128)}, u32[]{:S(2)}) copy-start(f32[3,4,32,128]{3,2,1,0:T(8,128)} %param.11) | copy-start | bytes 589828

commit v2 on v1

v2 whole, which is shorter than its diff:
```python
import math

import jax
import jax.numpy as jnp
from jax import lax
from jax.experimental import pallas as pl
from jax.experimental.pallas import tpu as pltpu
from jax.sharding import PartitionSpec as P

NPOLE = 4
LANES = 128


courant = 0.5


def exchange(array, axis, mask):
    return lax.ppermute(array, axis, [(i, i ^ mask) for i in range(lax.axis_size(axis))])


def gray(index):
    return index ^ (index >> 1)


def ungray(code, bits):
    index = code
    for step in range(1, bits):
        index = index ^ (code >> step)
    return index


def bits_of(size):
    return size.bit_length() - 1


def cmul(a, b):
    return (a[0] * b[0] - a[1] * b[1], a[0] * b[1] + a[1] * b[0])


def small_turn(angle):
    q = angle * angle
    c = 1.0 + q * (-1 / 2 + q * (1 / 24 + q * (-1 / 720 + q * (1 / 40320))))
    s = angle * (1.0 + q * (-1 / 6 + q * (1 / 120 + q * (-1 / 5040 + q * (1 / 362880)))))
    return c, s


def doubled(turn):
    c, s = turn
    return (c - s) * (c + s), 2.0 * (c * s)


def rotations(base, powers, rows):
    sub = lax.broadcasted_iota(jnp.int32, (8, base[0].shape[-1]), 0)
    value = tuple(jnp.broadcast_to(part, sub.shape) for part in base)
    for k in range(3):
        picked = (sub & (1 << k)) != 0
        value = cmul(value, (jnp.where(picked, powers[k][0], 1.0), jnp.where(picked, powers[k][1], 0.0)))
    blocks = [value]
    k = 3
    while len(blocks) * 8 < rows:
        blocks = blocks + [cmul(block, powers[k]) for block in blocks]
        k += 1
    return tuple(jnp.concatenate([block[i] for block in blocks], axis=0)[:rows] for i in (0, 1))


def split(value):
    high = value.astype(jnp.bfloat16)
    return high, (value - high.astype(jnp.float32)).astype(jnp.bfloat16)


def dot_nt(a, b):
    return lax.dot_general(a, b, (((1,), (1,)), ((), ())), preferred_element_type=jnp.float32)


def source_kernel(freqs, wx, half, sizes, zslots, xslots, scale, chunks):
    sx, sy, sz = sizes
    xbits = max(3, (wx - 1).bit_length())
    ybits = max(3, (half - 1).bit_length())
    per = 4 // zslots
    main = 4 * xslots * wx

    def body(*refs):
        wave_ref, phase_ref = refs[:2]
        cots = refs[2 : 2 + chunks]
        coss = refs[2 + chunks : 2 + 2 * chunks]
        keep, send = refs[2 + 2 * chunks : 4 + 2 * chunks]
        xbase, xpow, ypow, acc_even, acc_odd = refs[4 + 2 * chunks :]
        ix, iy, iz = (lax.axis_index(name) for name in ("gx", "gy", "gz"))
        xbit, ybit, zbit = bits_of(sx), bits_of(sy), bits_of(zslots)
        starts = []
        for slot in range(xslots):
            code = gray(ix)
            for k in range(1, xbit):
                code = code ^ (((slot >> (xbit - 1 - k)) & 1) << k)
            starts.append((ungray(code, xbit) * wx).astype(jnp.float32))
        zcode = 0
        for k in range(zbit):
            zcode = zcode * 2 + ((gray(iz) >> k) & 1)
        ycode = gray(iy)
        center = (2 * half - 1) / 2.0
        which = lax.broadcasted_iota(jnp.int32, (freqs, 1), 0)
        wave = jnp.zeros((freqs, 1), jnp.float32)
        phase = jnp.zeros((freqs, 1), jnp.float32)
        for f in range(freqs):
            wave = jnp.where(which == f, wave_ref[f], wave)
            phase = jnp.where(which == f, phase_ref[f], phase)
        for n in range(chunks):
            along_x = wave * coss[n][0:1, :]
            along_y = wave * coss[n][1:2, :]
            origin = along_y * center - phase
            for xr in range(xslots):
                angle = along_x * starts[xr] + origin
                xbase[n, xr, 0] = jnp.cos(angle)
                xbase[n, xr, 1] = jnp.sin(angle)
            turn = doubled(small_turn(0.5 * along_x))
            for k in range(xbits):
                xpow[n, k, 0], xpow[n, k, 1] = turn
                turn = doubled(turn)
            turn = small_turn(0.5 * along_y)
            for k in range(ybits + 1):
                ypow[n, k, 0], ypow[n, k, 1] = turn
                turn = doubled(turn)
        acc_even[...] = jnp.zeros_like(acc_even)
        acc_odd[...] = jnp.zeros_like(acc_odd)

        def one(f, carry):
            firsts, seconds, coses, sines = [], [], [], []
            for n in range(chunks):
                def row(ref, *where):
                    return tuple(ref[(n, *where, i, pl.ds(f, 1), slice(None))] for i in (0, 1))

                powers = [row(ypow, k) for k in range(ybits + 1)]
                cy, sy_ = rotations(powers[0], powers[1:], half)
                coses.append(cy)
                sines.append(sy_)
                powers = [row(xpow, k) for k in range(xbits)]
                bases = [row(xbase, xr) for xr in range(xslots)]
                turns = [rotations(base, powers, wx) for base in bases]
                first, second = [], []
                for zr in range(zslots):
                    for xr in range(xslots):
                        cx, sx_ = turns[xr]
                        for c2 in range(per):
                            at = 2 * ((zcode ^ zr) * per + c2)
                            p = cots[n][f, pl.ds(at, 1), :]
                            q = cots[n][f, pl.ds(at + 1, 1), :]
                            first.append(p * cx - q * sx_)
                            second.append(p * sx_ + q * cx)
                back = (powers[0][0], -powers[0][1])
                p = cots[n][f, 6:7, :]
                q = cots[n][f, 7:8, :]
                line = lax.broadcasted_iota(jnp.int32, (8, p.shape[-1]), 0)
                one_first = jnp.zeros(line.shape, jnp.float32)
                one_second = one_first
                for xr in range(xslots):
                    cx, sx_ = cmul(bases[xr], back)
                    one_first = jnp.where(line == xr, p * cx - q * sx_, one_first)
                    one_second = jnp.where(line == xr, p * sx_ + q * cx, one_second)
                firsts.append(jnp.concatenate(first + [one_first], axis=0))
                seconds.append(jnp.concatenate(second + [one_second], axis=0))

            def product(lefts, rights):
                lh, ll = split(jnp.concatenate(lefts, axis=1))
                rh, rl = split(jnp.concatenate(rights, axis=1))
                return dot_nt(lh, rh) + dot_nt(lh, rl) + dot_nt(ll, rh)

            acc_even[...] += product(firsts, coses)
            acc_odd[...] += product(seconds, sines)
            return carry

        lax.fori_loop(0, freqs, one, 0)

        def slot(tile):
            code = gray(tile) ^ ycode
            place = 0
            for k in range(ybit):
                place = place * 2 + ((code >> k) & 1)
            return place

        def place(zr):
            return (keep, zr) if zr < zslots // 2 else (send, zr - zslots // 2)

        extra = per * wx
        for zr in range(zslots):
            ref, z = place(zr)
            for y in range(sy):
                for xr in range(xslots):
                    ref[z, y, xr, extra : extra + 8] = jnp.zeros((8, LANES), jnp.float32)
        turned = 2 // per
        spare = 2 % per
        for j in range(sy // 2):
            lanes = slice(j * LANES, (j + 1) * LANES)
            up = slot(sy // 2 + j)
            down = slot(sy // 2 - 1 - j)
            at = 0
            for zr in range(zslots):
                ref, z = place(zr)
                for xr in range(xslots):
                    for c2 in range(per):
                        rows = slice(at * wx, (at + 1) * wx)
                        even = acc_even[rows, lanes] * scale
                        odd = acc_odd[rows, lanes] * scale
                        ref[z, up, xr, c2 * wx : (c2 + 1) * wx] = even - odd
                        ref[z, down, xr, c2 * wx : (c2 + 1) * wx] = even + odd
                        at += 1
            for xr in range(xslots):
                even = acc_even[main + xr : main + xr + 1, lanes] * scale
                odd = acc_odd[main + xr : main + xr + 1, lanes] * scale
                for zr in range(zslots):
                    ref, z = place(zr)
                    ref[z, up, xr, extra : extra + 1] = even - odd
                    ref[z, down, xr, extra : extra + 1] = even + odd
                start = (((zcode ^ turned) * xslots + xr) * per + spare) * wx
                rows = pl.ds(pl.multiple_of(start, wx), wx)
                even = (acc_even[rows, lanes] * scale).T
                odd = (acc_odd[rows, lanes] * scale).T
                lower = slot(sy // 2 - j)
                for zr in range(zslots):
                    ref, z = place(zr)
                    ref[z, lower, xr, extra + 1 : extra + 2, 0:wx] = even[0:1] + odd[0:1]
                if j < sy // 2 - 1:
                    upper = slot(sy // 2 + j + 1)
                    for zr in range(zslots):
                        ref, z = place(zr)
                        ref[z, upper, xr, extra + 1 : extra + 2, 0:wx] = even[LANES - 1 :] - odd[LANES - 1 :]

    return body


def near_flags(index, bits):
    low, high = [], []
    for k in range(bits):
        upper = (index >> k) & 1
        rest = index & ((1 << k) - 1)
        low.append(((upper == 1) & (rest == 0)).astype(jnp.float32))
        high.append(((upper == 0) & (rest == (1 << k) - 1)).astype(jnp.float32))
    return low, high


def weighted(flags, values):
    total = flags[0] * values[0]
    for flag, value in zip(flags[1:], values[1:]):
        total = total + flag * value
    return total


def column_kernel(depth, wx, wy, zbits):
    def body(*refs):
        e, h, xe = refs[:3]
        zs = refs[3 : 3 + zbits]
        first, last = refs[3 + zbits :]
        low, high = near_flags(lax.axis_index("gz"), zbits)
        lane = lax.broadcasted_iota(jnp.int32, (1, LANES), 1)
        first[...] = jnp.zeros_like(first)
        last[...] = jnp.zeros_like(last)
        for i, field in enumerate((e[0], e[1], e[2], h[0], h[2])):
            turned = field.reshape(depth * wx, wy).T
            first[i : i + 1] = turned[0:1]
            last[i : i + 1] = turned[wy - 1 :]
        for i, layer in (
            (5, weighted(high, [z[1, 0:wx] for z in zs])),
            (6, weighted(low, [z[2, 0:wx] for z in zs])),
        ):
            turned = layer.T
            first[i : i + 1, 0:wx] = turned[0:1]
            last[i : i + 1, 0:wx] = turned[wy - 1 :]
        for ref, y in ((first, 0), (last, wy - 1)):
            corner = jnp.zeros((1, LANES), jnp.float32)
            for z in range(depth):
                corner = jnp.where(lane == z, xe[0, z : z + 1, y : y + 1], corner)
                corner = jnp.where(lane == z * wx + wx - 1, xe[1, z : z + 1, y : y + 1], corner)
            ref[7:8] = corner

    return body


def row_kernel(depth, wx, wy, zbits, ybits, k):
    def body(*refs):
        e, h = refs[:2]
        zs = refs[2 : 2 + zbits]
        ys = refs[2 + zbits : 2 + zbits + ybits]
        out = refs[2 + zbits + ybits]
        zlow, zhigh = near_flags(lax.axis_index("gz"), zbits)
        ylow, yhigh = near_flags(lax.axis_index("gy"), ybits)
        at = (1 - ((lax.axis_index("gx") >> k) & 1)) * (wx - 1)
        for i in range(3):
            for z in range(depth):
                out[i * depth + z : i * depth + z + 1] = e[i, z, pl.ds(at, 1), :]
                out[(3 + i) * depth + z : (3 + i) * depth + z + 1] = h[i, z, pl.ds(at, 1), :]
        base = 6 * depth
        out[base : base + 1] = weighted(zhigh, [z[0, pl.ds(at, 1), :] for z in zs])
        out[base + 1 : base + 2] = weighted(zlow, [z[2, pl.ds(at, 1), :] for z in zs])
        out[base + 2 : base + 3] = weighted(yhigh, [y[0:1] for y in ys])
        out[base + 3 : base + 4] = weighted(ylow, [y[1:2] for y in ys])
        out[base + 4 : base + 8] = jnp.zeros((4, LANES), jnp.float32)

    return body


def field_kernel(depth, wx, wy, xbits, ybits, zbits):
    def body(*refs):
        table, e, h, pole, material, first, xe = refs[:7]
        zs = refs[7 : 7 + zbits]
        ys = refs[7 + zbits : 7 + zbits + ybits]
        xs = refs[7 + zbits + ybits : 6 + zbits + ybits + xbits]
        e_out, h_out, pole_out, e_top, h_top, coef_top = refs[6 + zbits + ybits + xbits :]
        ix, iy, iz = (lax.axis_index(name) for name in ("gx", "gy", "gz"))
        xlow, xhigh = near_flags(ix, xbits)
        ylow, yhigh = near_flags(iy, ybits)
        zlow, zhigh = near_flags(iz, zbits)
        size = depth * wx
        base = 6 * depth
        lane = lax.broadcasted_iota(jnp.int32, (size, wy), 1)
        line = lax.broadcasted_iota(jnp.int32, (size, wy), 0) & (wx - 1)
        inside_x, inside_y, inside_z = (
            (index > 0).astype(jnp.float32) for index in (ix, iy, iz)
        )

        def flat(ref, i):
            return ref[i].reshape(size, wy)

        ex, ey, ez = (flat(e, i) for i in range(3))
        oldx, oldy, oldz = (flat(h, i) for i in range(3))

        def spread(rows):
            return jnp.broadcast_to(rows[:, None, :], (depth, wx, wy)).reshape(size, wy)

        def next_y(value, column):
            rows = value.shape[0]
            return jnp.where(lane[:rows] == wy - 1, column, pltpu.roll(value, wy - 1, 1))

        def next_x(value, rows):
            return jnp.where(line == wx - 1, spread(rows), pltpu.roll(value, size - 1, 0))

        def next_z(value, layer):
            return jnp.concatenate([value[wx:], layer], axis=0)

        def last_y(value, column):
            return jnp.where(lane == 0, column, pltpu.roll(value, 1, 1))

        def last_x(value, rows):
            return jnp.where(line == 0, spread(rows), pltpu.roll(value, 1, 0))

        def last_z(value, layer):
            return jnp.concatenate([layer, value[:-wx]], axis=0)

        ylo = weighted(ylow, [y[...] for y in ys])
        yhi = weighted(yhigh, [y[...] for y in ys])
        above = yhi.T

        def rows_of(flags, i):
            at = slice(i * depth, (i + 1) * depth)
            return weighted(flags, [xe[i]] + [x[at] for x in xs])

        def extra_of(flags, early, i):
            return weighted(flags, [early] + [x[base + i : base + i + 1] for x in xs])

        def layer_of(flags, i):
            return weighted(flags, [z[i, 0:wx] for z in zs])

        def side_of(flags, i):
            return weighted(flags, [z[i, wx : wx + 1] for z in zs])

        up_x, up_y = layer_of(zhigh, 0), layer_of(zhigh, 1)
        hx = oldx - courant * ((next_y(ez, above[:, 2:3]) - ez) - (next_z(ey, up_y) - ey))
        hy = oldy - courant * (
            (next_z(ex, up_x) - ex) - (next_x(ez, rows_of(xhigh, 2)) - ez)
        )
        hz = oldz - courant * (
            (next_x(ey, rows_of(xhigh, 1)) - ey) - (next_y(ex, above[:, 0:1]) - ex)
        )
        mx, my, mz = (rows_of(xlow, i) for i in range(3))
        up = jnp.concatenate([mx[1:], extra_of(xlow, side_of(zhigh, 0), 0)], axis=0)
        low_hy = rows_of(xlow, 4) - courant * ((up - mx) - (e[2, :, 0, :] - mz))
        corner = xlow[0] * above[0:depth, 7:8]
        for flag, x in zip(xlow[1:], xs):
            tail = x[base : base + 8].T
            picks = [tail[z * wx + wx - 1 : (z + 1) * wx, 2:3] for z in range(depth)]
            corner = corner + flag * jnp.concatenate(picks, axis=0)
        low_hz = rows_of(xlow, 5) - courant * (
            (e[1, :, 0, :] - my) - (next_y(mx, corner) - mx)
        )
        strip = lax.broadcasted_iota(jnp.int32, (1, LANES), 1)
        lx, ly, lz = ylo[0:1], ylo[1:2], ylo[2:3]
        up = jnp.where(
            strip >= size - wx, pltpu.roll(ylo[5:6], size - wx, 1), pltpu.roll(ly, LANES - wx, 1)
        )
        side_hx = ylo[3:4] - courant * ((first[2:3] - lz) - (up - ly))
        corner = xhigh[0] * ylo[7:8]
        for flag, x in zip(xhigh[1:], xs):
            corner = corner + flag * pltpu.roll(x[base + 3 : base + 4], wx - 1, 1)
        right = jnp.where((strip & (wx - 1)) == wx - 1, corner, pltpu.roll(ly, LANES - 1, 1))
        side_hz = ylo[4:5] - courant * ((right - ly) - (first[0:1] - lx))
        both = jnp.concatenate([side_hx, side_hz, jnp.zeros((6, LANES), jnp.float32)], axis=0)
        both = (inside_y * both).T
        bx, by, bz = (layer_of(zlow, i) for i in range(3))
        under_hx = layer_of(zlow, 3) - courant * (
            (next_y(bz, above[0:wx, 6:7]) - bz) - (ey[:wx] - by)
        )
        right = jnp.concatenate([bz[1:], extra_of(xhigh, side_of(zlow, 2), 1)], axis=0)
        under_hy = layer_of(zlow, 4) - courant * ((ex[:wx] - bx) - (right - bz))
        under_hx = inside_z * under_hx
        under_hy = inside_z * under_hy
        low_hy = inside_x * low_hy
        low_hz = inside_x * low_hz
        curl = (
            (hz - last_y(hz, both[:, 1:2])) - (hy - last_z(hy, under_hy)),
            (hx - last_z(hx, under_hx)) - (hz - last_x(hz, low_hz)),
            (hy - last_x(hy, low_hy)) - (hx - last_y(hx, both[:, 0:1])),
        )
        kind = material[...].reshape(size, wy)

        def chosen(i):
            value = jnp.full((size, wy), table[i, NPOLE - 1], jnp.float32)
            for m in range(NPOLE - 1):
                value = jnp.where(kind == m, table[i, m], value)
            return value

        decay, drive, coef = (chosen(i) for i in range(3))
        shape = (depth, wx, wy)
        tail = size - wx
        for i, (electric, magnetic) in enumerate(zip((ex, ey, ez), (hx, hy, hz))):
            old = flat(pole, i)
            new = decay * old + drive * electric
            value = electric + coef * (curl[i] - 0.5 * (new + old))
            pole_out[i] = new.reshape(shape)
            h_out[i] = magnetic.reshape(shape)
            e_out[i] = value.reshape(shape)
            e_top[i] = value[tail:]
            h_top[i] = magnetic[tail:]
        coef_top[...] = coef[tail:]

    return body


def inject_kernel(depth, wx, wy, sz, per):
    def body(source, col, e_top, h_top, coef_top, e_in, h_in, e_out, h_out, e_new, h_new, sems):
        ix, iy, iz = (lax.axis_index(name) for name in ("gx", "gy", "gz"))

        @pl.when(iz == sz - 1)
        def _():
            inside_x, inside_y = ((index > 0).astype(jnp.float32) for index in (ix, iy))
            lane = lax.broadcasted_iota(jnp.int32, (wx, wy), 1)
            line = lax.broadcasted_iota(jnp.int32, (wx, wy), 0)
            block = per * wx + 8

            def channel(c):
                start = (c // per) * block + (c % per) * wx
                return source[start : start + wx]

            electric_x, electric_y, magnetic_x, magnetic_y = (channel(c) for c in range(4))
            start = (3 // per) * block + per * wx
            before = inside_x * source[start : start + 1]
            beside = inside_y * col[...].T[0:wx, 1:2]
            last_x = jnp.where(line == 0, before, pltpu.roll(magnetic_y, 1, 0))
            last_y = jnp.where(lane == 0, beside, pltpu.roll(magnetic_x, 1, 1))
            coef = coef_top[...]
            h_new[0] = h_top[0] - courant * magnetic_x
            h_new[1] = h_top[1] - courant * magnetic_y
            e_new[0] = e_top[0] + coef * (courant * magnetic_y - electric_x)
            e_new[1] = e_top[1] - coef * (courant * magnetic_x + electric_y)
            e_new[2] = e_top[2] + coef * courant * (
                (magnetic_x - last_y) - (magnetic_y - last_x)
            )
            copies = [
                pltpu.make_async_copy(e_new, e_out.at[:, depth - 1], sems.at[0]),
                pltpu.make_async_copy(h_new, h_out.at[0:2, depth - 1], sems.at[1]),
            ]
            for copy in copies:
                copy.start()
            for copy in copies:
                copy.wait()

    return body


def in_vmem(*arrays):
    return [pltpu.with_memory_space_constraint(array, pltpu.VMEM) for array in arrays]


def local(
    e_field, h_field, pole_current, material, pole_table, cotangent, cosines, wavenumber, time_phase
):
    depth, wx, wy = material.shape
    sizes = sx, sy, sz = tuple(lax.axis_size(name) for name in ("gx", "gy", "gz"))
    ix, iy, iz = (lax.axis_index(name) for name in ("gx", "gy", "gz"))
    freqs, _, count = cotangent.shape
    scale = 1.0 / math.sqrt(freqs * count * sx * sy * sz)
    assert wy == LANES and depth * wx == LANES and sx > 1 and sy > 1 and sz > 1
    pad = -count % LANES
    if pad:
        cotangent = jnp.pad(cotangent, ((0, 0), (0, 0), (0, pad)))
        cosines = jnp.pad(cosines, ((0, 0), (0, pad)))
    f32 = jnp.float32
    smem = pl.BlockSpec(memory_space=pltpu.SMEM)
    vmem = pl.BlockSpec(memory_space=pltpu.VMEM)
    hbm = pl.BlockSpec(memory_space=pl.ANY)
    small = pltpu.CompilerParams(vmem_limit_bytes=8 << 20)
    xslots = sx // 2
    zslots = min(sz, 4)
    per = 4 // zslots
    xbits, ybits, zbits = bits_of(sx), bits_of(sy), bits_of(sz)
    zcut = bits_of(zslots)

    cots = [cotangent, exchange(cotangent, "gx", 1)]
    coss = [cosines, exchange(cosines, "gx", 1)]
    at = (1 - (ix & 1)) * (wx - 1)
    rows = [lax.dynamic_index_in_dim(v, at, 2, keepdims=False) for v in (e_field, h_field)]
    xe = exchange(jnp.concatenate(rows, axis=0), "gx", 1)
    zs = []
    for k in range(zbits):
        at = (1 - ((iz >> k) & 1)) * (depth - 1)
        layers = [lax.dynamic_index_in_dim(v, at, 1, keepdims=False) for v in (e_field, h_field)]
        side = lax.dynamic_slice_in_dim(xe, at, 1, axis=1)
        message = jnp.concatenate([jnp.concatenate(layers, axis=0), side], axis=1)
        zs.append(exchange(message, "gz", (2 << k) - 1))

    half = sy * wy // 2
    xlevels = max(3, (wx - 1).bit_length())
    ylevels = max(3, (half - 1).bit_length()) + 1
    width = count + pad
    block = per * wx + 8
    part_shape = pltpu.VMEM((zslots // 2, sy, xslots, block, wy), f32)
    keep, send = pl.pallas_call(
        source_kernel(freqs, wx, half, sizes, zslots, xslots, scale, 2),
        out_shape=(part_shape, part_shape),
        in_specs=[smem, smem] + [vmem] * 4,
        out_specs=(vmem, vmem),
        scratch_shapes=[
            pltpu.VMEM((2, xslots, 2, freqs, width), f32),
            pltpu.VMEM((2, xlevels, 2, freqs, width), f32),
            pltpu.VMEM((2, ylevels, 2, freqs, width), f32),
            pltpu.VMEM((4 * xslots * wx + 8, half), f32),
            pltpu.VMEM((4 * xslots * wx + 8, half), f32),
        ],
        compiler_params=pltpu.CompilerParams(vmem_limit_bytes=24 << 20),
        name="source",
    )(wavenumber, time_phase, *in_vmem(*cots, *coss))

    e_near, h_near = in_vmem(e_field, h_field)
    strip = pltpu.VMEM((8, LANES), f32)
    first, last = pl.pallas_call(
        column_kernel(depth, wx, wy, zbits),
        out_shape=(strip, strip),
        in_specs=[vmem] * (3 + zbits),
        out_specs=(vmem, vmem),
        compiler_params=small,
        name="columns",
    )(e_near, h_near, *in_vmem(xe, *zs))

    part = keep + exchange(send, "gz", 1)
    for k in range(1, zbits):
        mask = (2 << k) - 1
        if k < zcut:
            cut = part.shape[0] // 2
            part = part[:cut] + exchange(part[cut:], "gz", mask)
        else:
            part = part + exchange(part, "gz", mask)
    part = part[0]

    def swap(part, halo, axis, k):
        cut = part.shape[0] // 2
        away = part[cut:].reshape(-1, LANES)
        got = exchange(jnp.concatenate([away, halo], axis=0), axis, (2 << k) - 1)
        return part[:cut] + got[: away.shape[0]].reshape(part[:cut].shape), got[away.shape[0] :]

    ys = []
    for k in range(ybits):
        part, halo = swap(part, jnp.where((iy >> k) & 1 == 1, first, last), "gy", k)
        ys.append(halo)
    part = part[0]
    near = in_vmem(*zs, *ys)
    xs = []
    for k in range(1, xbits):
        halo = pl.pallas_call(
            row_kernel(depth, wx, wy, zbits, ybits, k),
            out_shape=pltpu.VMEM((6 * depth + 8, LANES), f32),
            in_specs=[vmem] * (2 + zbits + ybits),
            out_specs=vmem,
            compiler_params=small,
            name="rows",
        )(e_near, h_near, *near)
        part, halo = swap(part, halo, "gx", k)
        xs.append(halo)
    part = part[0]

    whole = jax.ShapeDtypeStruct((3, depth, wx, wy), f32)
    layer = pltpu.VMEM((3, wx, wy), f32)
    e_next, h_next, pole_next, e_top, h_top, coef_top = pl.pallas_call(
        field_kernel(depth, wx, wy, xbits, ybits, zbits),
        out_shape=(whole, whole, whole, layer, layer, pltpu.VMEM((wx, wy), f32)),
        in_specs=[smem] + [vmem] * (5 + xbits + ybits + zbits),
        out_specs=(vmem,) * 6,
        compiler_params=pltpu.CompilerParams(vmem_limit_bytes=16 << 20),
        name="fields",
    )(
        pole_table,
        e_near,
        h_near,
        *in_vmem(pole_current, material, first, xe),
        *near,
        *in_vmem(*xs),
    )

    top = gray(sz - 1)
    for k in reversed(range(zcut)):
        other = exchange(part, "gz", (2 << k) - 1)
        part = jnp.concatenate([other, part] if (top >> k) & 1 else [part, other], axis=0)
    flipped = iy < sy // 2
    source = jnp.where(flipped, part[:, ::-1], part)
    start = (2 // per) * block + per * wx
    col = part[start : start + 8]
    e_next, h_next = pl.pallas_call(
        inject_kernel(depth, wx, wy, sz, per),
        out_shape=(whole, whole),
        in_specs=[vmem] * 5 + [hbm] * 2,
        out_specs=(hbm, hbm),
        scratch_shapes=[
            pltpu.VMEM((3, wx, wy), f32),
            pltpu.VMEM((2, wx, wy), f32),
            pltpu.SemaphoreType.DMA((2,)),
        ],
        input_output_aliases={5: 0, 6: 1},
        compiler_params=small,
        name="inject",
    )(*in_vmem(source, col, e_top, h_top, coef_top), e_next, h_next)
    return (e_next, h_next, pole_next)


def solution(mesh):
    in_specs = (
        P(None, "gz", "gx", "gy"),
        P(None, "gz", "gx", "gy"),
        P(None, "gz", "gx", "gy"),
        P("gz", "gx", "gy"),
        P(),
        P(None, None, ("gx", "gy", "gz")),
        P(None, ("gx", "gy", "gz")),
        P(),
        P(),
    )
    out_specs = (P(None, "gz", "gx", "gy"), P(None, "gz", "gx", "gy"), P(None, "gz", "gx", "gy"))
    return jax.shard_map(local, mesh=mesh, in_specs=in_specs, out_specs=out_specs, check_vma=False)
```

time: 64.2 us -> 43 us (0.67)
  the two profiles are of different devices: /device:TPU:20 before, /device:TPU:1 now
where the time goes in v2:
time: 43 us; the launch traced here: 42.7 us
  starting transfers between devices  17.8 us (41%)
  Pallas kernels  11.8 us (27%)
  waiting for transfers between devices  9.3 us (22%)
  local copies, waits for them, and re-layouts  2.77 us (6%)
  between operations  0.85 us (2%)
    ppermute x9, starting transfers between devices, exchange(): lax.ppermute(array, axis, [(i, i ^ mask) for i in range(lax.axis_size(axi...  17.8 us
    ppermute x9, waiting for transfers between devices, exchange(): lax.ppermute(array, axis, [(i, i ^ mask) for i in range(lax.axis_size(axi...  9.3 us
    pallas_call x1, Pallas kernels, local(): pl.pallas_call(source_kernel(freqs, wx, half, sizes, zslots, xslots, scal...  8.88 us
    pallas_call x1, Pallas kernels, local(): pl.pallas_call(field_kernel(depth, wx, wy, xbits, ybits, zbits), out_shap...  1.86 us
    squeeze x1, local copies, waits for them, and re-layouts, local(): lax.dynamic_index_in_dim(v, at, 1, keepdims=False)  0.88 us
    dynamic_slice x1, local copies, waits for them, and re-layouts, local(): lax.dynamic_index_in_dim(v, at, 2, keepdims=False)  0.87 us
  transfers between devices with their start and end apart: 9, of which 6 were waited for; matrix products, arithmetic and copies ran while one was open for 2% of the time, Pallas kernels for 26%

profile of v2, /device:TPU:1, one launch (start us, length us, event | category | flops | bytes accessed | tf_op | source)
XLA Modules:
  0.0 42.7 jit_solution(11544129502514998848)
XLA Ops:
  0.6 0.0 copy-start.4
  0.6 0.9 %constant_dynamic-slice_fusion.1 = (f32[3,4,1,128]{3,2,1,0:T(1,128)S(1)}, f32[3,4,1,128]{3,2,1,0:T(1,128)S(1)}) fusion(f32[3,4,32,128]{3,2,1,0:T(8,128)} %refs_2_.3, s32[]{:T(128)S(6)} %select_n.35, f32[3,4,32,128]{3,2,1,0:T(8,128)} %refs_1_.7), kind=kLoop, calls=%fused_computation.19 | loop fusion | bytes 24580 | tf_op jit(solution)/shard_map/jit(dynamic_index_in_dim)/dynamic_slice | solution.py:508
  1.5 2.2 %collective-permute-start.3 = (f32[6,4,128]{2,1,0:T(4,128)S(1)}, f32[6,4,128]{2,1,0:T(4,128)S(1)}, u32[]{:S(2)}, u32[]{:S(2)}) collective-permute-start(f32[6,4,128]{2,1,0:T(4,128)S(1)} %pad_maximum_fusion.5), channel_id=1, source_target_pairs={{0,8},{8,0},{16,24},{24,16},{1,9},{9,1},{17,25},{25,17},{2,10},{10... | collective-permute-start | bytes 36872 | tf_op jit(solution)/shard_map/ppermute | solution.py:18
  3.7 0.0 copy-done.4
  3.7 0.1 collective-permute-start
  3.8 0.0 copy-start.1
  3.8 0.9 %dynamic-slice_bitcast_fusion = (f32[3,32,128]{2,1,0:T(8,128)S(1)}, f32[3,32,128]{2,1,0:T(8,128)S(1)}) fusion(f32[3,4,32,128]{3,2,1,0:T(8,128)} %refs_2_.3, s32[]{:T(128)S(6)} %select_n.36, f32[3,4,32,128]{3,2,1,0:T(8,128)} %refs_1_.7), kind=kLoop, calls=%fused_computation.8 | loop fusion | bytes 196612 | tf_op jit(solution)/shard_map/jit(dynamic_index_in_dim)/squeeze | solution.py:513
  4.7 0.0 copy-start
  4.7 0.1 collective-permute-done.3.refs_2_.refs_6_
  4.8 0.0 copy-start.6
  4.8 0.0 copy-start.7
  4.8 0.0 copy-start.8
  4.9 1.6 %collective-permute-start.4 = (f32[6,33,128]{2,1,0:T(8,128)S(1)}, f32[6,33,128]{2,1,0:T(8,128)S(1)}, u32[]{:S(2)}, u32[]{:S(2)}) collective-permute-start(f32[6,33,128]{2,1,0:T(8,128)S(1)} %pad_maximum_fusion.1), channel_id=1, source_target_pairs={{0,1},{1,0},{2,3},{3,2},{4,5},{5,4},{6,7},{7,6},{8,9},{9,8},{10,11... | collective-permute-start | bytes 304136 | tf_op jit(solution)/shard_map/ppermute | solution.py:18
  6.5 0.0 copy-done.6
  6.5 1.7 %collective-permute-start.1 = (f32[2,128]{1,0:T(2,128)S(1)}, f32[2,128]{1,0:T(2,128)S(1)}, u32[]{:S(2)}, u32[]{:S(2)}) collective-permute-start(f32[2,128]{1,0:T(2,128)S(1)} %copy-done.6), channel_id=1, source_target_pairs={{0,8},{8,0},{16,24},{24,16},{1,9},{9,1},{17,25},{25,17},{2,10},{10... | collective-permute-start | bytes 3080 | tf_op jit(solution)/shard_map/ppermute | solution.py:18
  8.2 1.0 %collective-permute-done.1.refs_5_ = f32[2,128]{1,0:T(2,128)S(1)} collective-permute-done((f32[2,128]{1,0:T(2,128)S(1)}, f32[2,128]{1,0:T(2,128)S(1)}, u32[]{:S(2)}, u32[]{:S(2)}) %collective-permute-start.1) | collective-permute-done | bytes 1056 | tf_op jit(solution)/shard_map/ppermute | solution.py:18
  9.2 0.0 collective-permute-done.refs_3_
  9.2 0.0 copy-done.7
  9.2 0.0 copy-done.8
  9.2 8.9 %source.1 = (f32[1,4,2,72,128]{4,3,2,1,0:T(8,128)S(1)}, f32[1,4,2,72,128]{4,3,2,1,0:T(8,128)S(1)}) custom-call(f32[16]{0:T(128)S(1)} %copy-done.7, f32[16]{0:T(128)S(1)} %copy-done.8, f32[16,8,128]{2,1,0:T(8,128)S(1)} %copy-done.4, f32[16,8,128]{2,1,0:T(8,128)S(1)} %collective-permute-done.refs_3_, f32[2,128]{1,0:T(2,128)S(1)} %copy-done.6, ...), custom_call_target="tpu_custom_call" | custom-call | tf_op jit(solution)/shard_map/source/pallas_call | solution.py:524
  18.1 1.5 %collective-permute-start.2 = (f32[1,4,2,72,128]{4,3,2,1,0:T(8,128)S(1)}, f32[1,4,2,72,128]{4,3,2,1,0:T(8,128)S(1)}, u32[]{:S(2)}, u32[]{:S(2)}) collective-permute-start(f32[1,4,2,72,128]{4,3,2,1,0:T(8,128)S(1)} %get-tuple-element.16), channel_id=1, source_target_pairs={{0,1},{1,0},{2,3},{3,2},{4,5},{5,4},{6,7},{7,6},{8,9},{9,8},{10,11... | collective-permute-start | bytes 884744 | tf_op jit(solution)/shard_map/ppermute | solution.py:18
  19.6 0.0 collective-permute-done.4.refs_3_.refs_2_.refs_7_
  19.6 0.0 copy-done.1
  19.6 0.0 copy-done
  19.6 0.2 columns.1
  19.8 0.9 %collective-permute-done.2 = f32[1,4,2,72,128]{4,3,2,1,0:T(8,128)S(1)} collective-permute-done((f32[1,4,2,72,128]{4,3,2,1,0:T(8,128)S(1)}, f32[1,4,2,72,128]{4,3,2,1,0:T(8,128)S(1)}, u32[]{:S(2)}, u32[]{:S(2)}) %collective-permute-start.2) | collective-permute-done | bytes 294944 | tf_op jit(solution)/shard_map/ppermute | solution.py:18
  20.9 1.7 %collective-permute-start.5 = (f32[296,128]{1,0:T(8,128)S(1)}, f32[296,128]{1,0:T(8,128)S(1)}, u32[]{:S(2)}, u32[]{:S(2)}) collective-permute-start(f32[296,128]{1,0:T(8,128)S(1)} %pad_maximum_fusion), channel_id=1, source_target_pairs={{0,2},{2,0},{4,6},{6,4},{1,3},{3,1},{5,7},{7,5},{8,10},{10,8},{12,... | collective-permute-start | bytes 454664 | tf_op jit(solution)/shard_map/ppermute | solution.py:18
  22.6 3.9 %collective-permute-done.5 = f32[296,128]{1,0:T(8,128)S(1)} collective-permute-done((f32[296,128]{1,0:T(8,128)S(1)}, f32[296,128]{1,0:T(8,128)S(1)}, u32[]{:S(2)}, u32[]{:S(2)}) %collective-permute-start.5) | collective-permute-done | bytes 151584 | tf_op jit(solution)/shard_map/ppermute | solution.py:18
  26.5 2.3 %collective-permute-start.6 = (f32[152,128]{1,0:T(8,128)S(1)}, f32[152,128]{1,0:T(8,128)S(1)}, u32[]{:S(2)}, u32[]{:S(2)}) collective-permute-start(f32[152,128]{1,0:T(8,128)S(1)} %pad_maximum_fusion.2), channel_id=1, source_target_pairs={{0,6},{2,4},{4,2},{6,0},{1,7},{3,5},{5,3},{7,1},{8,14},{10,12},{12... | collective-permute-start | bytes 233480 | tf_op jit(solution)/shard_map/ppermute | solution.py:18
  28.8 1.9 %collective-permute-done.6 = f32[152,128]{1,0:T(8,128)S(1)} collective-permute-done((f32[152,128]{1,0:T(8,128)S(1)}, f32[152,128]{1,0:T(8,128)S(1)}, u32[]{:S(2)}, u32[]{:S(2)}) %collective-permute-start.6) | collective-permute-done | bytes 77856 | tf_op jit(solution)/shard_map/ppermute | solution.py:18
  30.8 0.0 copy-start.3
  30.8 0.0 copy-start.2
  30.8 3.4 %collective-permute-start.7 = (f32[104,128]{1,0:T(8,128)S(1)}, f32[104,128]{1,0:T(8,128)S(1)}, u32[]{:S(2)}, u32[]{:S(2)}) collective-permute-start(f32[104,128]{1,0:T(8,128)S(1)} %pad_maximum_fusion.4), channel_id=1, source_target_pairs={{0,24},{8,16},{16,8},{24,0},{1,25},{9,17},{17,9},{25,1},{2,26},{10... | collective-permute-start | bytes 159752 | tf_op jit(solution)/shard_map/ppermute | solution.py:18
  34.3 1.5 %collective-permute-done.7 = f32[104,128]{1,0:T(8,128)S(1)} collective-permute-done((f32[104,128]{1,0:T(8,128)S(1)}, f32[104,128]{1,0:T(8,128)S(1)}, u32[]{:S(2)}, u32[]{:S(2)}) %collective-permute-start.7) | collective-permute-done | bytes 53280 | tf_op jit(solution)/shard_map/ppermute | solution.py:18
  35.8 3.2 %collective-permute-start.8 = (f32[72,128]{1,0:T(8,128)S(1)}, f32[72,128]{1,0:T(8,128)S(1)}, u32[]{:S(2)}, u32[]{:S(2)}) collective-permute-start(f32[72,128]{1,0:T(8,128)S(1)} %slice_add_fusion.1), channel_id=1, source_target_pairs={{0,1},{1,0},{2,3},{3,2},{4,5},{5,4},{6,7},{7,6},{8,9},{9,8},{10,11... | collective-permute-start | bytes 110600 | tf_op jit(solution)/shard_map/ppermute | solution.py:18
  39.1 0.0 copy-start.5
  39.1 0.0 copy-done.3
  39.1 0.0 copy-done.2
  39.1 0.7 %copy-done.5 = f32[3,4]{1,0:T(4,128)S(1)} copy-done((f32[3,4]{1,0:T(4,128)S(1)}, f32[3,4]{1,0:T(4,128)}, u32[]{:S(2)}) %copy-start.5) | copy-done | bytes 72
  39.8 1.9 %fields.1 = (f32[3,4,32,128]{3,2,1,0:T(8,128)}, f32[3,4,32,128]{3,2,1,0:T(8,128)}, f32[3,4,32,128]{3,2,1,0:T(8,128)}, f32[3,32,128]{2,1,0:T(8,128)S(1)}, f32[3,3...) custom-call(f32[3,4]{1,0:T(4,128)S(1)} %copy-done.5, f32[3,4,32,128]{3,2,1,0:T(8,128)S(1)} %copy-done, ...), custom_call_target="tpu_custom_call" | custom-call | tf_op jit(solution)/shard_map/fields/pallas_call | solution.py:589
  41.6 0.0 collective-permute-done.8
  41.6 0.3 rev.3
  41.9 0.8 %inject.1 = (f32[3,4,32,128]{3,2,1,0:T(8,128)}, f32[3,4,32,128]{3,2,1,0:T(8,128)}) custom-call(f32[144,128]{1,0:T(8,128)S(1)} %broadcast_select_fusion.source, f32[8,128]{1,0:T(8,128)S(1)} %slice_bitcast_fusion.3.col, f32[3,32,128]{2,1,0:T(8,128)S(1)} %get-tuple-element.19.e_top, ...), custom_call_target="tpu_custom_call", output_to_operand_aliasing={{0}: (5, {}), {1}: (6, {})} | custom-call | tf_op jit(solution)/shard_map/inject/pallas_call | solution.py:613
  (23 shorter events, 0.2 us)
Async XLA Ops:
  0.6 3.1 %copy-start.4 = (f32[16,8,128]{2,1,0:T(8,128)S(1)}, f32[16,8,128]{2,1,0:T(8,128)}, u32[]{:S(2)}) copy-start(f32[16,8,128]{2,1,0:T(8,128)} %refs_2_.2) | copy-start | bytes 196612
  1.5 3.3 %collective-permute-start.3 = (f32[6,4,128]{2,1,0:T(4,128)S(1)}, f32[6,4,128]{2,1,0:T(4,128)S(1)}, u32[]{:S(2)}, u32[]{:S(2)}) collective-permute-start(f32[6,4,128]{2,1,0:T(4,128)S(1)} %pad_maximum_fusion.5), channel_id=1, source_target_pairs={{0,8},{8,0},{16,24},{24,16},{1,9},{9,1},{17,25},{25,17},{2,10},{10... | collective-permute-start | bytes 36872 | tf_op jit(solution)/shard_map/ppermute | solution.py:18
  3.7 5.5 %collective-permute-start = (f32[16,8,128]{2,1,0:T(8,128)S(1)}, f32[16,8,128]{2,1,0:T(8,128)S(1)}, u32[]{:S(2)}, u32[]{:S(2)}) collective-permute-start(f32[16,8,128]{2,1,0:T(8,128)S(1)} %copy-done.4), channel_id=1, source_target_pairs={{0,8},{8,0},{16,24},{24,16},{1,9},{9,1},{17,25},{25,17},{2,10},{10... | collective-permute-start | bytes 196616 | tf_op jit(solution)/shard_map/ppermute | solution.py:18
  3.8 15.8 %copy-start.1 = (f32[3,4,32,128]{3,2,1,0:T(8,128)S(1)}, f32[3,4,32,128]{3,2,1,0:T(8,128)}, u32[]{:S(2)}) copy-start(f32[3,4,32,128]{3,2,1,0:T(8,128)} %refs_2_.3) | copy-start | bytes 589828
  4.7 14.9 %copy-start = (f32[3,4,32,128]{3,2,1,0:T(8,128)S(1)}, f32[3,4,32,128]{3,2,1,0:T(8,128)}, u32[]{:S(2)}) copy-start(f32[3,4,32,128]{3,2,1,0:T(8,128)} %refs_1_.7) | copy-start | bytes 589828
  4.8 1.7 %copy-start.6 = (f32[2,128]{1,0:T(2,128)S(1)}, f32[2,128]{1,0:T(2,128)}, u32[]{:S(2)}) copy-start(f32[2,128]{1,0:T(2,128)} %refs_4_.2) | copy-start | bytes 3076
  4.8 4.4 %copy-start.7 = (f32[16]{0:T(128)S(1)}, f32[16]{0:T(128)}, u32[]{:S(2)}) copy-start(f32[16]{0:T(128)} %refs_0_.4) | copy-start | bytes 196
  4.8 4.4 %copy-start.8 = (f32[16]{0:T(128)S(1)}, f32[16]{0:T(128)}, u32[]{:S(2)}) copy-start(f32[16]{0:T(128)} %refs_1_.4) | copy-start | bytes 196
  4.9 14.7 %collective-permute-start.4 = (f32[6,33,128]{2,1,0:T(8,128)S(1)}, f32[6,33,128]{2,1,0:T(8,128)S(1)}, u32[]{:S(2)}, u32[]{:S(2)}) collective-permute-start(f32[6,33,128]{2,1,0:T(8,128)S(1)} %pad_maximum_fusion.1), channel_id=1, source_target_pairs={{0,1},{1,0},{2,3},{3,2},{4,5},{5,4},{6,7},{7,6},{8,9},{9,8},{10,11... | collective-permute-start | bytes 304136 | tf_op jit(solution)/shard_map/ppermute | solution.py:18
  6.5 2.7 %collective-permute-start.1 = (f32[2,128]{1,0:T(2,128)S(1)}, f32[2,128]{1,0:T(2,128)S(1)}, u32[]{:S(2)}, u32[]{:S(2)}) collective-permute-start(f32[2,128]{1,0:T(2,128)S(1)} %copy-done.6), channel_id=1, source_target_pairs={{0,8},{8,0},{16,24},{24,16},{1,9},{9,1},{17,25},{25,17},{2,10},{10... | collective-permute-start | bytes 3080 | tf_op jit(solution)/shard_map/ppermute | solution.py:18
  18.1 2.7 %collective-permute-start.2 = (f32[1,4,2,72,128]{4,3,2,1,0:T(8,128)S(1)}, f32[1,4,2,72,128]{4,3,2,1,0:T(8,128)S(1)}, u32[]{:S(2)}, u32[]{:S(2)}) collective-permute-start(f32[1,4,2,72,128]{4,3,2,1,0:T(8,128)S(1)} %get-tuple-element.16), channel_id=1, source_target_pairs={{0,1},{1,0},{2,3},{3,2},{4,5},{5,4},{6,7},{7,6},{8,9},{9,8},{10,11... | collective-permute-start | bytes 884744 | tf_op jit(solution)/shard_map/ppermute | solution.py:18
  20.9 5.6 %collective-permute-start.5 = (f32[296,128]{1,0:T(8,128)S(1)}, f32[296,128]{1,0:T(8,128)S(1)}, u32[]{:S(2)}, u32[]{:S(2)}) collective-permute-start(f32[296,128]{1,0:T(8,128)S(1)} %pad_maximum_fusion), channel_id=1, source_target_pairs={{0,2},{2,0},{4,6},{6,4},{1,3},{3,1},{5,7},{7,5},{8,10},{10,8},{12,... | collective-permute-start | bytes 454664 | tf_op jit(solution)/shard_map/ppermute | solution.py:18
  26.5 4.2 %collective-permute-start.6 = (f32[152,128]{1,0:T(8,128)S(1)}, f32[152,128]{1,0:T(8,128)S(1)}, u32[]{:S(2)}, u32[]{:S(2)}) collective-permute-start(f32[152,128]{1,0:T(8,128)S(1)} %pad_maximum_fusion.2), channel_id=1, source_target_pairs={{0,6},{2,4},{4,2},{6,0},{1,7},{3,5},{5,3},{7,1},{8,14},{10,12},{12... | collective-permute-start | bytes 233480 | tf_op jit(solution)/shard_map/ppermute | solution.py:18
  30.8 8.3 %copy-start.3 = (s32[4,32,128]{2,1,0:T(8,128)S(1)}, s32[4,32,128]{2,1,0:T(8,128)}, u32[]{:S(2)}) copy-start(s32[4,32,128]{2,1,0:T(8,128)} %refs_4_.3) | copy-start | bytes 196612
  30.8 8.3 %copy-start.2 = (f32[3,4,32,128]{3,2,1,0:T(8,128)S(1)}, f32[3,4,32,128]{3,2,1,0:T(8,128)}, u32[]{:S(2)}) copy-start(f32[3,4,32,128]{3,2,1,0:T(8,128)} %refs_3_.1) | copy-start | bytes 589828
  30.8 5.0 %collective-permute-start.7 = (f32[104,128]{1,0:T(8,128)S(1)}, f32[104,128]{1,0:T(8,128)S(1)}, u32[]{:S(2)}, u32[]{:S(2)}) collective-permute-start(f32[104,128]{1,0:T(8,128)S(1)} %pad_maximum_fusion.4), channel_id=1, source_target_pairs={{0,24},{8,16},{16,8},{24,0},{1,25},{9,17},{17,9},{25,1},{2,26},{10... | collective-permute-start | bytes 159752 | tf_op jit(solution)/shard_map/ppermute | solution.py:18
  35.8 5.8 %collective-permute-start.8 = (f32[72,128]{1,0:T(8,128)S(1)}, f32[72,128]{1,0:T(8,128)S(1)}, u32[]{:S(2)}, u32[]{:S(2)}) collective-permute-start(f32[72,128]{1,0:T(8,128)S(1)} %slice_add_fusion.1), channel_id=1, source_target_pairs={{0,1},{1,0},{2,3},{3,2},{4,5},{5,4},{6,7},{7,6},{8,9},{9,8},{10,11... | collective-permute-start | bytes 110600 | tf_op jit(solution)/shard_map/ppermute | solution.py:18
  39.1 0.7 %copy-start.5 = (f32[3,4]{1,0:T(4,128)S(1)}, f32[3,4]{1,0:T(4,128)}, u32[]{:S(2)}) copy-start(f32[3,4]{1,0:T(4,128)} %refs_0_.7) | copy-start | bytes 148

commit v3 on v2

--- a/solution.py
+++ b/solution.py
@@ -80,11 +80,10 @@
     main = 4 * xslots * wx
 
     def body(*refs):
-        wave_ref, phase_ref = refs[:2]
-        cots = refs[2 : 2 + chunks]
-        coss = refs[2 + chunks : 2 + 2 * chunks]
-        keep, send = refs[2 + 2 * chunks : 4 + 2 * chunks]
-        xbase, xpow, ypow, acc_even, acc_odd = refs[4 + 2 * chunks :]
+        waves = refs[0]
+        cots = refs[1 : 1 + chunks]
+        keep, send = refs[1 + chunks : 3 + chunks]
+        xbase, xpow, ypow, acc_even, acc_odd = refs[3 + chunks :]
         ix, iy, iz = (lax.axis_index(name) for name in ("gx", "gy", "gz"))
         xbit, ybit, zbit = bits_of(sx), bits_of(sy), bits_of(zslots)
         starts = []
@@ -98,15 +97,10 @@
             zcode = zcode * 2 + ((gray(iz) >> k) & 1)
         ycode = gray(iy)
         center = (2 * half - 1) / 2.0
-        which = lax.broadcasted_iota(jnp.int32, (freqs, 1), 0)
-        wave = jnp.zeros((freqs, 1), jnp.float32)
-        phase = jnp.zeros((freqs, 1), jnp.float32)
-        for f in range(freqs):
-            wave = jnp.where(which == f, wave_ref[f], wave)
-            phase = jnp.where(which == f, phase_ref[f], phase)
+        wave, phase = waves[0], waves[1]
         for n in range(chunks):
-            along_x = wave * coss[n][0:1, :]
-            along_y = wave * coss[n][1:2, :]
+            along_x = wave * cots[n][freqs, 0:1, :]
+            along_y = wave * cots[n][freqs, 1:2, :]
             origin = along_y * center - phase
             for xr in range(xslots):
                 angle = along_x * starts[xr] + origin
@@ -244,9 +238,60 @@
     return total
 
 
-def column_kernel(depth, wx, wy, zbits):
+def pack_kernel(freqs, depth, wx, zbits):
     def body(*refs):
-        e, h, xe = refs[:3]
+        e_in, h_in, cotangent, cosines, wavenumber, time_phase = refs[:6]
+        message, waves, e, h = refs[6:10]
+        layers = refs[10 : 10 + zbits]
+        cos_near, wave_near, phase_near, sems = refs[10 + zbits :]
+        copies = [
+            pltpu.make_async_copy(source, target, sems.at[i])
+            for i, (source, target) in enumerate(
+                (
+                    (e_in, e),
+                    (h_in, h),
+                    (cotangent, message.at[0:freqs]),
+                    (cosines, cos_near),
+                    (wavenumber, wave_near),
+                    (time_phase, phase_near),
+                )
+            )
+        ]
+        for copy in copies:
+            copy.start()
+        for copy in copies:
+            copy.wait()
+        message[freqs, 0:2] = cos_near[...]
+        message[freqs, 2:8] = jnp.zeros((6, LANES), jnp.float32)
+        which = lax.broadcasted_iota(jnp.int32, (freqs, LANES), 0)
+        for i, near in enumerate((wave_near, phase_near)):
+            value = jnp.zeros((freqs, LANES), jnp.float32)
+            for f in range(freqs):
+                value = jnp.where(which == f, near[f], value)
+            waves[i] = value
+        at = (1 - (lax.axis_index("gx") & 1)) * (wx - 1)
+        for i in range(6):
+            for z in range(depth):
+                row = i * depth + z
+                field = (e, h)[i // 3]
+                message[freqs + 1 + row // 8, row % 8 : row % 8 + 1] = field[i % 3, z, pl.ds(at, 1), :]
+        for k, layer in enumerate(layers):
+            at_z = (1 - ((lax.axis_index("gz") >> k) & 1)) * (depth - 1)
+            for i in range(3):
+                layer[i] = e[i, at_z]
+                layer[3 + i] = h[i, at_z]
+
+    return body
+
+
+def early_rows(message, freqs, depth, i):
+    row = i * depth
+    return message[freqs + 1 + row // 8, row % 8 : row % 8 + depth]
+
+
+def column_kernel(freqs, depth, wx, wy, zbits):
+    def body(*refs):
+        e, h, message = refs[:3]
         zs = refs[3 : 3 + zbits]
         first, last = refs[3 + zbits :]
         low, high = near_flags(lax.axis_index("gz"), zbits)
@@ -266,44 +311,115 @@
             last[i : i + 1, 0:wx] = turned[wy - 1 :]
         for ref, y in ((first, 0), (last, wy - 1)):
             corner = jnp.zeros((1, LANES), jnp.float32)
+            side_x, side_y = (early_rows(message, freqs, depth, i)[:, y : y + 1] for i in (0, 1))
             for z in range(depth):
-                corner = jnp.where(lane == z, xe[0, z : z + 1, y : y + 1], corner)
-                corner = jnp.where(lane == z * wx + wx - 1, xe[1, z : z + 1, y : y + 1], corner)
+                corner = jnp.where(lane == z, side_x[z : z + 1], corner)
+                corner = jnp.where(lane == z * wx + wx - 1, side_y[z : z + 1], corner)
             ref[7:8] = corner
 
     return body
 
 
-def row_kernel(depth, wx, wy, zbits, ybits, k):
+def total_of(terms, rows):
+    value = terms[0][rows]
+    for term in terms[1:]:
+        value = value + term[rows]
+    return value
+
+
+def merge_y_kernel(count, rows, k, ybits):
     def body(*refs):
-        e, h = refs[:2]
-        zs = refs[2 : 2 + zbits]
-        ys = refs[2 + zbits : 2 + zbits + ybits]
-        out = refs[2 + zbits + ybits]
+        terms, (first, last), outs = refs[:count], refs[count : count + 2], refs[count + 2 :]
+        iy = lax.axis_index("gy")
+        size = rows // len(outs)
+        swaps = (None, k) if len(outs) == 2 else (None, k + 1, k, None)
+        for i, (out, swap) in enumerate(zip(outs, swaps)):
+            out[0:size] = total_of(terms, slice(i * size, (i + 1) * size))
+            if swap is not None:
+                upper = ((iy >> swap) & 1).astype(jnp.float32)
+                out[size : size + 8] = upper * first[...] + (1.0 - upper) * last[...]
+
+    return body
+
+
+def halo_at(ref):
+    rows = ref.shape[0]
+    return ref[rows - 8 : rows]
+
+
+def merge_x_kernel(count, rows, depth, wx, wy, zbits, ybits, k):
+    def body(*refs):
+        terms = refs[:count]
+        e, h = refs[count : count + 2]
+        zs = refs[count + 2 : count + 2 + zbits]
+        ys = refs[count + 2 + zbits : count + 2 + zbits + ybits]
+        keep, out = refs[count + 3 + zbits + ybits :]
+        size = rows // 2
+        keep[...] = total_of(terms, slice(0, size))
+        out[0:size] = total_of(terms, slice(size, rows))
         zlow, zhigh = near_flags(lax.axis_index("gz"), zbits)
         ylow, yhigh = near_flags(lax.axis_index("gy"), ybits)
         at = (1 - ((lax.axis_index("gx") >> k) & 1)) * (wx - 1)
         for i in range(3):
             for z in range(depth):
-                out[i * depth + z : i * depth + z + 1] = e[i, z, pl.ds(at, 1), :]
-                out[(3 + i) * depth + z : (3 + i) * depth + z + 1] = h[i, z, pl.ds(at, 1), :]
-        base = 6 * depth
+                row = size + i * depth + z
+                out[row : row + 1] = e[i, z, pl.ds(at, 1), :]
+                row = size + (3 + i) * depth + z
+                out[row : row + 1] = h[i, z, pl.ds(at, 1), :]
+        base = size + 6 * depth
+        halos = [halo_at(y) for y in ys]
         out[base : base + 1] = weighted(zhigh, [z[0, pl.ds(at, 1), :] for z in zs])
         out[base + 1 : base + 2] = weighted(zlow, [z[2, pl.ds(at, 1), :] for z in zs])
-        out[base + 2 : base + 3] = weighted(yhigh, [y[0:1] for y in ys])
-        out[base + 3 : base + 4] = weighted(ylow, [y[1:2] for y in ys])
+        out[base + 2 : base + 3] = weighted(yhigh, [y[0:1] for y in halos])
+        out[base + 3 : base + 4] = weighted(ylow, [y[1:2] for y in halos])
         out[base + 4 : base + 8] = jnp.zeros((4, LANES), jnp.float32)
 
     return body
 
 
-def field_kernel(depth, wx, wy, xbits, ybits, zbits):
+def pole_kernel(depth, wx, wy):
+    def body(table_in, e, pole_in, material_in, after, pole_out, base, coef_out, *scratch):
+        table, pole, material, new_pole, sems = scratch
+        copies = [
+            pltpu.make_async_copy(source, target, sems.at[i])
+            for i, (source, target) in enumerate(
+                ((table_in, table), (material_in, material), (pole_in, pole))
+            )
+        ]
+        for copy in copies:
+            copy.start()
+        for copy in copies:
+            copy.wait()
+        kind = material[...]
+
+        def chosen(i):
+            value = jnp.full(kind.shape, table[i, NPOLE - 1], jnp.float32)
+            for m in range(NPOLE - 1):
+                value = jnp.where(kind == m, table[i, m], value)
+            return value
+
+        decay, drive, coef = (chosen(i) for i in range(3))
+        coef_out[...] = coef
+        for i in range(3):
+            old = pole[i]
+            electric = e[i]
+            new = decay * old + drive * electric
+            new_pole[i] = new
+            base[i] = electric - coef * (0.5 * (new + old))
+        copy = pltpu.make_async_copy(new_pole, pole_out, sems.at[0])
+        copy.start()
+        copy.wait()
+
+    return body
+
+
+def field_kernel(freqs, depth, wx, wy, xbits, ybits, zbits):
     def body(*refs):
-        table, e, h, pole, material, first, xe = refs[:7]
-        zs = refs[7 : 7 + zbits]
-        ys = refs[7 + zbits : 7 + zbits + ybits]
-        xs = refs[7 + zbits + ybits : 6 + zbits + ybits + xbits]
-        e_out, h_out, pole_out, e_top, h_top, coef_top = refs[6 + zbits + ybits + xbits :]
+        e, h, base_e, coef_ref, first, message = refs[:6]
+        zs = refs[6 : 6 + zbits]
+        ys = refs[6 + zbits : 6 + zbits + ybits]
+        xs = [x[x.shape[0] - 6 * depth - 8 :] for x in refs[6 + zbits + ybits : 5 + zbits + ybits + xbits]]
+        e_out, h_out, e_top, h_top, coef_top = refs[5 + zbits + ybits + xbits :]
         ix, iy, iz = (lax.axis_index(name) for name in ("gx", "gy", "gz"))
         xlow, xhigh = near_flags(ix, xbits)
         ylow, yhigh = near_flags(iy, ybits)
@@ -344,13 +460,13 @@
         def last_z(value, layer):
             return jnp.concatenate([layer, value[:-wx]], axis=0)
 
-        ylo = weighted(ylow, [y[...] for y in ys])
-        yhi = weighted(yhigh, [y[...] for y in ys])
+        ylo = weighted(ylow, [halo_at(y) for y in ys])
+        yhi = weighted(yhigh, [halo_at(y) for y in ys])
         above = yhi.T
 
         def rows_of(flags, i):
             at = slice(i * depth, (i + 1) * depth)
-            return weighted(flags, [xe[i]] + [x[at] for x in xs])
+            return weighted(flags, [early_rows(message, freqs, depth, i)] + [x[at] for x in xs])
 
         def extra_of(flags, early, i):
             return weighted(flags, [early] + [x[base + i : base + i + 1] for x in xs])
@@ -408,22 +524,11 @@
             (hx - last_z(hx, under_hx)) - (hz - last_x(hz, low_hz)),
             (hy - last_x(hy, low_hy)) - (hx - last_y(hx, both[:, 0:1])),
         )
-        kind = material[...].reshape(size, wy)
-
-        def chosen(i):
-            value = jnp.full((size, wy), table[i, NPOLE - 1], jnp.float32)
-            for m in range(NPOLE - 1):
-                value = jnp.where(kind == m, table[i, m], value)
-            return value
-
-        decay, drive, coef = (chosen(i) for i in range(3))
+        coef = coef_ref[...].reshape(size, wy)
         shape = (depth, wx, wy)
         tail = size - wx
-        for i, (electric, magnetic) in enumerate(zip((ex, ey, ez), (hx, hy, hz))):
-            old = flat(pole, i)
-            new = decay * old + drive * electric
-            value = electric + coef * (curl[i] - 0.5 * (new + old))
-            pole_out[i] = new.reshape(shape)
+        for i, magnetic in enumerate((hx, hy, hz)):
+            value = flat(base_e, i) + coef * curl[i]
             h_out[i] = magnetic.reshape(shape)
             e_out[i] = value.reshape(shape)
             e_top[i] = value[tail:]
@@ -433,8 +538,10 @@
     return body
 
 
-def inject_kernel(depth, wx, wy, sz, per):
-    def body(source, col, e_top, h_top, coef_top, e_in, h_in, e_out, h_out, e_new, h_new, sems):
+def inject_kernel(depth, wx, wy, sy, sz, per, zcut):
+    def body(*refs):
+        blocks = refs[: 1 << zcut]
+        e_top, h_top, coef_top, e_in, h_in, e_out, h_out, e_new, h_new, sems = refs[1 << zcut :]
         ix, iy, iz = (lax.axis_index(name) for name in ("gx", "gy", "gz"))
 
         @pl.when(iz == sz - 1)
@@ -442,16 +549,28 @@
             inside_x, inside_y = ((index > 0).astype(jnp.float32) for index in (ix, iy))
             lane = lax.broadcasted_iota(jnp.int32, (wx, wy), 1)
             line = lax.broadcasted_iota(jnp.int32, (wx, wy), 0)
-            block = per * wx + 8
+            flip = (
+                lax.broadcasted_iota(jnp.int32, (wy, wy), 0)
+                + lax.broadcasted_iota(jnp.int32, (wy, wy), 1)
+                == wy - 1
+            ).astype(jnp.float32)
+            flipped = iy < sy // 2
+
+            def straight(value):
+                turned = jnp.dot(
+                    value, flip, precision=lax.Precision.HIGHEST, preferred_element_type=jnp.float32
+                )
+                return jnp.where(flipped, turned, value)
+
+            tiles = [straight(ref[...]) for ref in blocks]
 
             def channel(c):
-                start = (c // per) * block + (c % per) * wx
-                return source[start : start + wx]
+                start = (c % per) * wx
+                return tiles[c // per][start : start + wx]
 
             electric_x, electric_y, magnetic_x, magnetic_y = (channel(c) for c in range(4))
-            start = (3 // per) * block + per * wx
-            before = inside_x * source[start : start + 1]
-            beside = inside_y * col[...].T[0:wx, 1:2]
+            before = inside_x * tiles[3 // per][per * wx : per * wx + 1]
+            beside = inside_y * blocks[2 // per][per * wx : per * wx + 8].T[0:wx, 1:2]
             last_x = jnp.where(line == 0, before, pltpu.roll(magnetic_y, 1, 0))
             last_y = jnp.where(lane == 0, beside, pltpu.roll(magnetic_x, 1, 1))
             coef = coef_top[...]
@@ -474,6 +593,10 @@
     return body
 
 
+def in_hbm(*arrays):
+    return [pltpu.with_memory_space_constraint(array, pltpu.HBM) for array in arrays]
+
+
 def in_vmem(*arrays):
     return [pltpu.with_memory_space_constraint(array, pltpu.VMEM) for array in arrays]
 
@@ -494,7 +617,7 @@
     f32 = jnp.float32
     smem = pl.BlockSpec(memory_space=pltpu.SMEM)
     vmem = pl.BlockSpec(memory_space=pltpu.VMEM)
-    hbm = pl.BlockSpec(memory_space=pl.ANY)
+    hbm = pl.BlockSpec(memory_space=pltpu.HBM)
     small = pltpu.CompilerParams(vmem_limit_bytes=8 << 20)
     xslots = sx // 2
     zslots = min(sz, 4)
@@ -502,18 +625,35 @@
     xbits, ybits, zbits = bits_of(sx), bits_of(sy), bits_of(sz)
     zcut = bits_of(zslots)
 
-    cots = [cotangent, exchange(cotangent, "gx", 1)]
-    coss = [cosines, exchange(cosines, "gx", 1)]
-    at = (1 - (ix & 1)) * (wx - 1)
-    rows = [lax.dynamic_index_in_dim(v, at, 2, keepdims=False) for v in (e_field, h_field)]
-    xe = exchange(jnp.concatenate(rows, axis=0), "gx", 1)
+    assert 8 % depth == 0
+    mine, waves, e_near, h_near, *layers = pl.pallas_call(
+        pack_kernel(freqs, depth, wx, zbits),
+        out_shape=[
+            pltpu.VMEM((freqs + 1 + 6 * depth // 8, 8, LANES), f32),
+            pltpu.VMEM((2, freqs, LANES), f32),
+            pltpu.VMEM(e_field.shape, f32),
+            pltpu.VMEM(h_field.shape, f32),
+        ]
+        + [pltpu.VMEM((6, wx, wy), f32)] * zbits,
+        in_specs=[hbm] * 6,
+        out_specs=[vmem] * (4 + zbits),
+        scratch_shapes=[
+            pltpu.VMEM((2, LANES), f32),
+            pltpu.SMEM((freqs,), f32),
+            pltpu.SMEM((freqs,), f32),
+            pltpu.SemaphoreType.DMA((6,)),
+        ],
+        compiler_params=small,
+        name="pack",
+    )(*in_hbm(e_field, h_field, cotangent, cosines, wavenumber, time_phase))
+    e_near, h_near = in_vmem(e_near, h_near)
+    theirs = exchange(mine, "gx", 1)
+    side = theirs[freqs + 1 :].reshape(6, depth, LANES)
     zs = []
     for k in range(zbits):
         at = (1 - ((iz >> k) & 1)) * (depth - 1)
-        layers = [lax.dynamic_index_in_dim(v, at, 1, keepdims=False) for v in (e_field, h_field)]
-        side = lax.dynamic_slice_in_dim(xe, at, 1, axis=1)
-        message = jnp.concatenate([jnp.concatenate(layers, axis=0), side], axis=1)
-        zs.append(exchange(message, "gz", (2 << k) - 1))
+        row = lax.dynamic_slice_in_dim(side, at, 1, axis=1)
+        zs.append(exchange(jnp.concatenate([layers[k], row], axis=1), "gz", (2 << k) - 1))
 
     half = sy * wy // 2
     xlevels = max(3, (wx - 1).bit_length())
@@ -524,7 +664,7 @@
     keep, send = pl.pallas_call(
         source_kernel(freqs, wx, half, sizes, zslots, xslots, scale, 2),
         out_shape=(part_shape, part_shape),
-        in_specs=[smem, smem] + [vmem] * 4,
+        in_specs=[vmem] * 3,
         out_specs=(vmem, vmem),
         scratch_shapes=[
             pltpu.VMEM((2, xslots, 2, freqs, width), f32),
@@ -535,95 +675,125 @@
         ],
         compiler_params=pltpu.CompilerParams(vmem_limit_bytes=24 << 20),
         name="source",
-    )(wavenumber, time_phase, *in_vmem(*cots, *coss))
-
-    e_near, h_near = in_vmem(e_field, h_field)
+    )(*in_vmem(waves, mine, theirs))
+
     strip = pltpu.VMEM((8, LANES), f32)
     first, last = pl.pallas_call(
-        column_kernel(depth, wx, wy, zbits),
+        column_kernel(freqs, depth, wx, wy, zbits),
         out_shape=(strip, strip),
         in_specs=[vmem] * (3 + zbits),
         out_specs=(vmem, vmem),
         compiler_params=small,
         name="columns",
-    )(e_near, h_near, *in_vmem(xe, *zs))
-
-    part = keep + exchange(send, "gz", 1)
+    )(e_near, h_near, *in_vmem(theirs, *zs))
+
+    whole = jax.ShapeDtypeStruct((3, depth, wx, wy), f32)
+    pole_next, base_e, coef = pl.pallas_call(
+        pole_kernel(depth, wx, wy),
+        out_shape=(whole, pltpu.VMEM(whole.shape, f32), pltpu.VMEM((depth, wx, wy), f32)),
+        in_specs=[hbm, vmem, hbm, hbm, vmem],
+        out_specs=(hbm, vmem, vmem),
+        scratch_shapes=[
+            pltpu.SMEM(pole_table.shape, f32),
+            pltpu.VMEM(whole.shape, f32),
+            pltpu.VMEM((depth, wx, wy), jnp.int32),
+            pltpu.VMEM(whole.shape, f32),
+            pltpu.SemaphoreType.DMA((3,)),
+        ],
+        compiler_params=small,
+        name="pole",
+    )(*in_hbm(pole_table), e_near, *in_hbm(pole_current, material), *in_vmem(first))
+    base_e, coef = in_vmem(base_e, coef)
+
+    def flat(value):
+        return value.reshape(-1, LANES)
+
+    terms = [keep, exchange(send, "gz", 1)]
     for k in range(1, zbits):
+        part = terms[0] + terms[1]
         mask = (2 << k) - 1
         if k < zcut:
-            cut = part.shape[0] // 2
-            part = part[:cut] + exchange(part[cut:], "gz", mask)
+            middle = part.shape[0] // 2
+            terms = [part[:middle], exchange(part[middle:], "gz", mask)]
         else:
-            part = part + exchange(part, "gz", mask)
-    part = part[0]
-
-    def swap(part, halo, axis, k):
-        cut = part.shape[0] // 2
-        away = part[cut:].reshape(-1, LANES)
-        got = exchange(jnp.concatenate([away, halo], axis=0), axis, (2 << k) - 1)
-        return part[:cut] + got[: away.shape[0]].reshape(part[:cut].shape), got[away.shape[0] :]
-
-    ys = []
-    for k in range(ybits):
-        part, halo = swap(part, jnp.where((iy >> k) & 1 == 1, first, last), "gy", k)
-        ys.append(halo)
-    part = part[0]
+            terms = [part, exchange(part, "gz", mask)]
+    terms = [flat(term) for term in terms]
+    rows = sy * xslots * block
+
+    ys = [None] * ybits
+    k = 0
+    while k < ybits:
+        both = k + 1 < ybits
+        size = rows // 4 if both else rows // 2
+        plain, laden = pltpu.VMEM((size, LANES), f32), pltpu.VMEM((size + 8, LANES), f32)
+        shapes = (plain, laden, laden, plain) if both else (plain, laden)
+        keep, *away = pl.pallas_call(
+            merge_y_kernel(len(terms), rows, k, ybits),
+            out_shape=shapes,
+            in_specs=[vmem] * (len(terms) + 2),
+            out_specs=(vmem,) * len(shapes),
+            compiler_params=small,
+            name="merge_y",
+        )(*in_vmem(*terms, first, last))
+        if both:
+            ys[k] = exchange(away[1], "gy", (2 << k) - 1)
+            other = exchange(away[2], "gy", 2 << k)
+            ys[k + 1] = exchange(away[0], "gy", (4 << k) - 1)
+            terms = [keep, ys[k], ys[k + 1], other]
+            k += 2
+        else:
+            ys[k] = exchange(away[0], "gy", (2 << k) - 1)
+            terms = [keep, ys[k]]
+            k += 1
+        rows = size
     near = in_vmem(*zs, *ys)
     xs = []
     for k in range(1, xbits):
-        halo = pl.pallas_call(
-            row_kernel(depth, wx, wy, zbits, ybits, k),
-            out_shape=pltpu.VMEM((6 * depth + 8, LANES), f32),
-            in_specs=[vmem] * (2 + zbits + ybits),
-            out_specs=vmem,
+        keep, away = pl.pallas_call(
+            merge_x_kernel(len(terms), rows, depth, wx, wy, zbits, ybits, k),
+            out_shape=(
+                pltpu.VMEM((rows // 2, LANES), f32),
+                pltpu.VMEM((rows // 2 + 6 * depth + 8, LANES), f32),
+            ),
+            in_specs=[vmem] * (len(terms) + 3 + zbits + ybits),
+            out_specs=(vmem, vmem),
             compiler_params=small,
-            name="rows",
-        )(e_near, h_near, *near)
-        part, halo = swap(part, halo, "gx", k)
-        xs.append(halo)
-    part = part[0]
-
-    whole = jax.ShapeDtypeStruct((3, depth, wx, wy), f32)
+            name="merge_x",
+        )(*in_vmem(*terms), e_near, h_near, *near, coef)
+        xs.append(exchange(away, "gx", (2 << k) - 1))
+        rows //= 2
+        terms = [keep, xs[-1]]
+    part = sum(term[:rows] for term in terms)
+
     layer = pltpu.VMEM((3, wx, wy), f32)
-    e_next, h_next, pole_next, e_top, h_top, coef_top = pl.pallas_call(
-        field_kernel(depth, wx, wy, xbits, ybits, zbits),
-        out_shape=(whole, whole, whole, layer, layer, pltpu.VMEM((wx, wy), f32)),
-        in_specs=[smem] + [vmem] * (5 + xbits + ybits + zbits),
-        out_specs=(vmem,) * 6,
+    e_next, h_next, e_top, h_top, coef_top = pl.pallas_call(
+        field_kernel(freqs, depth, wx, wy, xbits, ybits, zbits),
+        out_shape=(whole, whole, layer, layer, pltpu.VMEM((wx, wy), f32)),
+        in_specs=[vmem] * (5 + xbits + ybits + zbits),
+        out_specs=(vmem,) * 5,
         compiler_params=pltpu.CompilerParams(vmem_limit_bytes=16 << 20),
         name="fields",
-    )(
-        pole_table,
-        e_near,
-        h_near,
-        *in_vmem(pole_current, material, first, xe),
-        *near,
-        *in_vmem(*xs),
-    )
+    )(e_near, h_near, base_e, coef, *in_vmem(first, theirs), *near, *in_vmem(*xs))
 
     top = gray(sz - 1)
+    blocks = [part]
     for k in reversed(range(zcut)):
-        other = exchange(part, "gz", (2 << k) - 1)
-        part = jnp.concatenate([other, part] if (top >> k) & 1 else [part, other], axis=0)
-    flipped = iy < sy // 2
-    source = jnp.where(flipped, part[:, ::-1], part)
-    start = (2 // per) * block + per * wx
-    col = part[start : start + 8]
+        others = [exchange(value, "gz", (2 << k) - 1) for value in blocks]
+        blocks = others + blocks if (top >> k) & 1 else blocks + others
     e_next, h_next = pl.pallas_call(
-        inject_kernel(depth, wx, wy, sz, per),
+        inject_kernel(depth, wx, wy, sy, sz, per, zcut),
         out_shape=(whole, whole),
-        in_specs=[vmem] * 5 + [hbm] * 2,
+        in_specs=[vmem] * (len(blocks) + 3) + [hbm] * 2,
         out_specs=(hbm, hbm),
         scratch_shapes=[
             pltpu.VMEM((3, wx, wy), f32),
             pltpu.VMEM((2, wx, wy), f32),
             pltpu.SemaphoreType.DMA((2,)),
         ],
-        input_output_aliases={5: 0, 6: 1},
+        input_output_aliases={len(blocks) + 3: 0, len(blocks) + 4: 1},
         compiler_params=small,
         name="inject",
-    )(*in_vmem(source, col, e_top, h_top, coef_top), e_next, h_next)
+    )(*in_vmem(*blocks, e_top, h_top, coef_top), e_next, h_next)
     return (e_next, h_next, pole_next)
 
 

time: 43 us -> 35.1 us (0.82)
  starting transfers between devices: 17.8 us -> 11.9 us
  local copies, waits for them, and re-layouts: 2.77 us -> 0.01 us
  Pallas kernels: 11.8 us -> 13.8 us
  waiting for transfers between devices: 9.3 us -> 8.57 us
    ppermute x9 -> x8, starting transfers between devices: 17.8 us -> 11.9 us  [exchange(): lax.ppermute(array, axis, [(i, i ^ mask) for i in range(lax.axis_size(axi...]
    pallas_call x4 -> x7, Pallas kernels: 2.96 us -> 5.44 us  [the longest x1 1.72 us: local(): pl.pallas_call(pole_kernel(depth, wx, wy), out_shape=(whole, pltpu.VMEM(w...]
    squeeze x1 -> x0, local copies, waits for them, and re-layouts: 0.88 us -> none  [local(): lax.dynamic_index_in_dim(v, at, 1, keepdims=False)]
    dynamic_slice x2 -> x1, local copies, waits for them, and re-layouts: 0.88 us -> 0.01 us  [local(): row = lax.dynamic_slice_in_dim(side, at, 1, axis=1)]
    ppermute x9 -> x8, waiting for transfers between devices: 9.3 us -> 8.57 us  [exchange(): lax.ppermute(array, axis, [(i, i ^ mask) for i in range(lax.axis_size(axi...]
    unnamed x18 -> x0, local copies, waits for them, and re-layouts: 0.7 us -> none
    pallas_call x1, Pallas kernels: 8.88 us -> 8.34 us  [local(): pl.pallas_call(source_kernel(freqs, wx, half, sizes, zslots, xslots, scal...]
  transfers between devices with their start and end apart: 9 -> 8, of which waited for: 6 -> 4; matrix products, arithmetic and copies ran while one was open for 2% -> 0% of each run, Pallas kernels for 26% -> 9%
where the time goes in v3:
time: 35.1 us; the launch traced here: 34.9 us
  Pallas kernels  13.8 us (39%)
  starting transfers between devices  11.9 us (34%)
  waiting for transfers between devices  8.57 us (24%)
  between operations  0.68 us (2%)
    ppermute x8, starting transfers between devices, exchange(): lax.ppermute(array, axis, [(i, i ^ mask) for i in range(lax.axis_size(axi...  11.9 us
    ppermute x8, waiting for transfers between devices, exchange(): lax.ppermute(array, axis, [(i, i ^ mask) for i in range(lax.axis_size(axi...  8.57 us
    pallas_call x1, Pallas kernels, local(): pl.pallas_call(source_kernel(freqs, wx, half, sizes, zslots, xslots, scal...  8.34 us
    pallas_call x1, Pallas kernels, local(): pl.pallas_call(pole_kernel(depth, wx, wy), out_shape=(whole, pltpu.VMEM(w...  1.72 us
    pallas_call x1, Pallas kernels, local(): pl.pallas_call(field_kernel(freqs, depth, wx, wy, xbits, ybits, zbits), o...  1.25 us
    pallas_call x1, Pallas kernels, local(): pl.pallas_call(pack_kernel(freqs, depth, wx, zbits), out_shape=[pltpu.VME...  1.14 us
    pallas_call x1, Pallas kernels, local(): pl.pallas_call(inject_kernel(depth, wx, wy, sy, sz, per, zcut), out_shape...  0.99 us
  transfers between devices with their start and end apart: 8, of which 4 were waited for; matrix products, arithmetic and copies ran while one was open for 0% of the time, Pallas kernels for 9%

profile of v3, /device:TPU:1, one launch (start us, length us, event | category | flops | bytes accessed | tf_op | source)
XLA Modules:
  0.0 34.9 jit_solution(12346260277244508910)
XLA Ops:
  0.6 1.1 %pack.1 = (f32[20,8,128]{2,1,0:T(8,128)S(1)}, f32[2,16,128]{2,1,0:T(8,128)S(1)}, f32[3,4,32,128]{3,2,1,0:T(8,128)S(1)}, f32[3,4,32,128]{3,2,1,0:T(8,128)S(1)}, f32[6,32,128]{2,1,0:T(8,128)S(1)}) custom-call(f32[3,4,32,128]{3,2,1,0:T(8,128)} %refs_0_.1, f32[3,4,32,128]{3,2,1,0:T(8,128)} %refs_1_.1, f32[16,8,128]{2,1,0:T(8,128)} %refs_2_.1, f32[2,128]{1,0:T(2,128)} %refs_3_.1, ...), custom_call_target="tpu_custom_call" | custom-call | tf_op jit(solution)/shard_map/pack/pallas_call | solution.py:629
  1.8 2.2 %collective-permute-start = (f32[20,8,128]{2,1,0:T(8,128)S(1)}, f32[20,8,128]{2,1,0:T(8,128)S(1)}, u32[]{:S(2)}, u32[]{:S(2)}) collective-permute-start(f32[20,8,128]{2,1,0:T(8,128)S(1)} %get-tuple-element.29.refs_1_), channel_id=1, source_target_pairs={{0,8},{8,0},{16,24},{24,16},{1,9},{9,1},{17,25},{25,17},{2,10},{10... | collective-permute-start | bytes 245768 | tf_op jit(solution)/shard_map/ppermute | solution.py:18
  4.0 2.1 %collective-permute-done.refs_2_.refs_5_ = f32[20,8,128]{2,1,0:T(8,128)S(1)} collective-permute-done((f32[20,8,128]{2,1,0:T(8,128)S(1)}, f32[20,8,128]{2,1,0:T(8,128)S(1)}, u32[]{:S(2)}, u32[]{:S(2)}) %collective-permute-start) | collective-permute-done | bytes 81952 | tf_op jit(solution)/shard_map/ppermute | solution.py:18
  6.1 8.3 %source.1 = (f32[1,4,2,72,128]{4,3,2,1,0:T(8,128)S(1)}, f32[1,4,2,72,128]{4,3,2,1,0:T(8,128)S(1)}) custom-call(f32[2,16,128]{2,1,0:T(8,128)S(1)} %get-tuple-element.28.refs_0_, f32[20,8,128]{2,1,0:T(8,128)S(1)} %get-tuple-element.29.refs_1_, f32[20,8,128]{2,1,0:T(8,128)S(1)} %collective-permute-done.refs_2_.refs_5_), custom_call_target="tpu_custom_call" | custom-call | tf_op jit(solution)/shard_map/source/pallas_call | solution.py:664
  14.4 1.3 %collective-permute-start.1 = (f32[1,4,2,72,128]{4,3,2,1,0:T(8,128)S(1)}, f32[1,4,2,72,128]{4,3,2,1,0:T(8,128)S(1)}, u32[]{:S(2)}, u32[]{:S(2)}) collective-permute-start(f32[1,4,2,72,128]{4,3,2,1,0:T(8,128)S(1)} %get-tuple-element.31), channel_id=1, source_target_pairs={{0,1},{1,0},{2,3},{3,2},{4,5},{5,4},{6,7},{7,6},{8,9},{9,8},{10,11... | collective-permute-start | bytes 884744 | tf_op jit(solution)/shard_map/ppermute | solution.py:18
  15.8 0.1 collective-permute-start.2
  15.9 1.3 %collective-permute-done.2.refs_3_.refs_6_ = f32[6,33,128]{2,1,0:T(8,128)S(1)} collective-permute-done((f32[6,33,128]{2,1,0:T(8,128)S(1)}, f32[6,33,128]{2,1,0:T(8,128)S(1)}, u32[]{:S(2)}, u32[]{:S(2)}) %collective-permute-start.2) | collective-permute-done | bytes 101408 | tf_op jit(solution)/shard_map/ppermute | solution.py:18
  17.2 0.2 columns.1
  17.4 0.0 collective-permute-done.1
  17.5 0.1 merge_y.1
  17.5 1.7 %collective-permute-start.3 = (f32[152,128]{1,0:T(8,128)S(1)}, f32[152,128]{1,0:T(8,128)S(1)}, u32[]{:S(2)}, u32[]{:S(2)}) collective-permute-start(f32[152,128]{1,0:T(8,128)S(1)} %get-tuple-element.38), channel_id=1, source_target_pairs={{0,2},{2,0},{4,6},{6,4},{1,3},{3,1},{5,7},{7,5},{8,10},{10,8},{12,... | collective-permute-start | bytes 233480 | tf_op jit(solution)/shard_map/ppermute | solution.py:18
  19.2 1.2 %collective-permute-start.4 = (f32[152,128]{1,0:T(8,128)S(1)}, f32[152,128]{1,0:T(8,128)S(1)}, u32[]{:S(2)}, u32[]{:S(2)}) collective-permute-start(f32[152,128]{1,0:T(8,128)S(1)} %get-tuple-element.39), channel_id=1, source_target_pairs={{0,6},{2,4},{4,2},{6,0},{1,7},{3,5},{5,3},{7,1},{8,14},{10,12},{12... | collective-permute-start | bytes 233480 | tf_op jit(solution)/shard_map/ppermute | solution.py:18
  20.4 0.0 collective-permute-start.5
  20.5 1.7 %pole.1 = (f32[3,4,32,128]{3,2,1,0:T(8,128)}, f32[3,4,32,128]{3,2,1,0:T(8,128)S(1)}, f32[4,32,128]{2,1,0:T(8,128)S(1)}) custom-call(f32[3,4]{1,0:T(4,128)} %table_in.1, f32[3,4,32,128]{3,2,1,0:T(8,128)S(1)} %get-tuple-element.32.refs_0_.e.refs_4_, f32[3,4,32,128]{3,2,1,0:T(8,128)} %pole_in.1, s32[4,32,128]{2,1,0:T(8,128)} %material_in.1, ...), custom_call_target="tpu_custom_call" | custom-call | tf_op jit(solution)/shard_map/pole/pallas_call | solution.py:691
  22.2 3.6 %collective-permute-done.5.refs_3_ = f32[144,128]{1,0:T(8,128)S(1)} collective-permute-done((f32[144,128]{1,0:T(8,128)S(1)}, f32[144,128]{1,0:T(8,128)S(1)}, u32[]{:S(2)}, u32[]{:S(2)}) %collective-permute-start.5) | collective-permute-done | bytes 73760 | tf_op jit(solution)/shard_map/ppermute | solution.py:18
  25.8 0.0 collective-permute-done.3.refs_1_.refs_7_
  25.8 0.0 collective-permute-done.4.refs_2_.refs_8_
  25.8 3.4 %collective-permute-start.6 = (f32[104,128]{1,0:T(8,128)S(1)}, f32[104,128]{1,0:T(8,128)S(1)}, u32[]{:S(2)}, u32[]{:S(2)}) collective-permute-start(f32[104,128]{1,0:T(8,128)S(1)} %get-tuple-element.43), channel_id=1, source_target_pairs={{0,24},{8,16},{16,8},{24,0},{1,25},{9,17},{17,9},{25,1},{2,26},{10... | collective-permute-start | bytes 159752 | tf_op jit(solution)/shard_map/ppermute | solution.py:18
  29.2 1.5 %collective-permute-done.6.refs_9_ = f32[104,128]{1,0:T(8,128)S(1)} collective-permute-done((f32[104,128]{1,0:T(8,128)S(1)}, f32[104,128]{1,0:T(8,128)S(1)}, u32[]{:S(2)}, u32[]{:S(2)}) %collective-permute-start.6) | collective-permute-done | bytes 53280 | tf_op jit(solution)/shard_map/ppermute | solution.py:18
  30.8 1.9 %collective-permute-start.7 = (f32[72,128]{1,0:T(8,128)S(1)}, f32[72,128]{1,0:T(8,128)S(1)}, u32[]{:S(2)}, u32[]{:S(2)}) collective-permute-start(f32[72,128]{1,0:T(8,128)S(1)} %slice_add_fusion.refs_1_), channel_id=1, source_target_pairs={{0,1},{1,0},{2,3},{3,2},{4,5},{5,4},{6,7},{7,6},{8,9},{9,8},{10,11... | collective-permute-start | bytes 110600 | tf_op jit(solution)/shard_map/ppermute | solution.py:18
  32.7 1.2 %fields.1 = (f32[3,4,32,128]{3,2,1,0:T(8,128)}, f32[3,4,32,128]{3,2,1,0:T(8,128)}, f32[3,32,128]{2,1,0:T(8,128)S(1)}, f32[3,32,128]{2,1,0:T(8,128)S(1)}, f32[32,128]{1,0:T(8,128)S(1)}) custom-call(f32[3,4,32,128]{3,2,1,0:T(8,128)S(1)} %get-tuple-element.32.refs_0_.e.refs_4_, f32[3,4,32,128]{3,2,1,0:T(8,128)S(1)} %get-tuple-element.33.refs_1_.refs_5_, ...), custom_call_target="tpu_custom_call" | custom-call | tf_op jit(solution)/shard_map/fields/pallas_call | solution.py:769
  33.9 0.0 collective-permute-done.7.refs_0_
  33.9 1.0 %inject.1 = (f32[3,4,32,128]{3,2,1,0:T(8,128)}, f32[3,4,32,128]{3,2,1,0:T(8,128)}) custom-call(f32[72,128]{1,0:T(8,128)S(1)} %collective-permute-done.7.refs_0_, f32[72,128]{1,0:T(8,128)S(1)} %slice_add_fusion.refs_1_, f32[3,32,128]{2,1,0:T(8,128)S(1)} %get-tuple-element.45.refs_2_, ...), custom_call_target="tpu_custom_call", output_to_operand_aliasing={{0}: (5, {}), {1}: (6, {})} | custom-call | tf_op jit(solution)/shard_map/inject/pallas_call | solution.py:783
  (5 shorter events, 0.1 us)
Async XLA Ops:
  1.8 4.3 %collective-permute-start = (f32[20,8,128]{2,1,0:T(8,128)S(1)}, f32[20,8,128]{2,1,0:T(8,128)S(1)}, u32[]{:S(2)}, u32[]{:S(2)}) collective-permute-start(f32[20,8,128]{2,1,0:T(8,128)S(1)} %get-tuple-element.29.refs_1_), channel_id=1, source_target_pairs={{0,8},{8,0},{16,24},{24,16},{1,9},{9,1},{17,25},{25,17},{2,10},{10... | collective-permute-start | bytes 245768 | tf_op jit(solution)/shard_map/ppermute | solution.py:18
  14.4 3.0 %collective-permute-start.1 = (f32[1,4,2,72,128]{4,3,2,1,0:T(8,128)S(1)}, f32[1,4,2,72,128]{4,3,2,1,0:T(8,128)S(1)}, u32[]{:S(2)}, u32[]{:S(2)}) collective-permute-start(f32[1,4,2,72,128]{4,3,2,1,0:T(8,128)S(1)} %get-tuple-element.31), channel_id=1, source_target_pairs={{0,1},{1,0},{2,3},{3,2},{4,5},{5,4},{6,7},{7,6},{8,9},{9,8},{10,11... | collective-permute-start | bytes 884744 | tf_op jit(solution)/shard_map/ppermute | solution.py:18
  15.8 1.4 %collective-permute-start.2 = (f32[6,33,128]{2,1,0:T(8,128)S(1)}, f32[6,33,128]{2,1,0:T(8,128)S(1)}, u32[]{:S(2)}, u32[]{:S(2)}) collective-permute-start(f32[6,33,128]{2,1,0:T(8,128)S(1)} %pad_maximum_fusion), channel_id=1, source_target_pairs={{0,1},{1,0},{2,3},{3,2},{4,5},{5,4},{6,7},{7,6},{8,9},{9,8},{10,11... | collective-permute-start | bytes 304136 | tf_op jit(solution)/shard_map/ppermute | solution.py:18
  17.5 8.3 %collective-permute-start.3 = (f32[152,128]{1,0:T(8,128)S(1)}, f32[152,128]{1,0:T(8,128)S(1)}, u32[]{:S(2)}, u32[]{:S(2)}) collective-permute-start(f32[152,128]{1,0:T(8,128)S(1)} %get-tuple-element.38), channel_id=1, source_target_pairs={{0,2},{2,0},{4,6},{6,4},{1,3},{3,1},{5,7},{7,5},{8,10},{10,8},{12,... | collective-permute-start | bytes 233480 | tf_op jit(solution)/shard_map/ppermute | solution.py:18
  19.2 6.6 %collective-permute-start.4 = (f32[152,128]{1,0:T(8,128)S(1)}, f32[152,128]{1,0:T(8,128)S(1)}, u32[]{:S(2)}, u32[]{:S(2)}) collective-permute-start(f32[152,128]{1,0:T(8,128)S(1)} %get-tuple-element.39), channel_id=1, source_target_pairs={{0,6},{2,4},{4,2},{6,0},{1,7},{3,5},{5,3},{7,1},{8,14},{10,12},{12... | collective-permute-start | bytes 233480 | tf_op jit(solution)/shard_map/ppermute | solution.py:18
  20.4 5.3 %collective-permute-start.5 = (f32[144,128]{1,0:T(8,128)S(1)}, f32[144,128]{1,0:T(8,128)S(1)}, u32[]{:S(2)}, u32[]{:S(2)}) collective-permute-start(f32[144,128]{1,0:T(8,128)S(1)} %get-tuple-element.40), channel_id=1, source_target_pairs={{0,4},{2,6},{4,0},{6,2},{1,5},{3,7},{5,1},{7,3},{8,12},{10,14},{12... | collective-permute-start | bytes 221192 | tf_op jit(solution)/shard_map/ppermute | solution.py:18
  25.8 4.9 %collective-permute-start.6 = (f32[104,128]{1,0:T(8,128)S(1)}, f32[104,128]{1,0:T(8,128)S(1)}, u32[]{:S(2)}, u32[]{:S(2)}) collective-permute-start(f32[104,128]{1,0:T(8,128)S(1)} %get-tuple-element.43), channel_id=1, source_target_pairs={{0,24},{8,16},{16,8},{24,0},{1,25},{9,17},{17,9},{25,1},{2,26},{10... | collective-permute-start | bytes 159752 | tf_op jit(solution)/shard_map/ppermute | solution.py:18
  30.8 3.2 %collective-permute-start.7 = (f32[72,128]{1,0:T(8,128)S(1)}, f32[72,128]{1,0:T(8,128)S(1)}, u32[]{:S(2)}, u32[]{:S(2)}) collective-permute-start(f32[72,128]{1,0:T(8,128)S(1)} %slice_add_fusion.refs_1_), channel_id=1, source_target_pairs={{0,1},{1,0},{2,3},{3,2},{4,5},{5,4},{6,7},{7,6},{8,9},{9,8},{10,11... | collective-permute-start | bytes 110600 | tf_op jit(solution)/shard_map/ppermute | solution.py:18

commit v4 on v3

--- a/solution.py
+++ b/solution.py
@@ -72,7 +72,7 @@
     return lax.dot_general(a, b, (((1,), (1,)), ((), ())), preferred_element_type=jnp.float32)
 
 
-def source_kernel(freqs, wx, half, sizes, zslots, xslots, scale, chunks):
+def source_kernel(freqs, depth, wx, half, sizes, zslots, xslots, scale, zbits, closing):
     sx, sy, sz = sizes
     xbits = max(3, (wx - 1).bit_length())
     ybits = max(3, (half - 1).bit_length())
@@ -80,10 +80,12 @@
     main = 4 * xslots * wx
 
     def body(*refs):
-        waves = refs[0]
-        cots = refs[1 : 1 + chunks]
-        keep, send = refs[1 + chunks : 3 + chunks]
-        xbase, xpow, ypow, acc_even, acc_odd = refs[3 + chunks :]
+        waves, packed = refs[:2]
+        if closing:
+            old_even, old_odd = refs[2:4]
+            keep, send, xbase, xpow, ypow, acc_even, acc_odd = refs[4 + zbits :]
+        else:
+            acc_even, acc_odd, xbase, xpow, ypow = refs[2:]
         ix, iy, iz = (lax.axis_index(name) for name in ("gx", "gy", "gz"))
         xbit, ybit, zbit = bits_of(sx), bits_of(sy), bits_of(zslots)
         starts = []
@@ -98,30 +100,35 @@
         ycode = gray(iy)
         center = (2 * half - 1) / 2.0
         wave, phase = waves[0], waves[1]
-        for n in range(chunks):
-            along_x = wave * cots[n][freqs, 0:1, :]
-            along_y = wave * cots[n][freqs, 1:2, :]
-            origin = along_y * center - phase
-            for xr in range(xslots):
-                angle = along_x * starts[xr] + origin
-                xbase[n, xr, 0] = jnp.cos(angle)
-                xbase[n, xr, 1] = jnp.sin(angle)
-            turn = doubled(small_turn(0.5 * along_x))
-            for k in range(xbits):
-                xpow[n, k, 0], xpow[n, k, 1] = turn
-                turn = doubled(turn)
-            turn = small_turn(0.5 * along_y)
-            for k in range(ybits + 1):
-                ypow[n, k, 0], ypow[n, k, 1] = turn
-                turn = doubled(turn)
-        acc_even[...] = jnp.zeros_like(acc_even)
-        acc_odd[...] = jnp.zeros_like(acc_odd)
-
-        def one(f, carry):
+        along_x = wave * packed[freqs, 0:1, :]
+        along_y = wave * packed[freqs, 1:2, :]
+        origin = along_y * center - phase
+        for xr in range(xslots):
+            angle = along_x * starts[xr] + origin
+            xbase[xr, 0] = jnp.cos(angle)
+            xbase[xr, 1] = jnp.sin(angle)
+        turn = doubled(small_turn(0.5 * along_x))
+        for k in range(xbits):
+            xpow[k, 0], xpow[k, 1] = turn
+            turn = doubled(turn)
+        turn = small_turn(0.5 * along_y)
+        for k in range(ybits + 1):
+            ypow[k, 0], ypow[k, 1] = turn
+            turn = doubled(turn)
+        if closing:
+            acc_even[...] = old_even[...]
+            acc_odd[...] = old_odd[...]
+        else:
+            acc_even[...] = jnp.zeros_like(acc_even)
+            acc_odd[...] = jnp.zeros_like(acc_odd)
+
+        def pair(step, carry):
             firsts, seconds, coses, sines = [], [], [], []
-            for n in range(chunks):
+            for n in range(2):
+                f = 2 * step + n
+
                 def row(ref, *where):
-                    return tuple(ref[(n, *where, i, pl.ds(f, 1), slice(None))] for i in (0, 1))
+                    return tuple(ref[(*where, i, pl.ds(f, 1), slice(None))] for i in (0, 1))
 
                 powers = [row(ypow, k) for k in range(ybits + 1)]
                 cy, sy_ = rotations(powers[0], powers[1:], half)
@@ -136,13 +143,13 @@
                         cx, sx_ = turns[xr]
                         for c2 in range(per):
                             at = 2 * ((zcode ^ zr) * per + c2)
-                            p = cots[n][f, pl.ds(at, 1), :]
-                            q = cots[n][f, pl.ds(at + 1, 1), :]
+                            p = packed[f, pl.ds(at, 1), :]
+                            q = packed[f, pl.ds(at + 1, 1), :]
                             first.append(p * cx - q * sx_)
                             second.append(p * sx_ + q * cx)
                 back = (powers[0][0], -powers[0][1])
-                p = cots[n][f, 6:7, :]
-                q = cots[n][f, 7:8, :]
+                p = packed[f, 6:7, :]
+                q = packed[f, 7:8, :]
                 line = lax.broadcasted_iota(jnp.int32, (8, p.shape[-1]), 0)
                 one_first = jnp.zeros(line.shape, jnp.float32)
                 one_second = one_first
@@ -162,7 +169,9 @@
             acc_odd[...] += product(seconds, sines)
             return carry
 
-        lax.fori_loop(0, freqs, one, 0)
+        lax.fori_loop(0, freqs // 2, pair, 0)
+        if not closing:
+            return
 
         def slot(tile):
             code = gray(tile) ^ ycode
@@ -180,6 +189,12 @@
             for y in range(sy):
                 for xr in range(xslots):
                     ref[z, y, xr, extra : extra + 8] = jnp.zeros((8, LANES), jnp.float32)
+        at_z = (1 - (iz & 1)) * (depth - 1)
+        for i in range(6):
+            row = i * depth
+            send[0, 0, 0, extra + 2 + i : extra + 3 + i] = packed[
+                freqs + 1 + row // 8, pl.ds(row % 8 + at_z, 1), :
+            ]
         turned = 2 // per
         spare = 2 % per
         for j in range(sy // 2):
@@ -413,13 +428,14 @@
     return body
 
 
-def field_kernel(freqs, depth, wx, wy, xbits, ybits, zbits):
+def field_kernel(freqs, depth, wx, wy, xbits, ybits, zbits, side_row):
     def body(*refs):
         e, h, base_e, coef_ref, first, message = refs[:6]
         zs = refs[6 : 6 + zbits]
         ys = refs[6 + zbits : 6 + zbits + ybits]
         xs = [x[x.shape[0] - 6 * depth - 8 :] for x in refs[6 + zbits + ybits : 5 + zbits + ybits + xbits]]
-        e_out, h_out, e_top, h_top, coef_top = refs[5 + zbits + ybits + xbits :]
+        sides = refs[5 + zbits + ybits + xbits : 5 + 2 * zbits + ybits + xbits]
+        e_out, h_out, e_top, h_top, coef_top = refs[5 + 2 * zbits + ybits + xbits :]
         ix, iy, iz = (lax.axis_index(name) for name in ("gx", "gy", "gz"))
         xlow, xhigh = near_flags(ix, xbits)
         ylow, yhigh = near_flags(iy, ybits)
@@ -475,7 +491,8 @@
             return weighted(flags, [z[i, 0:wx] for z in zs])
 
         def side_of(flags, i):
-            return weighted(flags, [z[i, wx : wx + 1] for z in zs])
+            at = side_row + i
+            return weighted(flags, [side[at : at + 1] for side in sides])
 
         up_x, up_y = layer_of(zhigh, 0), layer_of(zhigh, 1)
         hx = oldx - courant * ((next_y(ez, above[:, 2:3]) - ez) - (next_z(ey, up_y) - ey))
@@ -576,19 +593,17 @@
             coef = coef_top[...]
             h_new[0] = h_top[0] - courant * magnetic_x
             h_new[1] = h_top[1] - courant * magnetic_y
+            h_copy = pltpu.make_async_copy(h_new, h_out.at[0:2, depth - 1], sems.at[1])
+            h_copy.start()
             e_new[0] = e_top[0] + coef * (courant * magnetic_y - electric_x)
             e_new[1] = e_top[1] - coef * (courant * magnetic_x + electric_y)
             e_new[2] = e_top[2] + coef * courant * (
                 (magnetic_x - last_y) - (magnetic_y - last_x)
             )
-            copies = [
-                pltpu.make_async_copy(e_new, e_out.at[:, depth - 1], sems.at[0]),
-                pltpu.make_async_copy(h_new, h_out.at[0:2, depth - 1], sems.at[1]),
-            ]
-            for copy in copies:
-                copy.start()
-            for copy in copies:
-                copy.wait()
+            e_copy = pltpu.make_async_copy(e_new, e_out.at[:, depth - 1], sems.at[0])
+            e_copy.start()
+            h_copy.wait()
+            e_copy.wait()
 
     return body
 
@@ -648,12 +663,8 @@
     )(*in_hbm(e_field, h_field, cotangent, cosines, wavenumber, time_phase))
     e_near, h_near = in_vmem(e_near, h_near)
     theirs = exchange(mine, "gx", 1)
-    side = theirs[freqs + 1 :].reshape(6, depth, LANES)
-    zs = []
-    for k in range(zbits):
-        at = (1 - ((iz >> k) & 1)) * (depth - 1)
-        row = lax.dynamic_slice_in_dim(side, at, 1, axis=1)
-        zs.append(exchange(jnp.concatenate([layers[k], row], axis=1), "gz", (2 << k) - 1))
+    zs = [exchange(layers[k], "gz", (2 << k) - 1) for k in range(zbits)]
+    zs = in_vmem(*zs)
 
     half = sy * wy // 2
     xlevels = max(3, (wx - 1).bit_length())
@@ -661,21 +672,34 @@
     width = count + pad
     block = per * wx + 8
     part_shape = pltpu.VMEM((zslots // 2, sy, xslots, block, wy), f32)
-    keep, send = pl.pallas_call(
-        source_kernel(freqs, wx, half, sizes, zslots, xslots, scale, 2),
-        out_shape=(part_shape, part_shape),
-        in_specs=[vmem] * 3,
+    assert freqs % 2 == 0
+    sums = pltpu.VMEM((4 * xslots * wx + 8, half), f32)
+    tables = [
+        pltpu.VMEM((xslots, 2, freqs, width), f32),
+        pltpu.VMEM((xlevels, 2, freqs, width), f32),
+        pltpu.VMEM((ylevels, 2, freqs, width), f32),
+    ]
+    medium = pltpu.CompilerParams(vmem_limit_bytes=24 << 20)
+    waves, mine = in_vmem(waves, mine)
+    own = pl.pallas_call(
+        source_kernel(freqs, depth, wx, half, sizes, zslots, xslots, scale, zbits, False),
+        out_shape=(sums, sums),
+        in_specs=[vmem] * 2,
         out_specs=(vmem, vmem),
-        scratch_shapes=[
-            pltpu.VMEM((2, xslots, 2, freqs, width), f32),
-            pltpu.VMEM((2, xlevels, 2, freqs, width), f32),
-            pltpu.VMEM((2, ylevels, 2, freqs, width), f32),
-            pltpu.VMEM((4 * xslots * wx + 8, half), f32),
-            pltpu.VMEM((4 * xslots * wx + 8, half), f32),
-        ],
-        compiler_params=pltpu.CompilerParams(vmem_limit_bytes=24 << 20),
-        name="source",
-    )(*in_vmem(waves, mine, theirs))
+        scratch_shapes=tables,
+        compiler_params=medium,
+        name="source_own",
+    )(waves, mine)
+    with jax.named_scope("source_all"):
+        keep, send = pl.pallas_call(
+            source_kernel(freqs, depth, wx, half, sizes, zslots, xslots, scale, zbits, True),
+            out_shape=(part_shape, part_shape),
+            in_specs=[vmem] * (4 + zbits),
+            out_specs=(vmem, vmem),
+            scratch_shapes=tables + [sums, sums],
+            compiler_params=medium,
+            name="source_both",
+        )(waves, *in_vmem(theirs, *own), *zs)
 
     strip = pltpu.VMEM((8, LANES), f32)
     first, last = pl.pallas_call(
@@ -685,7 +709,7 @@
         out_specs=(vmem, vmem),
         compiler_params=small,
         name="columns",
-    )(e_near, h_near, *in_vmem(theirs, *zs))
+    )(e_near, h_near, *in_vmem(theirs), *zs)
 
     whole = jax.ShapeDtypeStruct((3, depth, wx, wy), f32)
     pole_next, base_e, coef = pl.pallas_call(
@@ -709,6 +733,12 @@
         return value.reshape(-1, LANES)
 
     terms = [keep, exchange(send, "gz", 1)]
+    sides = [flat(terms[1])]
+    for k in range(1, zbits):
+        at = (1 - ((iz >> k) & 1)) * (depth - 1)
+        rows = theirs[freqs + 1 :].reshape(6, depth, LANES)
+        rows = lax.dynamic_index_in_dim(rows, at, 1, keepdims=False)
+        sides.append(exchange(jnp.pad(rows, ((per * wx + 2, 0), (0, 0))), "gz", (2 << k) - 1))
     for k in range(1, zbits):
         part = terms[0] + terms[1]
         mask = (2 << k) - 1
@@ -746,7 +776,7 @@
             terms = [keep, ys[k]]
             k += 1
         rows = size
-    near = in_vmem(*zs, *ys)
+    near = [*zs, *in_vmem(*ys)]
     xs = []
     for k in range(1, xbits):
         keep, away = pl.pallas_call(
@@ -767,13 +797,13 @@
 
     layer = pltpu.VMEM((3, wx, wy), f32)
     e_next, h_next, e_top, h_top, coef_top = pl.pallas_call(
-        field_kernel(freqs, depth, wx, wy, xbits, ybits, zbits),
+        field_kernel(freqs, depth, wx, wy, xbits, ybits, zbits, per * wx + 2),
         out_shape=(whole, whole, layer, layer, pltpu.VMEM((wx, wy), f32)),
-        in_specs=[vmem] * (5 + xbits + ybits + zbits),
+        in_specs=[vmem] * (5 + xbits + ybits + 2 * zbits),
         out_specs=(vmem,) * 5,
         compiler_params=pltpu.CompilerParams(vmem_limit_bytes=16 << 20),
         name="fields",
-    )(e_near, h_near, base_e, coef, *in_vmem(first, theirs), *near, *in_vmem(*xs))
+    )(e_near, h_near, base_e, coef, *in_vmem(first, theirs), *near, *in_vmem(*xs, *sides))
 
     top = gray(sz - 1)
     blocks = [part]

time: 35.1 us -> 31.8 us (0.906)
  waiting for transfers between devices: 8.57 us -> 6.83 us
  starting transfers between devices: 11.9 us -> 10.4 us
    ppermute x8, waiting for transfers between devices: 8.57 us -> 6.83 us  [exchange(): lax.ppermute(array, axis, [(i, i ^ mask) for i in range(lax.axis_size(axi...]
    ppermute x8, starting transfers between devices: 11.9 us -> 10.4 us  [exchange(): lax.ppermute(array, axis, [(i, i ^ mask) for i in range(lax.axis_size(axi...]
    pallas_call x2 -> x3, Pallas kernels: 9.59 us -> 9.57 us  [the longest x2 8.32 us: local(): pl.pallas_call(source_kernel(freqs, depth, wx, half, sizes, zslots, xslot...]
  transfers between devices with their start and end apart: 8 -> 8, of which waited for: 4 -> 3; matrix products, arithmetic and copies ran while one was open for 0% -> 0% of each run, Pallas kernels for 9% -> 23%
where the time goes in v4:
time: 31.8 us; the launch traced here: 31.6 us
  Pallas kernels  13.7 us (43%)
  starting transfers between devices  10.4 us (33%)
  waiting for transfers between devices  6.83 us (21%)
  between operations  0.69 us (2%)
    ppermute x8, starting transfers between devices, exchange(): lax.ppermute(array, axis, [(i, i ^ mask) for i in range(lax.axis_size(axi...  10.4 us
    pallas_call x2, Pallas kernels, local(): pl.pallas_call(source_kernel(freqs, depth, wx, half, sizes, zslots, xslot...  8.32 us
    ppermute x8, waiting for transfers between devices, exchange(): lax.ppermute(array, axis, [(i, i ^ mask) for i in range(lax.axis_size(axi...  6.83 us
    pallas_call x1, Pallas kernels, local(): pl.pallas_call(pole_kernel(depth, wx, wy), out_shape=(whole, pltpu.VMEM(w...  1.72 us
    pallas_call x1, Pallas kernels, local(): pl.pallas_call(field_kernel(freqs, depth, wx, wy, xbits, ybits, zbits, pe...  1.24 us
    pallas_call x1, Pallas kernels, local(): pl.pallas_call(pack_kernel(freqs, depth, wx, zbits), out_shape=[pltpu.VME...  1.14 us
    pallas_call x1, Pallas kernels, local(): pl.pallas_call(inject_kernel(depth, wx, wy, sy, sz, per, zcut), out_shape...  0.98 us
  transfers between devices with their start and end apart: 8, of which 3 were waited for; matrix products, arithmetic and copies ran while one was open for 0% of the time, Pallas kernels for 23%

profile of v4, /device:TPU:1, one launch (start us, length us, event | category | flops | bytes accessed | tf_op | source)
XLA Modules:
  0.0 31.6 jit_solution(17141662704500926115)
XLA Ops:
  0.6 1.1 %pack.1 = (f32[20,8,128]{2,1,0:T(8,128)S(1)}, f32[2,16,128]{2,1,0:T(8,128)S(1)}, f32[3,4,32,128]{3,2,1,0:T(8,128)S(1)}, f32[3,4,32,128]{3,2,1,0:T(8,128)S(1)}, f32[6,32,128]{2,1,0:T(8,128)S(1)}) custom-call(f32[3,4,32,128]{3,2,1,0:T(8,128)} %refs_0_.1, f32[3,4,32,128]{3,2,1,0:T(8,128)} %refs_1_.1, f32[16,8,128]{2,1,0:T(8,128)} %refs_2_.1, f32[2,128]{1,0:T(2,128)} %refs_3_.1, ...), custom_call_target="tpu_custom_call" | custom-call | tf_op jit(solution)/shard_map/pack/pallas_call | solution.py:644
  1.8 0.1 collective-permute-start.1
  1.9 2.8 %collective-permute-start = (f32[20,8,128]{2,1,0:T(8,128)S(1)}, f32[20,8,128]{2,1,0:T(8,128)S(1)}, u32[]{:S(2)}, u32[]{:S(2)}) collective-permute-start(f32[20,8,128]{2,1,0:T(8,128)S(1)} %get-tuple-element.31.refs_1_), channel_id=1, source_target_pairs={{0,8},{8,0},{16,24},{24,16},{1,9},{9,1},{17,25},{25,17},{2,10},{10... | collective-permute-start | bytes 245768 | tf_op jit(solution)/shard_map/ppermute | solution.py:18
  4.6 4.1 %source_own.1 = (f32[264,256]{1,0:T(8,128)S(1)}, f32[264,256]{1,0:T(8,128)S(1)}) custom-call(f32[2,16,128]{2,1,0:T(8,128)S(1)} %get-tuple-element.30.refs_0_, f32[20,8,128]{2,1,0:T(8,128)S(1)} %get-tuple-element.31.refs_1_), custom_call_target="tpu_custom_call" | custom-call | tf_op jit(solution)/shard_map/source_own/pallas_call | solution.py:684
  8.7 0.0 collective-permute-done.refs_1_.refs_2_.refs_5_
  8.7 0.0 collective-permute-done.1.refs_4_.refs_3_.refs_6_
  8.8 4.2 %source_both.1 = (f32[1,4,2,72,128]{4,3,2,1,0:T(8,128)S(1)}, f32[1,4,2,72,128]{4,3,2,1,0:T(8,128)S(1)}) custom-call(f32[2,16,128]{2,1,0:T(8,128)S(1)} %get-tuple-element.30.refs_0_, f32[20,8,128]{2,1,0:T(8,128)S(1)} %collective-permute-done.refs_1_.refs_2_.refs_5_, f32[264,256]{1,0:T(8,128)S(1)} %get-tuple-element.32.refs_2_, ...), custom_call_target="tpu_custom_call" | custom-call | tf_op jit(solution)/shard_map/source_all/source_both/pallas_call | solution.py:694
  13.0 0.4 %collective-permute-start.2 = (f32[1,4,2,72,128]{4,3,2,1,0:T(8,128)S(1)}, f32[1,4,2,72,128]{4,3,2,1,0:T(8,128)S(1)}, u32[]{:S(2)}, u32[]{:S(2)}) collective-permute-start(f32[1,4,2,72,128]{4,3,2,1,0:T(8,128)S(1)} %get-tuple-element.36), channel_id=1, source_target_pairs={{0,1},{1,0},{2,3},{3,2},{4,5},{5,4},{6,7},{7,6},{8,9},{9,8},{10,11... | collective-permute-start | bytes 884744 | tf_op jit(solution)/shard_map/ppermute | solution.py:18
  13.4 0.2 columns.1
  13.6 1.0 %collective-permute-done.2 = f32[1,4,2,72,128]{4,3,2,1,0:T(8,128)S(1)} collective-permute-done((f32[1,4,2,72,128]{4,3,2,1,0:T(8,128)S(1)}, f32[1,4,2,72,128]{4,3,2,1,0:T(8,128)S(1)}, u32[]{:S(2)}, u32[]{:S(2)}) %collective-permute-start.2) | collective-permute-done | bytes 294944 | tf_op jit(solution)/shard_map/ppermute | solution.py:18
  14.7 1.3 %collective-permute-start.3 = (f32[152,128]{1,0:T(8,128)S(1)}, f32[152,128]{1,0:T(8,128)S(1)}, u32[]{:S(2)}, u32[]{:S(2)}) collective-permute-start(f32[152,128]{1,0:T(8,128)S(1)} %get-tuple-element.42), channel_id=1, source_target_pairs={{0,2},{2,0},{4,6},{6,4},{1,3},{3,1},{5,7},{7,5},{8,10},{10,8},{12,... | collective-permute-start | bytes 233480 | tf_op jit(solution)/shard_map/ppermute | solution.py:18
  15.9 1.2 %collective-permute-start.4 = (f32[152,128]{1,0:T(8,128)S(1)}, f32[152,128]{1,0:T(8,128)S(1)}, u32[]{:S(2)}, u32[]{:S(2)}) collective-permute-start(f32[152,128]{1,0:T(8,128)S(1)} %get-tuple-element.43), channel_id=1, source_target_pairs={{0,6},{2,4},{4,2},{6,0},{1,7},{3,5},{5,3},{7,1},{8,14},{10,12},{12... | collective-permute-start | bytes 233480 | tf_op jit(solution)/shard_map/ppermute | solution.py:18
  17.2 0.2 collective-permute-start.5
  17.4 1.7 %pole.1 = (f32[3,4,32,128]{3,2,1,0:T(8,128)}, f32[3,4,32,128]{3,2,1,0:T(8,128)S(1)}, f32[4,32,128]{2,1,0:T(8,128)S(1)}) custom-call(f32[3,4]{1,0:T(4,128)} %table_in.1, f32[3,4,32,128]{3,2,1,0:T(8,128)S(1)} %get-tuple-element.37.refs_0_.e.refs_4_, f32[3,4,32,128]{3,2,1,0:T(8,128)} %pole_in.1, s32[4,32,128]{2,1,0:T(8,128)} %material_in.1, ...), custom_call_target="tpu_custom_call" | custom-call | tf_op jit(solution)/shard_map/pole/pallas_call | solution.py:715
  19.1 3.4 %collective-permute-done.5.refs_3_ = f32[144,128]{1,0:T(8,128)S(1)} collective-permute-done((f32[144,128]{1,0:T(8,128)S(1)}, f32[144,128]{1,0:T(8,128)S(1)}, u32[]{:S(2)}, u32[]{:S(2)}) %collective-permute-start.5) | collective-permute-done | bytes 73760 | tf_op jit(solution)/shard_map/ppermute | solution.py:18
  22.5 0.0 collective-permute-done.3.refs_1_.refs_7_
  22.5 0.0 collective-permute-done.4.refs_2_.refs_8_
  22.6 2.5 %collective-permute-start.6 = (f32[104,128]{1,0:T(8,128)S(1)}, f32[104,128]{1,0:T(8,128)S(1)}, u32[]{:S(2)}, u32[]{:S(2)}) collective-permute-start(f32[104,128]{1,0:T(8,128)S(1)} %get-tuple-element.47), channel_id=1, source_target_pairs={{0,24},{8,16},{16,8},{24,0},{1,25},{9,17},{17,9},{25,1},{2,26},{10... | collective-permute-start | bytes 159752 | tf_op jit(solution)/shard_map/ppermute | solution.py:18
  25.0 2.4 %collective-permute-done.6.refs_9_ = f32[104,128]{1,0:T(8,128)S(1)} collective-permute-done((f32[104,128]{1,0:T(8,128)S(1)}, f32[104,128]{1,0:T(8,128)S(1)}, u32[]{:S(2)}, u32[]{:S(2)}) %collective-permute-start.6) | collective-permute-done | bytes 53280 | tf_op jit(solution)/shard_map/ppermute | solution.py:18
  27.5 2.0 %collective-permute-start.7 = (f32[72,128]{1,0:T(8,128)S(1)}, f32[72,128]{1,0:T(8,128)S(1)}, u32[]{:S(2)}, u32[]{:S(2)}) collective-permute-start(f32[72,128]{1,0:T(8,128)S(1)} %slice_add_fusion.refs_1_), channel_id=1, source_target_pairs={{0,1},{1,0},{2,3},{3,2},{4,5},{5,4},{6,7},{7,6},{8,9},{9,8},{10,11... | collective-permute-start | bytes 110600 | tf_op jit(solution)/shard_map/ppermute | solution.py:18
  29.4 1.2 %fields.1 = (f32[3,4,32,128]{3,2,1,0:T(8,128)}, f32[3,4,32,128]{3,2,1,0:T(8,128)}, f32[3,32,128]{2,1,0:T(8,128)S(1)}, f32[3,32,128]{2,1,0:T(8,128)S(1)}, f32[32,128]{1,0:T(8,128)S(1)}) custom-call(f32[3,4,32,128]{3,2,1,0:T(8,128)S(1)} %get-tuple-element.37.refs_0_.e.refs_4_, f32[3,4,32,128]{3,2,1,0:T(8,128)S(1)} %get-tuple-element.38.refs_1_.refs_5_, ...), custom_call_target="tpu_custom_call" | custom-call | tf_op jit(solution)/shard_map/fields/pallas_call | solution.py:799
  30.7 0.0 collective-permute-done.7.refs_0_
  30.7 1.0 %inject.1 = (f32[3,4,32,128]{3,2,1,0:T(8,128)}, f32[3,4,32,128]{3,2,1,0:T(8,128)}) custom-call(f32[72,128]{1,0:T(8,128)S(1)} %collective-permute-done.7.refs_0_, f32[72,128]{1,0:T(8,128)S(1)} %slice_add_fusion.refs_1_, f32[3,32,128]{2,1,0:T(8,128)S(1)} %get-tuple-element.49.refs_2_, ...), custom_call_target="tpu_custom_call", output_to_operand_aliasing={{0}: (5, {}), {1}: (6, {})} | custom-call | tf_op jit(solution)/shard_map/inject/pallas_call | solution.py:813
  (3 shorter events, 0.1 us)
Async XLA Ops:
  1.8 7.0 %collective-permute-start.1 = (f32[6,32,128]{2,1,0:T(8,128)S(1)}, f32[6,32,128]{2,1,0:T(8,128)S(1)}, u32[]{:S(2)}, u32[]{:S(2)}) collective-permute-start(f32[6,32,128]{2,1,0:T(8,128)S(1)} %get-tuple-element.34), channel_id=1, source_target_pairs={{0,1},{1,0},{2,3},{3,2},{4,5},{5,4},{6,7},{7,6},{8,9},{9,8},{10,11... | collective-permute-start | bytes 294920 | tf_op jit(solution)/shard_map/ppermute | solution.py:18
  1.9 6.9 %collective-permute-start = (f32[20,8,128]{2,1,0:T(8,128)S(1)}, f32[20,8,128]{2,1,0:T(8,128)S(1)}, u32[]{:S(2)}, u32[]{:S(2)}) collective-permute-start(f32[20,8,128]{2,1,0:T(8,128)S(1)} %get-tuple-element.31.refs_1_), channel_id=1, source_target_pairs={{0,8},{8,0},{16,24},{24,16},{1,9},{9,1},{17,25},{25,17},{2,10},{10... | collective-permute-start | bytes 245768 | tf_op jit(solution)/shard_map/ppermute | solution.py:18
  13.0 1.6 %collective-permute-start.2 = (f32[1,4,2,72,128]{4,3,2,1,0:T(8,128)S(1)}, f32[1,4,2,72,128]{4,3,2,1,0:T(8,128)S(1)}, u32[]{:S(2)}, u32[]{:S(2)}) collective-permute-start(f32[1,4,2,72,128]{4,3,2,1,0:T(8,128)S(1)} %get-tuple-element.36), channel_id=1, source_target_pairs={{0,1},{1,0},{2,3},{3,2},{4,5},{5,4},{6,7},{7,6},{8,9},{9,8},{10,11... | collective-permute-start | bytes 884744 | tf_op jit(solution)/shard_map/ppermute | solution.py:18
  14.7 7.8 %collective-permute-start.3 = (f32[152,128]{1,0:T(8,128)S(1)}, f32[152,128]{1,0:T(8,128)S(1)}, u32[]{:S(2)}, u32[]{:S(2)}) collective-permute-start(f32[152,128]{1,0:T(8,128)S(1)} %get-tuple-element.42), channel_id=1, source_target_pairs={{0,2},{2,0},{4,6},{6,4},{1,3},{3,1},{5,7},{7,5},{8,10},{10,8},{12,... | collective-permute-start | bytes 233480 | tf_op jit(solution)/shard_map/ppermute | solution.py:18
  15.9 6.6 %collective-permute-start.4 = (f32[152,128]{1,0:T(8,128)S(1)}, f32[152,128]{1,0:T(8,128)S(1)}, u32[]{:S(2)}, u32[]{:S(2)}) collective-permute-start(f32[152,128]{1,0:T(8,128)S(1)} %get-tuple-element.43), channel_id=1, source_target_pairs={{0,6},{2,4},{4,2},{6,0},{1,7},{3,5},{5,3},{7,1},{8,14},{10,12},{12... | collective-permute-start | bytes 233480 | tf_op jit(solution)/shard_map/ppermute | solution.py:18
  17.2 5.3 %collective-permute-start.5 = (f32[144,128]{1,0:T(8,128)S(1)}, f32[144,128]{1,0:T(8,128)S(1)}, u32[]{:S(2)}, u32[]{:S(2)}) collective-permute-start(f32[144,128]{1,0:T(8,128)S(1)} %get-tuple-element.44), channel_id=1, source_target_pairs={{0,4},{2,6},{4,0},{6,2},{1,5},{3,7},{5,1},{7,3},{8,12},{10,14},{12... | collective-permute-start | bytes 221192 | tf_op jit(solution)/shard_map/ppermute | solution.py:18
  22.6 4.9 %collective-permute-start.6 = (f32[104,128]{1,0:T(8,128)S(1)}, f32[104,128]{1,0:T(8,128)S(1)}, u32[]{:S(2)}, u32[]{:S(2)}) collective-permute-start(f32[104,128]{1,0:T(8,128)S(1)} %get-tuple-element.47), channel_id=1, source_target_pairs={{0,24},{8,16},{16,8},{24,0},{1,25},{9,17},{17,9},{25,1},{2,26},{10... | collective-permute-start | bytes 159752 | tf_op jit(solution)/shard_map/ppermute | solution.py:18
  27.5 3.2 %collective-permute-start.7 = (f32[72,128]{1,0:T(8,128)S(1)}, f32[72,128]{1,0:T(8,128)S(1)}, u32[]{:S(2)}, u32[]{:S(2)}) collective-permute-start(f32[72,128]{1,0:T(8,128)S(1)} %slice_add_fusion.refs_1_), channel_id=1, source_target_pairs={{0,1},{1,0},{2,3},{3,2},{4,5},{5,4},{6,7},{7,6},{8,9},{9,8},{10,11... | collective-permute-start | bytes 110600 | tf_op jit(solution)/shard_map/ppermute | solution.py:18

commit v5 on v4

--- a/solution.py
+++ b/solution.py
@@ -150,7 +150,7 @@
                 back = (powers[0][0], -powers[0][1])
                 p = packed[f, 6:7, :]
                 q = packed[f, 7:8, :]
-                line = lax.broadcasted_iota(jnp.int32, (8, p.shape[-1]), 0)
+                line = lax.broadcasted_iota(jnp.int32, (16, p.shape[-1]), 0)
                 one_first = jnp.zeros(line.shape, jnp.float32)
                 one_second = one_first
                 for xr in range(xslots):
@@ -163,13 +163,15 @@
             def product(lefts, rights):
                 lh, ll = split(jnp.concatenate(lefts, axis=1))
                 rh, rl = split(jnp.concatenate(rights, axis=1))
-                return dot_nt(lh, rh) + dot_nt(lh, rl) + dot_nt(ll, rh)
+                both = dot_nt(jnp.concatenate([lh, ll], axis=0), rh)
+                rows = lh.shape[0]
+                return both[:rows] + dot_nt(lh, rl) + both[rows:]
 
             acc_even[...] += product(firsts, coses)
             acc_odd[...] += product(seconds, sines)
             return carry
 
-        lax.fori_loop(0, freqs // 2, pair, 0)
+        lax.fori_loop(0, freqs // 2, pair, 0, unroll=4)
         if not closing:
             return
 
@@ -673,7 +675,7 @@
     block = per * wx + 8
     part_shape = pltpu.VMEM((zslots // 2, sy, xslots, block, wy), f32)
     assert freqs % 2 == 0
-    sums = pltpu.VMEM((4 * xslots * wx + 8, half), f32)
+    sums = pltpu.VMEM((4 * xslots * wx + 16, half), f32)
     tables = [
         pltpu.VMEM((xslots, 2, freqs, width), f32),
         pltpu.VMEM((xlevels, 2, freqs, width), f32),

time: 31.8 us -> 29.6 us (0.931)
  Pallas kernels: 13.7 us -> 11.2 us
  starting transfers between devices: 10.4 us -> 11.5 us
  waiting for transfers between devices: 6.83 us -> 6.08 us
    pallas_call x2, Pallas kernels: 8.32 us -> 5.77 us  [local(): pl.pallas_call(source_kernel(freqs, depth, wx, half, sizes, zslots, xslot...]
    ppermute x8, starting transfers between devices: 10.4 us -> 11.5 us  [exchange(): lax.ppermute(array, axis, [(i, i ^ mask) for i in range(lax.axis_size(axi...]
    ppermute x8, waiting for transfers between devices: 6.83 us -> 6.08 us  [exchange(): lax.ppermute(array, axis, [(i, i ^ mask) for i in range(lax.axis_size(axi...]
  transfers between devices with their start and end apart: 8 -> 8, of which waited for: 3 -> 3; matrix products, arithmetic and copies ran while one was open for 0% -> 0% of each run, Pallas kernels for 23% -> 21%
where the time goes in v5:
time: 29.6 us; the launch traced here: 29.4 us
  starting transfers between devices  11.5 us (39%)
  Pallas kernels  11.2 us (38%)
  waiting for transfers between devices  6.08 us (21%)
  between operations  0.69 us (2%)
    ppermute x8, starting transfers between devices, exchange(): lax.ppermute(array, axis, [(i, i ^ mask) for i in range(lax.axis_size(axi...  11.5 us
    ppermute x8, waiting for transfers between devices, exchange(): lax.ppermute(array, axis, [(i, i ^ mask) for i in range(lax.axis_size(axi...  6.08 us
    pallas_call x2, Pallas kernels, local(): pl.pallas_call(source_kernel(freqs, depth, wx, half, sizes, zslots, xslot...  5.77 us
    pallas_call x1, Pallas kernels, local(): pl.pallas_call(pole_kernel(depth, wx, wy), out_shape=(whole, pltpu.VMEM(w...  1.72 us
    pallas_call x1, Pallas kernels, local(): pl.pallas_call(field_kernel(freqs, depth, wx, wy, xbits, ybits, zbits, pe...  1.24 us
    pallas_call x1, Pallas kernels, local(): pl.pallas_call(pack_kernel(freqs, depth, wx, zbits), out_shape=[pltpu.VME...  1.14 us
    pallas_call x1, Pallas kernels, local(): pl.pallas_call(inject_kernel(depth, wx, wy, sy, sz, per, zcut), out_shape...  0.98 us
  transfers between devices with their start and end apart: 8, of which 3 were waited for; matrix products, arithmetic and copies ran while one was open for 0% of the time, Pallas kernels for 21%

profile of v5, /device:TPU:1, one launch (start us, length us, event | category | flops | bytes accessed | tf_op | source)
XLA Modules:
  0.0 29.4 jit_solution(10443226164927825753)
XLA Ops:
  0.6 1.1 %pack.1 = (f32[20,8,128]{2,1,0:T(8,128)S(1)}, f32[2,16,128]{2,1,0:T(8,128)S(1)}, f32[3,4,32,128]{3,2,1,0:T(8,128)S(1)}, f32[3,4,32,128]{3,2,1,0:T(8,128)S(1)}, f32[6,32,128]{2,1,0:T(8,128)S(1)}) custom-call(f32[3,4,32,128]{3,2,1,0:T(8,128)} %refs_0_.1, f32[3,4,32,128]{3,2,1,0:T(8,128)} %refs_1_.1, f32[16,8,128]{2,1,0:T(8,128)} %refs_2_.1, f32[2,128]{1,0:T(2,128)} %refs_3_.1, ...), custom_call_target="tpu_custom_call" | custom-call | tf_op jit(solution)/shard_map/pack/pallas_call | solution.py:646
  1.8 0.1 collective-permute-start.1
  1.9 2.8 %collective-permute-start = (f32[20,8,128]{2,1,0:T(8,128)S(1)}, f32[20,8,128]{2,1,0:T(8,128)S(1)}, u32[]{:S(2)}, u32[]{:S(2)}) collective-permute-start(f32[20,8,128]{2,1,0:T(8,128)S(1)} %get-tuple-element.31.refs_1_), channel_id=1, source_target_pairs={{0,8},{8,0},{16,24},{24,16},{1,9},{9,1},{17,25},{25,17},{2,10},{10... | collective-permute-start | bytes 245768 | tf_op jit(solution)/shard_map/ppermute | solution.py:18
  4.6 2.8 %source_own.1 = (f32[272,256]{1,0:T(8,128)S(1)}, f32[272,256]{1,0:T(8,128)S(1)}) custom-call(f32[2,16,128]{2,1,0:T(8,128)S(1)} %get-tuple-element.30.refs_0_, f32[20,8,128]{2,1,0:T(8,128)S(1)} %get-tuple-element.31.refs_1_), custom_call_target="tpu_custom_call" | custom-call | tf_op jit(solution)/shard_map/source_own/pallas_call | solution.py:686
  7.5 0.0 collective-permute-done.refs_1_.refs_2_.refs_5_
  7.5 0.0 collective-permute-done.1.refs_4_.refs_3_.refs_6_
  7.5 3.0 %source_both.1 = (f32[1,4,2,72,128]{4,3,2,1,0:T(8,128)S(1)}, f32[1,4,2,72,128]{4,3,2,1,0:T(8,128)S(1)}) custom-call(f32[2,16,128]{2,1,0:T(8,128)S(1)} %get-tuple-element.30.refs_0_, f32[20,8,128]{2,1,0:T(8,128)S(1)} %collective-permute-done.refs_1_.refs_2_.refs_5_, f32[272,256]{1,0:T(8,128)S(1)} %get-tuple-element.32.refs_2_, ...), custom_call_target="tpu_custom_call" | custom-call | tf_op jit(solution)/shard_map/source_all/source_both/pallas_call | solution.py:696
  10.4 0.6 %collective-permute-start.2 = (f32[1,4,2,72,128]{4,3,2,1,0:T(8,128)S(1)}, f32[1,4,2,72,128]{4,3,2,1,0:T(8,128)S(1)}, u32[]{:S(2)}, u32[]{:S(2)}) collective-permute-start(f32[1,4,2,72,128]{4,3,2,1,0:T(8,128)S(1)} %get-tuple-element.36), channel_id=1, source_target_pairs={{0,1},{1,0},{2,3},{3,2},{4,5},{5,4},{6,7},{7,6},{8,9},{9,8},{10,11... | collective-permute-start | bytes 884744 | tf_op jit(solution)/shard_map/ppermute | solution.py:18
  11.0 0.2 columns.1
  11.3 1.0 %collective-permute-done.2 = f32[1,4,2,72,128]{4,3,2,1,0:T(8,128)S(1)} collective-permute-done((f32[1,4,2,72,128]{4,3,2,1,0:T(8,128)S(1)}, f32[1,4,2,72,128]{4,3,2,1,0:T(8,128)S(1)}, u32[]{:S(2)}, u32[]{:S(2)}) %collective-permute-start.2) | collective-permute-done | bytes 294944 | tf_op jit(solution)/shard_map/ppermute | solution.py:18
  12.3 1.4 %collective-permute-start.3 = (f32[152,128]{1,0:T(8,128)S(1)}, f32[152,128]{1,0:T(8,128)S(1)}, u32[]{:S(2)}, u32[]{:S(2)}) collective-permute-start(f32[152,128]{1,0:T(8,128)S(1)} %get-tuple-element.42), channel_id=1, source_target_pairs={{0,2},{2,0},{4,6},{6,4},{1,3},{3,1},{5,7},{7,5},{8,10},{10,8},{12,... | collective-permute-start | bytes 233480 | tf_op jit(solution)/shard_map/ppermute | solution.py:18
  13.7 1.2 %collective-permute-start.4 = (f32[152,128]{1,0:T(8,128)S(1)}, f32[152,128]{1,0:T(8,128)S(1)}, u32[]{:S(2)}, u32[]{:S(2)}) collective-permute-start(f32[152,128]{1,0:T(8,128)S(1)} %get-tuple-element.43), channel_id=1, source_target_pairs={{0,6},{2,4},{4,2},{6,0},{1,7},{3,5},{5,3},{7,1},{8,14},{10,12},{12... | collective-permute-start | bytes 233480 | tf_op jit(solution)/shard_map/ppermute | solution.py:18
  14.9 0.1 collective-permute-start.5
  15.0 1.7 %pole.1 = (f32[3,4,32,128]{3,2,1,0:T(8,128)}, f32[3,4,32,128]{3,2,1,0:T(8,128)S(1)}, f32[4,32,128]{2,1,0:T(8,128)S(1)}) custom-call(f32[3,4]{1,0:T(4,128)} %table_in.1, f32[3,4,32,128]{3,2,1,0:T(8,128)S(1)} %get-tuple-element.37.refs_0_.e.refs_4_, f32[3,4,32,128]{3,2,1,0:T(8,128)} %pole_in.1, s32[4,32,128]{2,1,0:T(8,128)} %material_in.1, ...), custom_call_target="tpu_custom_call" | custom-call | tf_op jit(solution)/shard_map/pole/pallas_call | solution.py:717
  16.7 3.6 %collective-permute-done.5.refs_3_ = f32[144,128]{1,0:T(8,128)S(1)} collective-permute-done((f32[144,128]{1,0:T(8,128)S(1)}, f32[144,128]{1,0:T(8,128)S(1)}, u32[]{:S(2)}, u32[]{:S(2)}) %collective-permute-start.5) | collective-permute-done | bytes 73760 | tf_op jit(solution)/shard_map/ppermute | solution.py:18
  20.3 0.0 collective-permute-done.3.refs_1_.refs_7_
  20.3 0.0 collective-permute-done.4.refs_2_.refs_8_
  20.4 3.4 %collective-permute-start.6 = (f32[104,128]{1,0:T(8,128)S(1)}, f32[104,128]{1,0:T(8,128)S(1)}, u32[]{:S(2)}, u32[]{:S(2)}) collective-permute-start(f32[104,128]{1,0:T(8,128)S(1)} %get-tuple-element.47), channel_id=1, source_target_pairs={{0,24},{8,16},{16,8},{24,0},{1,25},{9,17},{17,9},{25,1},{2,26},{10... | collective-permute-start | bytes 159752 | tf_op jit(solution)/shard_map/ppermute | solution.py:18
  23.7 1.5 %collective-permute-done.6.refs_9_ = f32[104,128]{1,0:T(8,128)S(1)} collective-permute-done((f32[104,128]{1,0:T(8,128)S(1)}, f32[104,128]{1,0:T(8,128)S(1)}, u32[]{:S(2)}, u32[]{:S(2)}) %collective-permute-start.6) | collective-permute-done | bytes 53280 | tf_op jit(solution)/shard_map/ppermute | solution.py:18
  25.3 1.9 %collective-permute-start.7 = (f32[72,128]{1,0:T(8,128)S(1)}, f32[72,128]{1,0:T(8,128)S(1)}, u32[]{:S(2)}, u32[]{:S(2)}) collective-permute-start(f32[72,128]{1,0:T(8,128)S(1)} %slice_add_fusion.refs_1_), channel_id=1, source_target_pairs={{0,1},{1,0},{2,3},{3,2},{4,5},{5,4},{6,7},{7,6},{8,9},{9,8},{10,11... | collective-permute-start | bytes 110600 | tf_op jit(solution)/shard_map/ppermute | solution.py:18
  27.2 1.2 %fields.1 = (f32[3,4,32,128]{3,2,1,0:T(8,128)}, f32[3,4,32,128]{3,2,1,0:T(8,128)}, f32[3,32,128]{2,1,0:T(8,128)S(1)}, f32[3,32,128]{2,1,0:T(8,128)S(1)}, f32[32,128]{1,0:T(8,128)S(1)}) custom-call(f32[3,4,32,128]{3,2,1,0:T(8,128)S(1)} %get-tuple-element.37.refs_0_.e.refs_4_, f32[3,4,32,128]{3,2,1,0:T(8,128)S(1)} %get-tuple-element.38.refs_1_.refs_5_, ...), custom_call_target="tpu_custom_call" | custom-call | tf_op jit(solution)/shard_map/fields/pallas_call | solution.py:801
  28.4 0.0 collective-permute-done.7.refs_0_
  28.5 1.0 %inject.1 = (f32[3,4,32,128]{3,2,1,0:T(8,128)}, f32[3,4,32,128]{3,2,1,0:T(8,128)}) custom-call(f32[72,128]{1,0:T(8,128)S(1)} %collective-permute-done.7.refs_0_, f32[72,128]{1,0:T(8,128)S(1)} %slice_add_fusion.refs_1_, f32[3,32,128]{2,1,0:T(8,128)S(1)} %get-tuple-element.49.refs_2_, ...), custom_call_target="tpu_custom_call", output_to_operand_aliasing={{0}: (5, {}), {1}: (6, {})} | custom-call | tf_op jit(solution)/shard_map/inject/pallas_call | solution.py:815
  (3 shorter events, 0.1 us)
Async XLA Ops:
  1.8 5.7 %collective-permute-start.1 = (f32[6,32,128]{2,1,0:T(8,128)S(1)}, f32[6,32,128]{2,1,0:T(8,128)S(1)}, u32[]{:S(2)}, u32[]{:S(2)}) collective-permute-start(f32[6,32,128]{2,1,0:T(8,128)S(1)} %get-tuple-element.34), channel_id=1, source_target_pairs={{0,1},{1,0},{2,3},{3,2},{4,5},{5,4},{6,7},{7,6},{8,9},{9,8},{10,11... | collective-permute-start | bytes 294920 | tf_op jit(solution)/shard_map/ppermute | solution.py:18
  1.9 5.6 %collective-permute-start = (f32[20,8,128]{2,1,0:T(8,128)S(1)}, f32[20,8,128]{2,1,0:T(8,128)S(1)}, u32[]{:S(2)}, u32[]{:S(2)}) collective-permute-start(f32[20,8,128]{2,1,0:T(8,128)S(1)} %get-tuple-element.31.refs_1_), channel_id=1, source_target_pairs={{0,8},{8,0},{16,24},{24,16},{1,9},{9,1},{17,25},{25,17},{2,10},{10... | collective-permute-start | bytes 245768 | tf_op jit(solution)/shard_map/ppermute | solution.py:18
  10.4 1.8 %collective-permute-start.2 = (f32[1,4,2,72,128]{4,3,2,1,0:T(8,128)S(1)}, f32[1,4,2,72,128]{4,3,2,1,0:T(8,128)S(1)}, u32[]{:S(2)}, u32[]{:S(2)}) collective-permute-start(f32[1,4,2,72,128]{4,3,2,1,0:T(8,128)S(1)} %get-tuple-element.36), channel_id=1, source_target_pairs={{0,1},{1,0},{2,3},{3,2},{4,5},{5,4},{6,7},{7,6},{8,9},{9,8},{10,11... | collective-permute-start | bytes 884744 | tf_op jit(solution)/shard_map/ppermute | solution.py:18
  12.3 8.0 %collective-permute-start.3 = (f32[152,128]{1,0:T(8,128)S(1)}, f32[152,128]{1,0:T(8,128)S(1)}, u32[]{:S(2)}, u32[]{:S(2)}) collective-permute-start(f32[152,128]{1,0:T(8,128)S(1)} %get-tuple-element.42), channel_id=1, source_target_pairs={{0,2},{2,0},{4,6},{6,4},{1,3},{3,1},{5,7},{7,5},{8,10},{10,8},{12,... | collective-permute-start | bytes 233480 | tf_op jit(solution)/shard_map/ppermute | solution.py:18
  13.7 6.6 %collective-permute-start.4 = (f32[152,128]{1,0:T(8,128)S(1)}, f32[152,128]{1,0:T(8,128)S(1)}, u32[]{:S(2)}, u32[]{:S(2)}) collective-permute-start(f32[152,128]{1,0:T(8,128)S(1)} %get-tuple-element.43), channel_id=1, source_target_pairs={{0,6},{2,4},{4,2},{6,0},{1,7},{3,5},{5,3},{7,1},{8,14},{10,12},{12... | collective-permute-start | bytes 233480 | tf_op jit(solution)/shard_map/ppermute | solution.py:18
  14.9 5.3 %collective-permute-start.5 = (f32[144,128]{1,0:T(8,128)S(1)}, f32[144,128]{1,0:T(8,128)S(1)}, u32[]{:S(2)}, u32[]{:S(2)}) collective-permute-start(f32[144,128]{1,0:T(8,128)S(1)} %get-tuple-element.44), channel_id=1, source_target_pairs={{0,4},{2,6},{4,0},{6,2},{1,5},{3,7},{5,1},{7,3},{8,12},{10,14},{12... | collective-permute-start | bytes 221192 | tf_op jit(solution)/shard_map/ppermute | solution.py:18
  20.4 4.9 %collective-permute-start.6 = (f32[104,128]{1,0:T(8,128)S(1)}, f32[104,128]{1,0:T(8,128)S(1)}, u32[]{:S(2)}, u32[]{:S(2)}) collective-permute-start(f32[104,128]{1,0:T(8,128)S(1)} %get-tuple-element.47), channel_id=1, source_target_pairs={{0,24},{8,16},{16,8},{24,0},{1,25},{9,17},{17,9},{25,1},{2,26},{10... | collective-permute-start | bytes 159752 | tf_op jit(solution)/shard_map/ppermute | solution.py:18
  25.3 3.2 %collective-permute-start.7 = (f32[72,128]{1,0:T(8,128)S(1)}, f32[72,128]{1,0:T(8,128)S(1)}, u32[]{:S(2)}, u32[]{:S(2)}) collective-permute-start(f32[72,128]{1,0:T(8,128)S(1)} %slice_add_fusion.refs_1_), channel_id=1, source_target_pairs={{0,1},{1,0},{2,3},{3,2},{4,5},{5,4},{6,7},{7,6},{8,9},{9,8},{10,11... | collective-permute-start | bytes 110600 | tf_op jit(solution)/shard_map/ppermute | solution.py:18

commit v6 on v5

--- a/solution.py
+++ b/solution.py
@@ -85,7 +85,13 @@
             old_even, old_odd = refs[2:4]
             keep, send, xbase, xpow, ypow, acc_even, acc_odd = refs[4 + zbits :]
         else:
-            acc_even, acc_odd, xbase, xpow, ypow = refs[2:]
+            e_in, h_in, acc_even, acc_odd, e_near, h_near, xbase, xpow, ypow, sems = refs[2:]
+            copies = [
+                pltpu.make_async_copy(source, target, sems.at[i])
+                for i, (source, target) in enumerate(((e_in, e_near), (h_in, h_near)))
+            ]
+            for copy in copies:
+                copy.start()
         ix, iy, iz = (lax.axis_index(name) for name in ("gx", "gy", "gz"))
         xbit, ybit, zbit = bits_of(sx), bits_of(sy), bits_of(zslots)
         starts = []
@@ -173,6 +179,8 @@
 
         lax.fori_loop(0, freqs // 2, pair, 0, unroll=4)
         if not closing:
+            for copy in copies:
+                copy.wait()
             return
 
         def slot(tile):
@@ -257,22 +265,25 @@
 
 def pack_kernel(freqs, depth, wx, zbits):
     def body(*refs):
-        e_in, h_in, cotangent, cosines, wavenumber, time_phase = refs[:6]
-        message, waves, e, h = refs[6:10]
-        layers = refs[10 : 10 + zbits]
-        cos_near, wave_near, phase_near, sems = refs[10 + zbits :]
+        e_in, h_in, cotangent, cosines, wavenumber, time_phase, message, waves = refs[:8]
+        layers = refs[8 : 8 + zbits]
+        edge, cos_near, wave_near, phase_near, sems = refs[8 + zbits :]
+        upper = lax.axis_index("gx") & 1
+        tile = pl.ds(pl.multiple_of((1 - upper) * (wx - 8), 8), 8)
+        pairs = [
+            (cotangent, message.at[0:freqs]),
+            (e_in.at[:, :, tile], edge.at[0:3]),
+            (h_in.at[:, :, tile], edge.at[3:6]),
+            (cosines, cos_near),
+            (wavenumber, wave_near),
+            (time_phase, phase_near),
+        ]
+        for k, layer in enumerate(layers):
+            at = (1 - ((lax.axis_index("gz") >> k) & 1)) * (depth - 1)
+            pairs += [(e_in.at[:, at], layer.at[0:3]), (h_in.at[:, at], layer.at[3:6])]
         copies = [
             pltpu.make_async_copy(source, target, sems.at[i])
-            for i, (source, target) in enumerate(
-                (
-                    (e_in, e),
-                    (h_in, h),
-                    (cotangent, message.at[0:freqs]),
-                    (cosines, cos_near),
-                    (wavenumber, wave_near),
-                    (time_phase, phase_near),
-                )
-            )
+            for i, (source, target) in enumerate(pairs)
         ]
         for copy in copies:
             copy.start()
@@ -286,17 +297,11 @@
             for f in range(freqs):
                 value = jnp.where(which == f, near[f], value)
             waves[i] = value
-        at = (1 - (lax.axis_index("gx") & 1)) * (wx - 1)
+        at = (1 - upper) * 7
         for i in range(6):
             for z in range(depth):
                 row = i * depth + z
-                field = (e, h)[i // 3]
-                message[freqs + 1 + row // 8, row % 8 : row % 8 + 1] = field[i % 3, z, pl.ds(at, 1), :]
-        for k, layer in enumerate(layers):
-            at_z = (1 - ((lax.axis_index("gz") >> k) & 1)) * (depth - 1)
-            for i in range(3):
-                layer[i] = e[i, at_z]
-                layer[3 + i] = h[i, at_z]
+                message[freqs + 1 + row // 8, row % 8 : row % 8 + 1] = edge[i, z, pl.ds(at, 1), :]
 
     return body
 
@@ -437,7 +442,7 @@
         ys = refs[6 + zbits : 6 + zbits + ybits]
         xs = [x[x.shape[0] - 6 * depth - 8 :] for x in refs[6 + zbits + ybits : 5 + zbits + ybits + xbits]]
         sides = refs[5 + zbits + ybits + xbits : 5 + 2 * zbits + ybits + xbits]
-        e_out, h_out, e_top, h_top, coef_top = refs[5 + 2 * zbits + ybits + xbits :]
+        e_out, h_out = refs[5 + 2 * zbits + ybits + xbits :]
         ix, iy, iz = (lax.axis_index(name) for name in ("gx", "gy", "gz"))
         xlow, xhigh = near_flags(ix, xbits)
         ylow, yhigh = near_flags(iy, ybits)
@@ -545,14 +550,10 @@
         )
         coef = coef_ref[...].reshape(size, wy)
         shape = (depth, wx, wy)
-        tail = size - wx
         for i, magnetic in enumerate((hx, hy, hz)):
             value = flat(base_e, i) + coef * curl[i]
             h_out[i] = magnetic.reshape(shape)
             e_out[i] = value.reshape(shape)
-            e_top[i] = value[tail:]
-            h_top[i] = magnetic[tail:]
-        coef_top[...] = coef[tail:]
 
     return body
 
@@ -560,7 +561,18 @@
 def inject_kernel(depth, wx, wy, sy, sz, per, zcut):
     def body(*refs):
         blocks = refs[: 1 << zcut]
-        e_top, h_top, coef_top, e_in, h_in, e_out, h_out, e_new, h_new, sems = refs[1 << zcut :]
+        e_near, h_near, coef_ref, e_out, h_out, e_new, h_new, sems = refs[1 << zcut :]
+        last = depth - 1
+        others = slice(0, last)
+        copies = [
+            pltpu.make_async_copy(e_near.at[:, others], e_out.at[:, others], sems.at[0]),
+            pltpu.make_async_copy(h_near.at[:, others], h_out.at[:, others], sems.at[1]),
+            pltpu.make_async_copy(h_near.at[2, last], h_out.at[2, last], sems.at[2]),
+        ]
+        for copy in copies:
+            copy.start()
+        h_copy = pltpu.make_async_copy(h_new, h_out.at[0:2, last], sems.at[3])
+        e_copy = pltpu.make_async_copy(e_new, e_out.at[:, last], sems.at[4])
         ix, iy, iz = (lax.axis_index(name) for name in ("gx", "gy", "gz"))
 
         @pl.when(iz == sz - 1)
@@ -592,20 +604,26 @@
             beside = inside_y * blocks[2 // per][per * wx : per * wx + 8].T[0:wx, 1:2]
             last_x = jnp.where(line == 0, before, pltpu.roll(magnetic_y, 1, 0))
             last_y = jnp.where(lane == 0, beside, pltpu.roll(magnetic_x, 1, 1))
-            coef = coef_top[...]
-            h_new[0] = h_top[0] - courant * magnetic_x
-            h_new[1] = h_top[1] - courant * magnetic_y
-            h_copy = pltpu.make_async_copy(h_new, h_out.at[0:2, depth - 1], sems.at[1])
-            h_copy.start()
-            e_new[0] = e_top[0] + coef * (courant * magnetic_y - electric_x)
-            e_new[1] = e_top[1] - coef * (courant * magnetic_x + electric_y)
-            e_new[2] = e_top[2] + coef * courant * (
+            coef = coef_ref[last]
+            h_new[0] = h_near[0, last] - courant * magnetic_x
+            h_new[1] = h_near[1, last] - courant * magnetic_y
+            e_new[0] = e_near[0, last] + coef * (courant * magnetic_y - electric_x)
+            e_new[1] = e_near[1, last] - coef * (courant * magnetic_x + electric_y)
+            e_new[2] = e_near[2, last] + coef * courant * (
                 (magnetic_x - last_y) - (magnetic_y - last_x)
             )
-            e_copy = pltpu.make_async_copy(e_new, e_out.at[:, depth - 1], sems.at[0])
-            e_copy.start()
-            h_copy.wait()
-            e_copy.wait()
+
+        @pl.when(iz != sz - 1)
+        def _():
+            for i in range(3):
+                e_new[i] = e_near[i, last]
+            for i in range(2):
+                h_new[i] = h_near[i, last]
+
+        h_copy.start()
+        e_copy.start()
+        for copy in (*copies, h_copy, e_copy):
+            copy.wait()
 
     return body
 
@@ -643,27 +661,25 @@
     zcut = bits_of(zslots)
 
     assert 8 % depth == 0
-    mine, waves, e_near, h_near, *layers = pl.pallas_call(
+    mine, waves, *layers = pl.pallas_call(
         pack_kernel(freqs, depth, wx, zbits),
         out_shape=[
             pltpu.VMEM((freqs + 1 + 6 * depth // 8, 8, LANES), f32),
             pltpu.VMEM((2, freqs, LANES), f32),
-            pltpu.VMEM(e_field.shape, f32),
-            pltpu.VMEM(h_field.shape, f32),
         ]
         + [pltpu.VMEM((6, wx, wy), f32)] * zbits,
         in_specs=[hbm] * 6,
-        out_specs=[vmem] * (4 + zbits),
+        out_specs=[vmem] * (2 + zbits),
         scratch_shapes=[
+            pltpu.VMEM((6, depth, 8, LANES), f32),
             pltpu.VMEM((2, LANES), f32),
             pltpu.SMEM((freqs,), f32),
             pltpu.SMEM((freqs,), f32),
-            pltpu.SemaphoreType.DMA((6,)),
+            pltpu.SemaphoreType.DMA((6 + 2 * zbits,)),
         ],
         compiler_params=small,
         name="pack",
     )(*in_hbm(e_field, h_field, cotangent, cosines, wavenumber, time_phase))
-    e_near, h_near = in_vmem(e_near, h_near)
     theirs = exchange(mine, "gx", 1)
     zs = [exchange(layers[k], "gz", (2 << k) - 1) for k in range(zbits)]
     zs = in_vmem(*zs)
@@ -683,15 +699,16 @@
     ]
     medium = pltpu.CompilerParams(vmem_limit_bytes=24 << 20)
     waves, mine = in_vmem(waves, mine)
-    own = pl.pallas_call(
+    *own, e_near, h_near = pl.pallas_call(
         source_kernel(freqs, depth, wx, half, sizes, zslots, xslots, scale, zbits, False),
-        out_shape=(sums, sums),
-        in_specs=[vmem] * 2,
-        out_specs=(vmem, vmem),
-        scratch_shapes=tables,
+        out_shape=(sums, sums, pltpu.VMEM(e_field.shape, f32), pltpu.VMEM(h_field.shape, f32)),
+        in_specs=[vmem, vmem, hbm, hbm],
+        out_specs=(vmem,) * 4,
+        scratch_shapes=tables + [pltpu.SemaphoreType.DMA((2,))],
         compiler_params=medium,
         name="source_own",
-    )(waves, mine)
+    )(waves, mine, *in_hbm(e_field, h_field))
+    e_near, h_near = in_vmem(e_near, h_near)
     with jax.named_scope("source_all"):
         keep, send = pl.pallas_call(
             source_kernel(freqs, depth, wx, half, sizes, zslots, xslots, scale, zbits, True),
@@ -797,12 +814,11 @@
         terms = [keep, xs[-1]]
     part = sum(term[:rows] for term in terms)
 
-    layer = pltpu.VMEM((3, wx, wy), f32)
-    e_next, h_next, e_top, h_top, coef_top = pl.pallas_call(
+    e_most, h_most = pl.pallas_call(
         field_kernel(freqs, depth, wx, wy, xbits, ybits, zbits, per * wx + 2),
-        out_shape=(whole, whole, layer, layer, pltpu.VMEM((wx, wy), f32)),
+        out_shape=(pltpu.VMEM(whole.shape, f32), pltpu.VMEM(whole.shape, f32)),
         in_specs=[vmem] * (5 + xbits + ybits + 2 * zbits),
-        out_specs=(vmem,) * 5,
+        out_specs=(vmem,) * 2,
         compiler_params=pltpu.CompilerParams(vmem_limit_bytes=16 << 20),
         name="fields",
     )(e_near, h_near, base_e, coef, *in_vmem(first, theirs), *near, *in_vmem(*xs, *sides))
@@ -815,17 +831,16 @@
     e_next, h_next = pl.pallas_call(
         inject_kernel(depth, wx, wy, sy, sz, per, zcut),
         out_shape=(whole, whole),
-        in_specs=[vmem] * (len(blocks) + 3) + [hbm] * 2,
+        in_specs=[vmem] * (len(blocks) + 3),
         out_specs=(hbm, hbm),
         scratch_shapes=[
             pltpu.VMEM((3, wx, wy), f32),
             pltpu.VMEM((2, wx, wy), f32),
-            pltpu.SemaphoreType.DMA((2,)),
+            pltpu.SemaphoreType.DMA((5,)),
         ],
-        input_output_aliases={len(blocks) + 3: 0, len(blocks) + 4: 1},
         compiler_params=small,
         name="inject",
-    )(*in_vmem(*blocks, e_top, h_top, coef_top), e_next, h_next)
+    )(*in_vmem(*blocks, e_most, h_most), coef)
     return (e_next, h_next, pole_next)
 
 

time: 29.6 us -> 29.2 us (0.986)
  Pallas kernels: 11.2 us -> 10.4 us
    pallas_call x1, Pallas kernels: 1.24 us -> 0.56 us  [local(): pl.pallas_call(field_kernel(freqs, depth, wx, wy, xbits, ybits, zbits, pe...]
  transfers between devices with their start and end apart: 8 -> 8, of which waited for: 3 -> 4; matrix products, arithmetic and copies ran while one was open for 0% -> 0% of each run, Pallas kernels for 21% -> 19%
where the time goes in v6:
time: 29.2 us; the launch traced here: 29 us
  starting transfers between devices  11.5 us (39%)
  Pallas kernels  10.4 us (36%)
  waiting for transfers between devices  6.36 us (22%)
  between operations  0.7 us (2%)
    ppermute x8, starting transfers between devices, exchange(): lax.ppermute(array, axis, [(i, i ^ mask) for i in range(lax.axis_size(axi...  11.5 us
    ppermute x8, waiting for transfers between devices, exchange(): lax.ppermute(array, axis, [(i, i ^ mask) for i in range(lax.axis_size(axi...  6.36 us
    pallas_call x2, Pallas kernels, local(): pl.pallas_call(source_kernel(freqs, depth, wx, half, sizes, zslots, xslot...  5.8 us
    pallas_call x1, Pallas kernels, local(): pl.pallas_call(pole_kernel(depth, wx, wy), out_shape=(whole, pltpu.VMEM(w...  1.72 us
    pallas_call x1, Pallas kernels, local(): pl.pallas_call(inject_kernel(depth, wx, wy, sy, sz, per, zcut), out_shape...  1.02 us
    pallas_call x1, Pallas kernels, local(): pl.pallas_call(pack_kernel(freqs, depth, wx, zbits), out_shape=[pltpu.VME...  1.01 us
  transfers between devices with their start and end apart: 8, of which 4 were waited for; matrix products, arithmetic and copies ran while one was open for 0% of the time, Pallas kernels for 19%

profile of v6, /device:TPU:1, one launch (start us, length us, event | category | flops | bytes accessed | tf_op | source)
XLA Modules:
  0.0 29.0 jit_solution(1679633797828193523)
XLA Ops:
  0.6 1.0 %pack.1 = (f32[20,8,128]{2,1,0:T(8,128)S(1)}, f32[2,16,128]{2,1,0:T(8,128)S(1)}, f32[6,32,128]{2,1,0:T(8,128)S(1)}) custom-call(f32[3,4,32,128]{3,2,1,0:T(8,128)} %refs_2_.3, f32[3,4,32,128]{3,2,1,0:T(8,128)} %refs_3_.3, f32[16,8,128]{2,1,0:T(8,128)} %refs_2_.2, f32[2,128]{1,0:T(2,128)} %refs_3_.2, f32[16]{0:T(128)} %refs_4_.1, f32[16]{0:T(128)} %refs_5_.1), custom_call_target="tpu_custom_call" | custom-call | tf_op jit(solution)/shard_map/pack/pallas_call | solution.py:664
  1.6 0.1 collective-permute-start.1
  1.7 2.8 %collective-permute-start = (f32[20,8,128]{2,1,0:T(8,128)S(1)}, f32[20,8,128]{2,1,0:T(8,128)S(1)}, u32[]{:S(2)}, u32[]{:S(2)}) collective-permute-start(f32[20,8,128]{2,1,0:T(8,128)S(1)} %get-tuple-element.28.refs_1_), channel_id=1, source_target_pairs={{0,8},{8,0},{16,24},{24,16},{1,9},{9,1},{17,25},{25,17},{2,10},{10... | collective-permute-start | bytes 245768 | tf_op jit(solution)/shard_map/ppermute | solution.py:18
  4.5 2.8 %source_own.1 = (f32[272,256]{1,0:T(8,128)S(1)}, f32[272,256]{1,0:T(8,128)S(1)}, f32[3,4,32,128]{3,2,1,0:T(8,128)S(1)}, f32[3,4,32,128]{3,2,1,0:T(8,128)S(1)}) custom-call(f32[2,16,128]{2,1,0:T(8,128)S(1)} %get-tuple-element.27.refs_0_, f32[20,8,128]{2,1,0:T(8,128)S(1)} %get-tuple-element.28.refs_1_, f32[3,4,32,128]{3,2,1,0:T(8,128)} %refs_2_.3, ...), custom_call_target="tpu_custom_call" | custom-call | tf_op jit(solution)/shard_map/source_own/pallas_call | solution.py:702
  7.4 0.0 collective-permute-done.refs_1_.refs_2_.refs_5_
  7.4 0.0 collective-permute-done.1.refs_4_.refs_3_.refs_6_
  7.4 3.0 %source_both.1 = (f32[1,4,2,72,128]{4,3,2,1,0:T(8,128)S(1)}, f32[1,4,2,72,128]{4,3,2,1,0:T(8,128)S(1)}) custom-call(f32[2,16,128]{2,1,0:T(8,128)S(1)} %get-tuple-element.27.refs_0_, f32[20,8,128]{2,1,0:T(8,128)S(1)} %collective-permute-done.refs_1_.refs_2_.refs_5_, f32[272,256]{1,0:T(8,128)S(1)} %get-tuple-element.29.refs_2_, ...), custom_call_target="tpu_custom_call" | custom-call | tf_op jit(solution)/shard_map/source_all/source_both/pallas_call | solution.py:713
  10.3 0.6 %collective-permute-start.2 = (f32[1,4,2,72,128]{4,3,2,1,0:T(8,128)S(1)}, f32[1,4,2,72,128]{4,3,2,1,0:T(8,128)S(1)}, u32[]{:S(2)}, u32[]{:S(2)}) collective-permute-start(f32[1,4,2,72,128]{4,3,2,1,0:T(8,128)S(1)} %get-tuple-element.33), channel_id=1, source_target_pairs={{0,1},{1,0},{2,3},{3,2},{4,5},{5,4},{6,7},{7,6},{8,9},{9,8},{10,11... | collective-permute-start | bytes 884744 | tf_op jit(solution)/shard_map/ppermute | solution.py:18
  10.9 0.2 columns.1
  11.2 1.0 %collective-permute-done.2 = f32[1,4,2,72,128]{4,3,2,1,0:T(8,128)S(1)} collective-permute-done((f32[1,4,2,72,128]{4,3,2,1,0:T(8,128)S(1)}, f32[1,4,2,72,128]{4,3,2,1,0:T(8,128)S(1)}, u32[]{:S(2)}, u32[]{:S(2)}) %collective-permute-start.2) | collective-permute-done | bytes 294944 | tf_op jit(solution)/shard_map/ppermute | solution.py:18
  12.2 1.4 %collective-permute-start.3 = (f32[152,128]{1,0:T(8,128)S(1)}, f32[152,128]{1,0:T(8,128)S(1)}, u32[]{:S(2)}, u32[]{:S(2)}) collective-permute-start(f32[152,128]{1,0:T(8,128)S(1)} %get-tuple-element.39), channel_id=1, source_target_pairs={{0,2},{2,0},{4,6},{6,4},{1,3},{3,1},{5,7},{7,5},{8,10},{10,8},{12,... | collective-permute-start | bytes 233480 | tf_op jit(solution)/shard_map/ppermute | solution.py:18
  13.6 1.2 %collective-permute-start.4 = (f32[152,128]{1,0:T(8,128)S(1)}, f32[152,128]{1,0:T(8,128)S(1)}, u32[]{:S(2)}, u32[]{:S(2)}) collective-permute-start(f32[152,128]{1,0:T(8,128)S(1)} %get-tuple-element.40), channel_id=1, source_target_pairs={{0,6},{2,4},{4,2},{6,0},{1,7},{3,5},{5,3},{7,1},{8,14},{10,12},{12... | collective-permute-start | bytes 233480 | tf_op jit(solution)/shard_map/ppermute | solution.py:18
  14.8 0.1 collective-permute-start.5
  14.9 1.7 %pole.1 = (f32[3,4,32,128]{3,2,1,0:T(8,128)}, f32[3,4,32,128]{3,2,1,0:T(8,128)S(1)}, f32[4,32,128]{2,1,0:T(8,128)S(1)}) custom-call(f32[3,4]{1,0:T(4,128)} %table_in.1, f32[3,4,32,128]{3,2,1,0:T(8,128)S(1)} %get-tuple-element.34.refs_0_.e.refs_4_, f32[3,4,32,128]{3,2,1,0:T(8,128)} %pole_in.1, s32[4,32,128]{2,1,0:T(8,128)} %material_in.1, ...), custom_call_target="tpu_custom_call" | custom-call | tf_op jit(solution)/shard_map/pole/pallas_call | solution.py:734
  16.6 3.6 %collective-permute-done.5.refs_3_ = f32[144,128]{1,0:T(8,128)S(1)} collective-permute-done((f32[144,128]{1,0:T(8,128)S(1)}, f32[144,128]{1,0:T(8,128)S(1)}, u32[]{:S(2)}, u32[]{:S(2)}) %collective-permute-start.5) | collective-permute-done | bytes 73760 | tf_op jit(solution)/shard_map/ppermute | solution.py:18
  20.2 0.0 collective-permute-done.3.refs_1_.refs_7_
  20.2 0.0 collective-permute-done.4.refs_2_.refs_8_
  20.2 3.4 %collective-permute-start.6 = (f32[104,128]{1,0:T(8,128)S(1)}, f32[104,128]{1,0:T(8,128)S(1)}, u32[]{:S(2)}, u32[]{:S(2)}) collective-permute-start(f32[104,128]{1,0:T(8,128)S(1)} %get-tuple-element.44), channel_id=1, source_target_pairs={{0,24},{8,16},{16,8},{24,0},{1,25},{9,17},{17,9},{25,1},{2,26},{10... | collective-permute-start | bytes 159752 | tf_op jit(solution)/shard_map/ppermute | solution.py:18
  23.6 1.5 %collective-permute-done.6.refs_9_ = f32[104,128]{1,0:T(8,128)S(1)} collective-permute-done((f32[104,128]{1,0:T(8,128)S(1)}, f32[104,128]{1,0:T(8,128)S(1)}, u32[]{:S(2)}, u32[]{:S(2)}) %collective-permute-start.6) | collective-permute-done | bytes 53280 | tf_op jit(solution)/shard_map/ppermute | solution.py:18
  25.2 1.9 %collective-permute-start.7 = (f32[72,128]{1,0:T(8,128)S(1)}, f32[72,128]{1,0:T(8,128)S(1)}, u32[]{:S(2)}, u32[]{:S(2)}) collective-permute-start(f32[72,128]{1,0:T(8,128)S(1)} %slice_add_fusion.refs_1_), channel_id=1, source_target_pairs={{0,1},{1,0},{2,3},{3,2},{4,5},{5,4},{6,7},{7,6},{8,9},{9,8},{10,11... | collective-permute-start | bytes 110600 | tf_op jit(solution)/shard_map/ppermute | solution.py:18
  27.1 0.6 %fields.1 = (f32[3,4,32,128]{3,2,1,0:T(8,128)S(1)}, f32[3,4,32,128]{3,2,1,0:T(8,128)S(1)}) custom-call(f32[3,4,32,128]{3,2,1,0:T(8,128)S(1)} %get-tuple-element.34.refs_0_.e.refs_4_, f32[3,4,32,128]{3,2,1,0:T(8,128)S(1)} %get-tuple-element.35.refs_1_.refs_5_, f32[3,4,32,128]{3,2,1,0:T(8,128)S(1)} %get-tuple-element.45.refs_2_, ...), custom_call_target="tpu_custom_call" | custom-call | tf_op jit(solution)/shard_map/fields/pallas_call | solution.py:817
  27.6 0.3 %collective-permute-done.7.refs_0_ = f32[72,128]{1,0:T(8,128)S(1)} collective-permute-done((f32[72,128]{1,0:T(8,128)S(1)}, f32[72,128]{1,0:T(8,128)S(1)}, u32[]{:S(2)}, u32[]{:S(2)}) %collective-permute-start.7) | collective-permute-done | bytes 36896 | tf_op jit(solution)/shard_map/ppermute | solution.py:18
  27.9 1.0 %inject.1 = (f32[3,4,32,128]{3,2,1,0:T(8,128)}, f32[3,4,32,128]{3,2,1,0:T(8,128)}) custom-call(f32[72,128]{1,0:T(8,128)S(1)} %collective-permute-done.7.refs_0_, f32[72,128]{1,0:T(8,128)S(1)} %slice_add_fusion.refs_1_, f32[3,4,32,128]{3,2,1,0:T(8,128)S(1)} %get-tuple-element.46.refs_2_, f32[3,4,32,128]{3,2,1,0:T(8,128)S(1)} %get-tuple-element.47.refs_3_, ...), custom_call_target="tpu_custom_call" | custom-call | tf_op jit(solution)/shard_map/inject/pallas_call | solution.py:831
  (3 shorter events, 0.1 us)
Async XLA Ops:
  1.6 5.7 %collective-permute-start.1 = (f32[6,32,128]{2,1,0:T(8,128)S(1)}, f32[6,32,128]{2,1,0:T(8,128)S(1)}, u32[]{:S(2)}, u32[]{:S(2)}) collective-permute-start(f32[6,32,128]{2,1,0:T(8,128)S(1)} %get-tuple-element.31), channel_id=1, source_target_pairs={{0,1},{1,0},{2,3},{3,2},{4,5},{5,4},{6,7},{7,6},{8,9},{9,8},{10,11... | collective-permute-start | bytes 294920 | tf_op jit(solution)/shard_map/ppermute | solution.py:18
  1.7 5.6 %collective-permute-start = (f32[20,8,128]{2,1,0:T(8,128)S(1)}, f32[20,8,128]{2,1,0:T(8,128)S(1)}, u32[]{:S(2)}, u32[]{:S(2)}) collective-permute-start(f32[20,8,128]{2,1,0:T(8,128)S(1)} %get-tuple-element.28.refs_1_), channel_id=1, source_target_pairs={{0,8},{8,0},{16,24},{24,16},{1,9},{9,1},{17,25},{25,17},{2,10},{10... | collective-permute-start | bytes 245768 | tf_op jit(solution)/shard_map/ppermute | solution.py:18
  10.3 1.8 %collective-permute-start.2 = (f32[1,4,2,72,128]{4,3,2,1,0:T(8,128)S(1)}, f32[1,4,2,72,128]{4,3,2,1,0:T(8,128)S(1)}, u32[]{:S(2)}, u32[]{:S(2)}) collective-permute-start(f32[1,4,2,72,128]{4,3,2,1,0:T(8,128)S(1)} %get-tuple-element.33), channel_id=1, source_target_pairs={{0,1},{1,0},{2,3},{3,2},{4,5},{5,4},{6,7},{7,6},{8,9},{9,8},{10,11... | collective-permute-start | bytes 884744 | tf_op jit(solution)/shard_map/ppermute | solution.py:18
  12.2 8.0 %collective-permute-start.3 = (f32[152,128]{1,0:T(8,128)S(1)}, f32[152,128]{1,0:T(8,128)S(1)}, u32[]{:S(2)}, u32[]{:S(2)}) collective-permute-start(f32[152,128]{1,0:T(8,128)S(1)} %get-tuple-element.39), channel_id=1, source_target_pairs={{0,2},{2,0},{4,6},{6,4},{1,3},{3,1},{5,7},{7,5},{8,10},{10,8},{12,... | collective-permute-start | bytes 233480 | tf_op jit(solution)/shard_map/ppermute | solution.py:18
  13.6 6.6 %collective-permute-start.4 = (f32[152,128]{1,0:T(8,128)S(1)}, f32[152,128]{1,0:T(8,128)S(1)}, u32[]{:S(2)}, u32[]{:S(2)}) collective-permute-start(f32[152,128]{1,0:T(8,128)S(1)} %get-tuple-element.40), channel_id=1, source_target_pairs={{0,6},{2,4},{4,2},{6,0},{1,7},{3,5},{5,3},{7,1},{8,14},{10,12},{12... | collective-permute-start | bytes 233480 | tf_op jit(solution)/shard_map/ppermute | solution.py:18
  14.8 5.3 %collective-permute-start.5 = (f32[144,128]{1,0:T(8,128)S(1)}, f32[144,128]{1,0:T(8,128)S(1)}, u32[]{:S(2)}, u32[]{:S(2)}) collective-permute-start(f32[144,128]{1,0:T(8,128)S(1)} %get-tuple-element.41), channel_id=1, source_target_pairs={{0,4},{2,6},{4,0},{6,2},{1,5},{3,7},{5,1},{7,3},{8,12},{10,14},{12... | collective-permute-start | bytes 221192 | tf_op jit(solution)/shard_map/ppermute | solution.py:18
  20.2 4.9 %collective-permute-start.6 = (f32[104,128]{1,0:T(8,128)S(1)}, f32[104,128]{1,0:T(8,128)S(1)}, u32[]{:S(2)}, u32[]{:S(2)}) collective-permute-start(f32[104,128]{1,0:T(8,128)S(1)} %get-tuple-element.44), channel_id=1, source_target_pairs={{0,24},{8,16},{16,8},{24,0},{1,25},{9,17},{17,9},{25,1},{2,26},{10... | collective-permute-start | bytes 159752 | tf_op jit(solution)/shard_map/ppermute | solution.py:18
  25.2 2.8 %collective-permute-start.7 = (f32[72,128]{1,0:T(8,128)S(1)}, f32[72,128]{1,0:T(8,128)S(1)}, u32[]{:S(2)}, u32[]{:S(2)}) collective-permute-start(f32[72,128]{1,0:T(8,128)S(1)} %slice_add_fusion.refs_1_), channel_id=1, source_target_pairs={{0,1},{1,0},{2,3},{3,2},{4,5},{5,4},{6,7},{7,6},{8,9},{9,8},{10,11... | collective-permute-start | bytes 110600 | tf_op jit(solution)/shard_map/ppermute | solution.py:18

commit v7 on v6

--- a/solution.py
+++ b/solution.py
@@ -49,17 +49,51 @@
     return (c - s) * (c + s), 2.0 * (c * s)
 
 
-def rotations(base, powers, rows):
+def tree_levels(rows):
+    levels = 0
+    while 3 ** (levels + 1) * 8 <= rows:
+        levels += 1
+    return levels
+
+
+def turn_table(first, unit, rows):
+    powers = [unit]
+    for _ in range(2):
+        powers.append(doubled(powers[-1]))
+    step = doubled(powers[-1])
+    for level in range(max(1, tree_levels(rows))):
+        powers.append(step)
+        if level < tree_levels(rows):
+            first = cmul(first, step)
+        step = cmul(step, doubled(step))
+    return [first, *powers]
+
+
+def turn_count(rows):
+    return 4 + max(1, tree_levels(rows))
+
+
+def both_ways(value, turn):
+    cc, ss = value[0] * turn[0], value[1] * turn[1]
+    cs, sc = value[0] * turn[1], value[1] * turn[0]
+    return (cc - ss, sc + cs), (cc + ss, sc - cs)
+
+
+def rotations(table, rows):
+    base, powers = table[0], table[1:]
     sub = lax.broadcasted_iota(jnp.int32, (8, base[0].shape[-1]), 0)
     value = tuple(jnp.broadcast_to(part, sub.shape) for part in base)
     for k in range(3):
         picked = (sub & (1 << k)) != 0
         value = cmul(value, (jnp.where(picked, powers[k][0], 1.0), jnp.where(picked, powers[k][1], 0.0)))
     blocks = [value]
-    k = 3
+    last = 0
+    for level in range(tree_levels(rows)):
+        last = level
+        pairs = [both_ways(block, powers[3 + level]) for block in blocks]
+        blocks = [pair[1] for pair in pairs] + blocks + [pair[0] for pair in pairs]
     while len(blocks) * 8 < rows:
-        blocks = blocks + [cmul(block, powers[k]) for block in blocks]
-        k += 1
+        blocks.append(cmul(blocks[len(blocks) - 3**last], powers[3 + last]))
     return tuple(jnp.concatenate([block[i] for block in blocks], axis=0)[:rows] for i in (0, 1))
 
 
@@ -74,8 +108,6 @@
 
 def source_kernel(freqs, depth, wx, half, sizes, zslots, xslots, scale, zbits, closing):
     sx, sy, sz = sizes
-    xbits = max(3, (wx - 1).bit_length())
-    ybits = max(3, (half - 1).bit_length())
     per = 4 // zslots
     main = 4 * xslots * wx
 
@@ -83,9 +115,9 @@
         waves, packed = refs[:2]
         if closing:
             old_even, old_odd = refs[2:4]
-            keep, send, xbase, xpow, ypow, acc_even, acc_odd = refs[4 + zbits :]
+            keep, send, xback, xturn, yturn, acc_even, acc_odd = refs[4 + zbits :]
         else:
-            e_in, h_in, acc_even, acc_odd, e_near, h_near, xbase, xpow, ypow, sems = refs[2:]
+            e_in, h_in, acc_even, acc_odd, e_near, h_near, xback, xturn, yturn, sems = refs[2:]
             copies = [
                 pltpu.make_async_copy(source, target, sems.at[i])
                 for i, (source, target) in enumerate(((e_in, e_near), (h_in, h_near)))
@@ -109,18 +141,16 @@
         along_x = wave * packed[freqs, 0:1, :]
         along_y = wave * packed[freqs, 1:2, :]
         origin = along_y * center - phase
+        unit = doubled(small_turn(0.5 * along_x))
         for xr in range(xslots):
             angle = along_x * starts[xr] + origin
-            xbase[xr, 0] = jnp.cos(angle)
-            xbase[xr, 1] = jnp.sin(angle)
-        turn = doubled(small_turn(0.5 * along_x))
-        for k in range(xbits):
-            xpow[k, 0], xpow[k, 1] = turn
-            turn = doubled(turn)
-        turn = small_turn(0.5 * along_y)
-        for k in range(ybits + 1):
-            ypow[k, 0], ypow[k, 1] = turn
-            turn = doubled(turn)
+            first = jnp.cos(angle), jnp.sin(angle)
+            xback[xr, 0], xback[xr, 1] = cmul(first, (unit[0], -unit[1]))
+            for k, turn in enumerate(turn_table(first, unit, wx)):
+                xturn[xr, k, 0], xturn[xr, k, 1] = turn
+        first = small_turn(0.5 * along_y)
+        for k, turn in enumerate(turn_table(first, doubled(first), half)):
+            yturn[k, 0], yturn[k, 1] = turn
         if closing:
             acc_even[...] = old_even[...]
             acc_odd[...] = old_odd[...]
@@ -136,13 +166,13 @@
                 def row(ref, *where):
                     return tuple(ref[(*where, i, pl.ds(f, 1), slice(None))] for i in (0, 1))
 
-                powers = [row(ypow, k) for k in range(ybits + 1)]
-                cy, sy_ = rotations(powers[0], powers[1:], half)
+                cy, sy_ = rotations([row(yturn, k) for k in range(turn_count(half))], half)
                 coses.append(cy)
                 sines.append(sy_)
-                powers = [row(xpow, k) for k in range(xbits)]
-                bases = [row(xbase, xr) for xr in range(xslots)]
-                turns = [rotations(base, powers, wx) for base in bases]
+                turns = [
+                    rotations([row(xturn, xr, k) for k in range(turn_count(wx))], wx)
+                    for xr in range(xslots)
+                ]
                 first, second = [], []
                 for zr in range(zslots):
                     for xr in range(xslots):
@@ -153,14 +183,13 @@
                             q = packed[f, pl.ds(at + 1, 1), :]
                             first.append(p * cx - q * sx_)
                             second.append(p * sx_ + q * cx)
-                back = (powers[0][0], -powers[0][1])
                 p = packed[f, 6:7, :]
                 q = packed[f, 7:8, :]
                 line = lax.broadcasted_iota(jnp.int32, (16, p.shape[-1]), 0)
                 one_first = jnp.zeros(line.shape, jnp.float32)
                 one_second = one_first
                 for xr in range(xslots):
-                    cx, sx_ = cmul(bases[xr], back)
+                    cx, sx_ = row(xback, xr)
                     one_first = jnp.where(line == xr, p * cx - q * sx_, one_first)
                     one_second = jnp.where(line == xr, p * sx_ + q * cx, one_second)
                 firsts.append(jnp.concatenate(first + [one_first], axis=0))
@@ -193,16 +222,16 @@
         def place(zr):
             return (keep, zr) if zr < zslots // 2 else (send, zr - zslots // 2)
 
-        extra = per * wx
+        extra = xslots * per * wx
         for zr in range(zslots):
             ref, z = place(zr)
             for y in range(sy):
-                for xr in range(xslots):
-                    ref[z, y, xr, extra : extra + 8] = jnp.zeros((8, LANES), jnp.float32)
+                ref[z, y, extra : extra + 8] = jnp.zeros((8, LANES), jnp.float32)
         at_z = (1 - (iz & 1)) * (depth - 1)
         for i in range(6):
             row = i * depth
-            send[0, 0, 0, extra + 2 + i : extra + 3 + i] = packed[
+            spot = extra + 4 + i % 4
+            send[0, i // 4, spot : spot + 1] = packed[
                 freqs + 1 + row // 8, pl.ds(row % 8 + at_z, 1), :
             ]
         turned = 2 // per
@@ -219,29 +248,31 @@
                         rows = slice(at * wx, (at + 1) * wx)
                         even = acc_even[rows, lanes] * scale
                         odd = acc_odd[rows, lanes] * scale
-                        ref[z, up, xr, c2 * wx : (c2 + 1) * wx] = even - odd
-                        ref[z, down, xr, c2 * wx : (c2 + 1) * wx] = even + odd
+                        into = slice((xr * per + c2) * wx, (xr * per + c2 + 1) * wx)
+                        ref[z, up, into] = even - odd
+                        ref[z, down, into] = even + odd
                         at += 1
             for xr in range(xslots):
                 even = acc_even[main + xr : main + xr + 1, lanes] * scale
                 odd = acc_odd[main + xr : main + xr + 1, lanes] * scale
                 for zr in range(zslots):
                     ref, z = place(zr)
-                    ref[z, up, xr, extra : extra + 1] = even - odd
-                    ref[z, down, xr, extra : extra + 1] = even + odd
+                    ref[z, up, extra + 2 * xr : extra + 2 * xr + 1] = even - odd
+                    ref[z, down, extra + 2 * xr : extra + 2 * xr + 1] = even + odd
                 start = (((zcode ^ turned) * xslots + xr) * per + spare) * wx
                 rows = pl.ds(pl.multiple_of(start, wx), wx)
                 even = (acc_even[rows, lanes] * scale).T
                 odd = (acc_odd[rows, lanes] * scale).T
                 lower = slot(sy // 2 - j)
+                line = slice(extra + 2 * xr + 1, extra + 2 * xr + 2)
                 for zr in range(zslots):
                     ref, z = place(zr)
-                    ref[z, lower, xr, extra + 1 : extra + 2, 0:wx] = even[0:1] + odd[0:1]
+                    ref[z, lower, line, 0:wx] = even[0:1] + odd[0:1]
                 if j < sy // 2 - 1:
                     upper = slot(sy // 2 + j + 1)
                     for zr in range(zslots):
                         ref, z = place(zr)
-                        ref[z, upper, xr, extra + 1 : extra + 2, 0:wx] = even[LANES - 1 :] - odd[LANES - 1 :]
+                        ref[z, upper, line, 0:wx] = even[LANES - 1 :] - odd[LANES - 1 :]
 
     return body
 
@@ -369,16 +400,20 @@
     return ref[rows - 8 : rows]
 
 
-def merge_x_kernel(count, rows, depth, wx, wy, zbits, ybits, k):
+def merge_x_kernel(count, rows, depth, wx, zbits, ybits, slots, k):
     def body(*refs):
         terms = refs[:count]
         e, h = refs[count : count + 2]
         zs = refs[count + 2 : count + 2 + zbits]
         ys = refs[count + 2 + zbits : count + 2 + zbits + ybits]
         keep, out = refs[count + 3 + zbits + ybits :]
-        size = rows // 2
-        keep[...] = total_of(terms, slice(0, size))
-        out[0:size] = total_of(terms, slice(size, rows))
+        half = (rows - 8) // 2
+        size = half + 8
+        keep[0:half] = total_of(terms, slice(0, half))
+        out[0:half] = total_of(terms, slice(half, rows - 8))
+        extra = total_of(terms, slice(rows - 8, rows))
+        keep[half:size] = extra
+        out[half:size] = pltpu.roll(extra, 8 - slots, 0)
         zlow, zhigh = near_flags(lax.axis_index("gz"), zbits)
         ylow, yhigh = near_flags(lax.axis_index("gy"), ybits)
         at = (1 - ((lax.axis_index("gx") >> k) & 1)) * (wx - 1)
@@ -386,15 +421,15 @@
             for z in range(depth):
                 row = size + i * depth + z
                 out[row : row + 1] = e[i, z, pl.ds(at, 1), :]
-                row = size + (3 + i) * depth + z
-                out[row : row + 1] = h[i, z, pl.ds(at, 1), :]
-        base = size + 6 * depth
+                if i > 0:
+                    row = size + (2 + i) * depth + z
+                    out[row : row + 1] = h[i, z, pl.ds(at, 1), :]
+        base = size + 5 * depth
         halos = [halo_at(y) for y in ys]
         out[base : base + 1] = weighted(zhigh, [z[0, pl.ds(at, 1), :] for z in zs])
         out[base + 1 : base + 2] = weighted(zlow, [z[2, pl.ds(at, 1), :] for z in zs])
         out[base + 2 : base + 3] = weighted(yhigh, [y[0:1] for y in halos])
         out[base + 3 : base + 4] = weighted(ylow, [y[1:2] for y in halos])
-        out[base + 4 : base + 8] = jnp.zeros((4, LANES), jnp.float32)
 
     return body
 
@@ -435,12 +470,12 @@
     return body
 
 
-def field_kernel(freqs, depth, wx, wy, xbits, ybits, zbits, side_row):
+def field_kernel(freqs, depth, wx, wy, xbits, ybits, zbits, side_rows):
     def body(*refs):
         e, h, base_e, coef_ref, first, message = refs[:6]
         zs = refs[6 : 6 + zbits]
         ys = refs[6 + zbits : 6 + zbits + ybits]
-        xs = [x[x.shape[0] - 6 * depth - 8 :] for x in refs[6 + zbits + ybits : 5 + zbits + ybits + xbits]]
+        xs = [x[x.shape[0] - 5 * depth - 4 :] for x in refs[6 + zbits + ybits : 5 + zbits + ybits + xbits]]
         sides = refs[5 + zbits + ybits + xbits : 5 + 2 * zbits + ybits + xbits]
         e_out, h_out = refs[5 + 2 * zbits + ybits + xbits :]
         ix, iy, iz = (lax.axis_index(name) for name in ("gx", "gy", "gz"))
@@ -448,7 +483,7 @@
         ylow, yhigh = near_flags(iy, ybits)
         zlow, zhigh = near_flags(iz, zbits)
         size = depth * wx
-        base = 6 * depth
+        base = 5 * depth
         lane = lax.broadcasted_iota(jnp.int32, (size, wy), 1)
         line = lax.broadcasted_iota(jnp.int32, (size, wy), 0) & (wx - 1)
         inside_x, inside_y, inside_z = (
@@ -488,7 +523,8 @@
         above = yhi.T
 
         def rows_of(flags, i):
-            at = slice(i * depth, (i + 1) * depth)
+            line = i if i < 3 else i - 1
+            at = slice(line * depth, (line + 1) * depth)
             return weighted(flags, [early_rows(message, freqs, depth, i)] + [x[at] for x in xs])
 
         def extra_of(flags, early, i):
@@ -498,8 +534,8 @@
             return weighted(flags, [z[i, 0:wx] for z in zs])
 
         def side_of(flags, i):
-            at = side_row + i
-            return weighted(flags, [side[at : at + 1] for side in sides])
+            ats = [rows[i] for rows in side_rows]
+            return weighted(flags, [side[at : at + 1] for at, side in zip(ats, sides)])
 
         up_x, up_y = layer_of(zhigh, 0), layer_of(zhigh, 1)
         hx = oldx - courant * ((next_y(ez, above[:, 2:3]) - ez) - (next_z(ey, up_y) - ey))
@@ -644,7 +680,7 @@
     ix, iy, iz = (lax.axis_index(name) for name in ("gx", "gy", "gz"))
     freqs, _, count = cotangent.shape
     scale = 1.0 / math.sqrt(freqs * count * sx * sy * sz)
-    assert wy == LANES and depth * wx == LANES and sx > 1 and sy > 1 and sz > 1
+    assert wy == LANES and depth * wx == LANES and 1 < sx <= 4 and sy > 1 and sz > 1
     pad = -count % LANES
     if pad:
         cotangent = jnp.pad(cotangent, ((0, 0), (0, 0), (0, pad)))
@@ -685,17 +721,15 @@
     zs = in_vmem(*zs)
 
     half = sy * wy // 2
-    xlevels = max(3, (wx - 1).bit_length())
-    ylevels = max(3, (half - 1).bit_length()) + 1
     width = count + pad
-    block = per * wx + 8
-    part_shape = pltpu.VMEM((zslots // 2, sy, xslots, block, wy), f32)
+    block = xslots * per * wx + 8
+    part_shape = pltpu.VMEM((zslots // 2, sy, block, wy), f32)
     assert freqs % 2 == 0
     sums = pltpu.VMEM((4 * xslots * wx + 16, half), f32)
     tables = [
         pltpu.VMEM((xslots, 2, freqs, width), f32),
-        pltpu.VMEM((xlevels, 2, freqs, width), f32),
-        pltpu.VMEM((ylevels, 2, freqs, width), f32),
+        pltpu.VMEM((xslots, turn_count(wx), 2, freqs, width), f32),
+        pltpu.VMEM((turn_count(half), 2, freqs, width), f32),
     ]
     medium = pltpu.CompilerParams(vmem_limit_bytes=24 << 20)
     waves, mine = in_vmem(waves, mine)
@@ -753,11 +787,13 @@
 
     terms = [keep, exchange(send, "gz", 1)]
     sides = [flat(terms[1])]
+    side_rows = [[(i // 4) * block + block - 4 + i % 4 for i in range(6)]]
     for k in range(1, zbits):
         at = (1 - ((iz >> k) & 1)) * (depth - 1)
         rows = theirs[freqs + 1 :].reshape(6, depth, LANES)
         rows = lax.dynamic_index_in_dim(rows, at, 1, keepdims=False)
-        sides.append(exchange(jnp.pad(rows, ((per * wx + 2, 0), (0, 0))), "gz", (2 << k) - 1))
+        sides.append(exchange(jnp.pad(rows, ((0, 2), (0, 0))), "gz", (2 << k) - 1))
+        side_rows.append(list(range(6)))
     for k in range(1, zbits):
         part = terms[0] + terms[1]
         mask = (2 << k) - 1
@@ -767,7 +803,7 @@
         else:
             terms = [part, exchange(part, "gz", mask)]
     terms = [flat(term) for term in terms]
-    rows = sy * xslots * block
+    rows = sy * block
 
     ys = [None] * ybits
     k = 0
@@ -797,12 +833,14 @@
         rows = size
     near = [*zs, *in_vmem(*ys)]
     xs = []
+    slots = xslots
     for k in range(1, xbits):
+        size = (rows - 8) // 2 + 8
         keep, away = pl.pallas_call(
-            merge_x_kernel(len(terms), rows, depth, wx, wy, zbits, ybits, k),
+            merge_x_kernel(len(terms), rows, depth, wx, zbits, ybits, slots, k),
             out_shape=(
-                pltpu.VMEM((rows // 2, LANES), f32),
-                pltpu.VMEM((rows // 2 + 6 * depth + 8, LANES), f32),
+                pltpu.VMEM((size, LANES), f32),
+                pltpu.VMEM((size + 5 * depth + 4, LANES), f32),
             ),
             in_specs=[vmem] * (len(terms) + 3 + zbits + ybits),
             out_specs=(vmem, vmem),
@@ -810,12 +848,13 @@
             name="merge_x",
         )(*in_vmem(*terms), e_near, h_near, *near, coef)
         xs.append(exchange(away, "gx", (2 << k) - 1))
-        rows //= 2
+        rows = size
+        slots //= 2
         terms = [keep, xs[-1]]
     part = sum(term[:rows] for term in terms)
 
     e_most, h_most = pl.pallas_call(
-        field_kernel(freqs, depth, wx, wy, xbits, ybits, zbits, per * wx + 2),
+        field_kernel(freqs, depth, wx, wy, xbits, ybits, zbits, side_rows),
         out_shape=(pltpu.VMEM(whole.shape, f32), pltpu.VMEM(whole.shape, f32)),
         in_specs=[vmem] * (5 + xbits + ybits + 2 * zbits),
         out_specs=(vmem,) * 2,

time: 29.2 us -> 28.7 us (0.983)
  Pallas kernels: 10.4 us -> 9.94 us
    pallas_call x2, Pallas kernels: 5.8 us -> 5.32 us  [local(): pl.pallas_call(source_kernel(freqs, depth, wx, half, sizes, zslots, xslot...]
  transfers between devices with their start and end apart: 8 -> 8, of which waited for: 4 -> 5; matrix products, arithmetic and copies ran while one was open for 0% -> 0% of each run, Pallas kernels for 19% -> 18%
where the time goes in v7:
time: 28.7 us; the launch traced here: 28.5 us
  starting transfers between devices  11.6 us (40%)
  Pallas kernels  9.94 us (35%)
  waiting for transfers between devices  6.27 us (22%)
  between operations  0.69 us (2%)
    ppermute x8, starting transfers between devices, exchange(): lax.ppermute(array, axis, [(i, i ^ mask) for i in range(lax.axis_size(axi...  11.6 us
    ppermute x8, waiting for transfers between devices, exchange(): lax.ppermute(array, axis, [(i, i ^ mask) for i in range(lax.axis_size(axi...  6.27 us
    pallas_call x2, Pallas kernels, local(): pl.pallas_call(source_kernel(freqs, depth, wx, half, sizes, zslots, xslot...  5.32 us
    pallas_call x1, Pallas kernels, local(): pl.pallas_call(pole_kernel(depth, wx, wy), out_shape=(whole, pltpu.VMEM(w...  1.72 us
    pallas_call x1, Pallas kernels, local(): pl.pallas_call(inject_kernel(depth, wx, wy, sy, sz, per, zcut), out_shape...  1.02 us
    pallas_call x1, Pallas kernels, local(): pl.pallas_call(pack_kernel(freqs, depth, wx, zbits), out_shape=[pltpu.VME...  1.01 us
  transfers between devices with their start and end apart: 8, of which 5 were waited for; matrix products, arithmetic and copies ran while one was open for 0% of the time, Pallas kernels for 18%

profile of v7, /device:TPU:1, one launch (start us, length us, event | category | flops | bytes accessed | tf_op | source)
XLA Modules:
  0.0 28.5 jit_solution(15443041616414803480)
XLA Ops:
  0.6 1.0 %pack.1 = (f32[20,8,128]{2,1,0:T(8,128)S(1)}, f32[2,16,128]{2,1,0:T(8,128)S(1)}, f32[6,32,128]{2,1,0:T(8,128)S(1)}) custom-call(f32[3,4,32,128]{3,2,1,0:T(8,128)} %refs_2_.3, f32[3,4,32,128]{3,2,1,0:T(8,128)} %refs_3_.3, f32[16,8,128]{2,1,0:T(8,128)} %refs_2_.2, f32[2,128]{1,0:T(2,128)} %refs_3_.2, f32[16]{0:T(128)} %refs_4_.1, f32[16]{0:T(128)} %refs_5_.1), custom_call_target="tpu_custom_call" | custom-call | tf_op jit(solution)/shard_map/pack/pallas_call | solution.py:700
  1.6 0.1 collective-permute-start.1
  1.7 2.8 %collective-permute-start = (f32[20,8,128]{2,1,0:T(8,128)S(1)}, f32[20,8,128]{2,1,0:T(8,128)S(1)}, u32[]{:S(2)}, u32[]{:S(2)}) collective-permute-start(f32[20,8,128]{2,1,0:T(8,128)S(1)} %get-tuple-element.28.refs_1_), channel_id=1, source_target_pairs={{0,8},{8,0},{16,24},{24,16},{1,9},{9,1},{17,25},{25,17},{2,10},{10... | collective-permute-start | bytes 245768 | tf_op jit(solution)/shard_map/ppermute | solution.py:18
  4.5 2.6 %source_own.1 = (f32[272,256]{1,0:T(8,128)S(1)}, f32[272,256]{1,0:T(8,128)S(1)}, f32[3,4,32,128]{3,2,1,0:T(8,128)S(1)}, f32[3,4,32,128]{3,2,1,0:T(8,128)S(1)}) custom-call(f32[2,16,128]{2,1,0:T(8,128)S(1)} %get-tuple-element.27.refs_0_, f32[20,8,128]{2,1,0:T(8,128)S(1)} %get-tuple-element.28.refs_1_, f32[3,4,32,128]{3,2,1,0:T(8,128)} %refs_2_.3, ...), custom_call_target="tpu_custom_call" | custom-call | tf_op jit(solution)/shard_map/source_own/pallas_call | solution.py:736
  7.1 0.1 collective-permute-done.refs_1_.refs_2_.refs_5_
  7.2 0.0 collective-permute-done.1.refs_4_.refs_3_.refs_6_
  7.2 2.7 %source_both.1 = (f32[1,4,136,128]{3,2,1,0:T(8,128)S(1)}, f32[1,4,136,128]{3,2,1,0:T(8,128)S(1)}) custom-call(f32[2,16,128]{2,1,0:T(8,128)S(1)} %get-tuple-element.27.refs_0_, f32[20,8,128]{2,1,0:T(8,128)S(1)} %collective-permute-done.refs_1_.refs_2_.refs_5_, f32[272,256]{1,0:T(8,128)S(1)} %get-tuple-element.29.refs_2_, ...), custom_call_target="tpu_custom_call" | custom-call | tf_op jit(solution)/shard_map/source_all/source_both/pallas_call | solution.py:747
  10.0 0.7 %collective-permute-start.2 = (f32[1,4,136,128]{3,2,1,0:T(8,128)S(1)}, f32[1,4,136,128]{3,2,1,0:T(8,128)S(1)}, u32[]{:S(2)}, u32[]{:S(2)}) collective-permute-start(f32[1,4,136,128]{3,2,1,0:T(8,128)S(1)} %get-tuple-element.33), channel_id=1, source_target_pairs={{0,1},{1,0},{2,3},{3,2},{4,5},{5,4},{6,7},{7,6},{8,9},{9,8},{10,11... | collective-permute-start | bytes 835592 | tf_op jit(solution)/shard_map/ppermute | solution.py:18
  10.7 0.2 columns.1
  10.9 0.9 %collective-permute-done.2 = f32[1,4,136,128]{3,2,1,0:T(8,128)S(1)} collective-permute-done((f32[1,4,136,128]{3,2,1,0:T(8,128)S(1)}, f32[1,4,136,128]{3,2,1,0:T(8,128)S(1)}, u32[]{:S(2)}, u32[]{:S(2)}) %collective-permute-start.2) | collective-permute-done | bytes 278560 | tf_op jit(solution)/shard_map/ppermute | solution.py:18
  11.9 1.4 %collective-permute-start.3 = (f32[144,128]{1,0:T(8,128)S(1)}, f32[144,128]{1,0:T(8,128)S(1)}, u32[]{:S(2)}, u32[]{:S(2)}) collective-permute-start(f32[144,128]{1,0:T(8,128)S(1)} %get-tuple-element.39), channel_id=1, source_target_pairs={{0,2},{2,0},{4,6},{6,4},{1,3},{3,1},{5,7},{7,5},{8,10},{10,8},{12,... | collective-permute-start | bytes 221192 | tf_op jit(solution)/shard_map/ppermute | solution.py:18
  13.3 1.2 %collective-permute-start.4 = (f32[144,128]{1,0:T(8,128)S(1)}, f32[144,128]{1,0:T(8,128)S(1)}, u32[]{:S(2)}, u32[]{:S(2)}) collective-permute-start(f32[144,128]{1,0:T(8,128)S(1)} %get-tuple-element.40), channel_id=1, source_target_pairs={{0,6},{2,4},{4,2},{6,0},{1,7},{3,5},{5,3},{7,1},{8,14},{10,12},{12... | collective-permute-start | bytes 221192 | tf_op jit(solution)/shard_map/ppermute | solution.py:18
  14.6 0.1 collective-permute-start.5
  14.6 1.7 %pole.1 = (f32[3,4,32,128]{3,2,1,0:T(8,128)}, f32[3,4,32,128]{3,2,1,0:T(8,128)S(1)}, f32[4,32,128]{2,1,0:T(8,128)S(1)}) custom-call(f32[3,4]{1,0:T(4,128)} %table_in.1, f32[3,4,32,128]{3,2,1,0:T(8,128)S(1)} %get-tuple-element.34.refs_0_.e.refs_4_, f32[3,4,32,128]{3,2,1,0:T(8,128)} %pole_in.1, s32[4,32,128]{2,1,0:T(8,128)} %material_in.1, ...), custom_call_target="tpu_custom_call" | custom-call | tf_op jit(solution)/shard_map/pole/pallas_call | solution.py:768
  16.4 3.4 %collective-permute-done.5.refs_3_ = f32[136,128]{1,0:T(8,128)S(1)} collective-permute-done((f32[136,128]{1,0:T(8,128)S(1)}, f32[136,128]{1,0:T(8,128)S(1)}, u32[]{:S(2)}, u32[]{:S(2)}) %collective-permute-start.5) | collective-permute-done | bytes 69664 | tf_op jit(solution)/shard_map/ppermute | solution.py:18
  19.8 0.0 collective-permute-done.3.refs_1_.refs_7_
  19.8 0.0 collective-permute-done.4.refs_2_.refs_8_
  19.8 3.4 %collective-permute-start.6 = (f32[96,128]{1,0:T(8,128)S(1)}, f32[96,128]{1,0:T(8,128)S(1)}, u32[]{:S(2)}, u32[]{:S(2)}) collective-permute-start(f32[96,128]{1,0:T(8,128)S(1)} %get-tuple-element.44), channel_id=1, source_target_pairs={{0,24},{8,16},{16,8},{24,0},{1,25},{9,17},{17,9},{25,1},{2,26},{10... | collective-permute-start | bytes 147464 | tf_op jit(solution)/shard_map/ppermute | solution.py:18
  23.2 1.5 %collective-permute-done.6.refs_9_ = f32[96,128]{1,0:T(8,128)S(1)} collective-permute-done((f32[96,128]{1,0:T(8,128)S(1)}, f32[96,128]{1,0:T(8,128)S(1)}, u32[]{:S(2)}, u32[]{:S(2)}) %collective-permute-start.6) | collective-permute-done | bytes 49184 | tf_op jit(solution)/shard_map/ppermute | solution.py:18
  24.7 1.9 %collective-permute-start.7 = (f32[72,128]{1,0:T(8,128)S(1)}, f32[72,128]{1,0:T(8,128)S(1)}, u32[]{:S(2)}, u32[]{:S(2)}) collective-permute-start(f32[72,128]{1,0:T(8,128)S(1)} %slice_add_fusion.refs_1_), channel_id=1, source_target_pairs={{0,1},{1,0},{2,3},{3,2},{4,5},{5,4},{6,7},{7,6},{8,9},{9,8},{10,11... | collective-permute-start | bytes 110600 | tf_op jit(solution)/shard_map/ppermute | solution.py:18
  26.6 0.6 %fields.1 = (f32[3,4,32,128]{3,2,1,0:T(8,128)S(1)}, f32[3,4,32,128]{3,2,1,0:T(8,128)S(1)}) custom-call(f32[3,4,32,128]{3,2,1,0:T(8,128)S(1)} %get-tuple-element.34.refs_0_.e.refs_4_, f32[3,4,32,128]{3,2,1,0:T(8,128)S(1)} %get-tuple-element.35.refs_1_.refs_5_, f32[3,4,32,128]{3,2,1,0:T(8,128)S(1)} %get-tuple-element.45.refs_2_, ...), custom_call_target="tpu_custom_call" | custom-call | tf_op jit(solution)/shard_map/fields/pallas_call | solution.py:856
  27.2 0.3 %collective-permute-done.7.refs_0_ = f32[72,128]{1,0:T(8,128)S(1)} collective-permute-done((f32[72,128]{1,0:T(8,128)S(1)}, f32[72,128]{1,0:T(8,128)S(1)}, u32[]{:S(2)}, u32[]{:S(2)}) %collective-permute-start.7) | collective-permute-done | bytes 36896 | tf_op jit(solution)/shard_map/ppermute | solution.py:18
  27.5 1.0 %inject.1 = (f32[3,4,32,128]{3,2,1,0:T(8,128)}, f32[3,4,32,128]{3,2,1,0:T(8,128)}) custom-call(f32[72,128]{1,0:T(8,128)S(1)} %collective-permute-done.7.refs_0_, f32[72,128]{1,0:T(8,128)S(1)} %slice_add_fusion.refs_1_, f32[3,4,32,128]{3,2,1,0:T(8,128)S(1)} %get-tuple-element.46.refs_2_, f32[3,4,32,128]{3,2,1,0:T(8,128)S(1)} %get-tuple-element.47.refs_3_, ...), custom_call_target="tpu_custom_call" | custom-call | tf_op jit(solution)/shard_map/inject/pallas_call | solution.py:870
  (3 shorter events, 0.1 us)
Async XLA Ops:
  1.6 5.6 %collective-permute-start.1 = (f32[6,32,128]{2,1,0:T(8,128)S(1)}, f32[6,32,128]{2,1,0:T(8,128)S(1)}, u32[]{:S(2)}, u32[]{:S(2)}) collective-permute-start(f32[6,32,128]{2,1,0:T(8,128)S(1)} %get-tuple-element.31), channel_id=1, source_target_pairs={{0,1},{1,0},{2,3},{3,2},{4,5},{5,4},{6,7},{7,6},{8,9},{9,8},{10,11... | collective-permute-start | bytes 294920 | tf_op jit(solution)/shard_map/ppermute | solution.py:18
  1.7 5.5 %collective-permute-start = (f32[20,8,128]{2,1,0:T(8,128)S(1)}, f32[20,8,128]{2,1,0:T(8,128)S(1)}, u32[]{:S(2)}, u32[]{:S(2)}) collective-permute-start(f32[20,8,128]{2,1,0:T(8,128)S(1)} %get-tuple-element.28.refs_1_), channel_id=1, source_target_pairs={{0,8},{8,0},{16,24},{24,16},{1,9},{9,1},{17,25},{25,17},{2,10},{10... | collective-permute-start | bytes 245768 | tf_op jit(solution)/shard_map/ppermute | solution.py:18
  10.0 1.9 %collective-permute-start.2 = (f32[1,4,136,128]{3,2,1,0:T(8,128)S(1)}, f32[1,4,136,128]{3,2,1,0:T(8,128)S(1)}, u32[]{:S(2)}, u32[]{:S(2)}) collective-permute-start(f32[1,4,136,128]{3,2,1,0:T(8,128)S(1)} %get-tuple-element.33), channel_id=1, source_target_pairs={{0,1},{1,0},{2,3},{3,2},{4,5},{5,4},{6,7},{7,6},{8,9},{9,8},{10,11... | collective-permute-start | bytes 835592 | tf_op jit(solution)/shard_map/ppermute | solution.py:18
  11.9 7.9 %collective-permute-start.3 = (f32[144,128]{1,0:T(8,128)S(1)}, f32[144,128]{1,0:T(8,128)S(1)}, u32[]{:S(2)}, u32[]{:S(2)}) collective-permute-start(f32[144,128]{1,0:T(8,128)S(1)} %get-tuple-element.39), channel_id=1, source_target_pairs={{0,2},{2,0},{4,6},{6,4},{1,3},{3,1},{5,7},{7,5},{8,10},{10,8},{12,... | collective-permute-start | bytes 221192 | tf_op jit(solution)/shard_map/ppermute | solution.py:18
  13.3 6.4 %collective-permute-start.4 = (f32[144,128]{1,0:T(8,128)S(1)}, f32[144,128]{1,0:T(8,128)S(1)}, u32[]{:S(2)}, u32[]{:S(2)}) collective-permute-start(f32[144,128]{1,0:T(8,128)S(1)} %get-tuple-element.40), channel_id=1, source_target_pairs={{0,6},{2,4},{4,2},{6,0},{1,7},{3,5},{5,3},{7,1},{8,14},{10,12},{12... | collective-permute-start | bytes 221192 | tf_op jit(solution)/shard_map/ppermute | solution.py:18
  14.6 5.2 %collective-permute-start.5 = (f32[136,128]{1,0:T(8,128)S(1)}, f32[136,128]{1,0:T(8,128)S(1)}, u32[]{:S(2)}, u32[]{:S(2)}) collective-permute-start(f32[136,128]{1,0:T(8,128)S(1)} %get-tuple-element.41), channel_id=1, source_target_pairs={{0,4},{2,6},{4,0},{6,2},{1,5},{3,7},{5,1},{7,3},{8,12},{10,14},{12... | collective-permute-start | bytes 208904 | tf_op jit(solution)/shard_map/ppermute | solution.py:18
  19.8 4.9 %collective-permute-start.6 = (f32[96,128]{1,0:T(8,128)S(1)}, f32[96,128]{1,0:T(8,128)S(1)}, u32[]{:S(2)}, u32[]{:S(2)}) collective-permute-start(f32[96,128]{1,0:T(8,128)S(1)} %get-tuple-element.44), channel_id=1, source_target_pairs={{0,24},{8,16},{16,8},{24,0},{1,25},{9,17},{17,9},{25,1},{2,26},{10... | collective-permute-start | bytes 147464 | tf_op jit(solution)/shard_map/ppermute | solution.py:18
  24.7 2.8 %collective-permute-start.7 = (f32[72,128]{1,0:T(8,128)S(1)}, f32[72,128]{1,0:T(8,128)S(1)}, u32[]{:S(2)}, u32[]{:S(2)}) collective-permute-start(f32[72,128]{1,0:T(8,128)S(1)} %slice_add_fusion.refs_1_), channel_id=1, source_target_pairs={{0,1},{1,0},{2,3},{3,2},{4,5},{5,4},{6,7},{7,6},{8,9},{9,8},{10,11... | collective-permute-start | bytes 110600 | tf_op jit(solution)/shard_map/ppermute | solution.py:18

commit v8 on v7

--- a/solution.py
+++ b/solution.py
@@ -6,6 +6,7 @@
 from jax.experimental import pallas as pl
 from jax.experimental.pallas import tpu as pltpu
 from jax.sharding import PartitionSpec as P
+
 
 NPOLE = 4
 LANES = 128
@@ -107,7 +108,7 @@
 
 
 def source_kernel(freqs, depth, wx, half, sizes, zslots, xslots, scale, zbits, closing):
-    sx, sy, sz = sizes
+    sx, sy, _ = sizes
     per = 4 // zslots
     main = 4 * xslots * wx
 
@@ -380,7 +381,7 @@
     return value
 
 
-def merge_y_kernel(count, rows, k, ybits):
+def merge_y_kernel(count, rows, k):
     def body(*refs):
         terms, (first, last), outs = refs[:count], refs[count : count + 2], refs[count + 2 :]
         iy = lax.axis_index("gy")
@@ -434,7 +435,7 @@
     return body
 
 
-def pole_kernel(depth, wx, wy):
+def pole_kernel():
     def body(table_in, e, pole_in, material_in, after, pole_out, base, coef_out, *scratch):
         table, pole, material, new_pole, sems = scratch
         copies = [
@@ -677,7 +678,7 @@
 ):
     depth, wx, wy = material.shape
     sizes = sx, sy, sz = tuple(lax.axis_size(name) for name in ("gx", "gy", "gz"))
-    ix, iy, iz = (lax.axis_index(name) for name in ("gx", "gy", "gz"))
+    _, _, iz = (lax.axis_index(name) for name in ("gx", "gy", "gz"))
     freqs, _, count = cotangent.shape
     scale = 1.0 / math.sqrt(freqs * count * sx * sy * sz)
     assert wy == LANES and depth * wx == LANES and 1 < sx <= 4 and sy > 1 and sz > 1
@@ -743,16 +744,15 @@
         name="source_own",
     )(waves, mine, *in_hbm(e_field, h_field))
     e_near, h_near = in_vmem(e_near, h_near)
-    with jax.named_scope("source_all"):
-        keep, send = pl.pallas_call(
-            source_kernel(freqs, depth, wx, half, sizes, zslots, xslots, scale, zbits, True),
-            out_shape=(part_shape, part_shape),
-            in_specs=[vmem] * (4 + zbits),
-            out_specs=(vmem, vmem),
-            scratch_shapes=tables + [sums, sums],
-            compiler_params=medium,
-            name="source_both",
-        )(waves, *in_vmem(theirs, *own), *zs)
+    keep, send = pl.pallas_call(
+        source_kernel(freqs, depth, wx, half, sizes, zslots, xslots, scale, zbits, True),
+        out_shape=(part_shape, part_shape),
+        in_specs=[vmem] * (4 + zbits),
+        out_specs=(vmem, vmem),
+        scratch_shapes=tables + [sums, sums],
+        compiler_params=medium,
+        name="source_both",
+    )(waves, *in_vmem(theirs, *own), *zs)
 
     strip = pltpu.VMEM((8, LANES), f32)
     first, last = pl.pallas_call(
@@ -766,7 +766,7 @@
 
     whole = jax.ShapeDtypeStruct((3, depth, wx, wy), f32)
     pole_next, base_e, coef = pl.pallas_call(
-        pole_kernel(depth, wx, wy),
+        pole_kernel(),
         out_shape=(whole, pltpu.VMEM(whole.shape, f32), pltpu.VMEM((depth, wx, wy), f32)),
         in_specs=[hbm, vmem, hbm, hbm, vmem],
         out_specs=(hbm, vmem, vmem),
@@ -813,7 +813,7 @@
         plain, laden = pltpu.VMEM((size, LANES), f32), pltpu.VMEM((size + 8, LANES), f32)
         shapes = (plain, laden, laden, plain) if both else (plain, laden)
         keep, *away = pl.pallas_call(
-            merge_y_kernel(len(terms), rows, k, ybits),
+            merge_y_kernel(len(terms), rows, k),
             out_shape=shapes,
             in_specs=[vmem] * (len(terms) + 2),
             out_specs=(vmem,) * len(shapes),
@@ -896,4 +896,6 @@
         P(),
     )
     out_specs = (P(None, "gz", "gx", "gy"), P(None, "gz", "gx", "gy"), P(None, "gz", "gx", "gy"))
-    return jax.shard_map(local, mesh=mesh, in_specs=in_specs, out_specs=out_specs, check_vma=False)
+    return jax.shard_map(
+        local, mesh=mesh, in_specs=in_specs, out_specs=out_specs, check_vma=False
+    )

time: 28.7 us -> 28.7 us (level)
  no operation moved by 1% of the time
where the time goes in v8:
time: 28.7 us; the launch traced here: 28.5 us
  starting transfers between devices  11.6 us (40%)
  Pallas kernels  9.94 us (35%)
  waiting for transfers between devices  6.27 us (22%)
  between operations  0.69 us (2%)
    ppermute x8, starting transfers between devices, exchange(): lax.ppermute(array, axis, [(i, i ^ mask) for i in range(lax.axis_size(axi...  11.6 us
    ppermute x8, waiting for transfers between devices, exchange(): lax.ppermute(array, axis, [(i, i ^ mask) for i in range(lax.axis_size(axi...  6.27 us
    pallas_call x2, Pallas kernels, local(): pl.pallas_call(source_kernel(freqs, depth, wx, half, sizes, zslots, xslot...  5.32 us
    pallas_call x1, Pallas kernels, local(): pl.pallas_call(pole_kernel(), out_shape=(whole, pltpu.VMEM(whole.shape, f...  1.72 us
    pallas_call x1, Pallas kernels, local(): pl.pallas_call(inject_kernel(depth, wx, wy, sy, sz, per, zcut), out_shape...  1.02 us
    pallas_call x1, Pallas kernels, local(): pl.pallas_call(pack_kernel(freqs, depth, wx, zbits), out_shape=[pltpu.VME...  1.01 us
  transfers between devices with their start and end apart: 8, of which 5 were waited for; matrix products, arithmetic and copies ran while one was open for 0% of the time, Pallas kernels for 18%

profile of v8, /device:TPU:1, one launch (start us, length us, event | category | flops | bytes accessed | tf_op | source)
XLA Modules:
  0.0 28.5 jit_solution(15443041616414803480)
XLA Ops:
  0.6 1.0 %pack.1 = (f32[20,8,128]{2,1,0:T(8,128)S(1)}, f32[2,16,128]{2,1,0:T(8,128)S(1)}, f32[6,32,128]{2,1,0:T(8,128)S(1)}) custom-call(f32[3,4,32,128]{3,2,1,0:T(8,128)} %refs_2_.3, f32[3,4,32,128]{3,2,1,0:T(8,128)} %refs_3_.3, f32[16,8,128]{2,1,0:T(8,128)} %refs_2_.2, f32[2,128]{1,0:T(2,128)} %refs_3_.2, f32[16]{0:T(128)} %refs_4_.1, f32[16]{0:T(128)} %refs_5_.1), custom_call_target="tpu_custom_call" | custom-call | tf_op jit(solution)/shard_map/pack/pallas_call | solution.py:701
  1.6 0.1 collective-permute-start.1
  1.7 2.8 %collective-permute-start = (f32[20,8,128]{2,1,0:T(8,128)S(1)}, f32[20,8,128]{2,1,0:T(8,128)S(1)}, u32[]{:S(2)}, u32[]{:S(2)}) collective-permute-start(f32[20,8,128]{2,1,0:T(8,128)S(1)} %get-tuple-element.28.refs_1_), channel_id=1, source_target_pairs={{0,8},{8,0},{16,24},{24,16},{1,9},{9,1},{17,25},{25,17},{2,10},{10... | collective-permute-start | bytes 245768 | tf_op jit(solution)/shard_map/ppermute | solution.py:19
  4.5 2.6 %source_own.1 = (f32[272,256]{1,0:T(8,128)S(1)}, f32[272,256]{1,0:T(8,128)S(1)}, f32[3,4,32,128]{3,2,1,0:T(8,128)S(1)}, f32[3,4,32,128]{3,2,1,0:T(8,128)S(1)}) custom-call(f32[2,16,128]{2,1,0:T(8,128)S(1)} %get-tuple-element.27.refs_0_, f32[20,8,128]{2,1,0:T(8,128)S(1)} %get-tuple-element.28.refs_1_, f32[3,4,32,128]{3,2,1,0:T(8,128)} %refs_2_.3, ...), custom_call_target="tpu_custom_call" | custom-call | tf_op jit(solution)/shard_map/source_own/pallas_call | solution.py:737
  7.1 0.1 collective-permute-done.refs_1_.refs_2_.refs_5_
  7.2 0.0 collective-permute-done.1.refs_4_.refs_3_.refs_6_
  7.2 2.7 %source_both.1 = (f32[1,4,136,128]{3,2,1,0:T(8,128)S(1)}, f32[1,4,136,128]{3,2,1,0:T(8,128)S(1)}) custom-call(f32[2,16,128]{2,1,0:T(8,128)S(1)} %get-tuple-element.27.refs_0_, f32[20,8,128]{2,1,0:T(8,128)S(1)} %collective-permute-done.refs_1_.refs_2_.refs_5_, f32[272,256]{1,0:T(8,128)S(1)} %get-tuple-element.29.refs_2_, ...), custom_call_target="tpu_custom_call" | custom-call | tf_op jit(solution)/shard_map/source_both/pallas_call | solution.py:747
  10.0 0.7 %collective-permute-start.2 = (f32[1,4,136,128]{3,2,1,0:T(8,128)S(1)}, f32[1,4,136,128]{3,2,1,0:T(8,128)S(1)}, u32[]{:S(2)}, u32[]{:S(2)}) collective-permute-start(f32[1,4,136,128]{3,2,1,0:T(8,128)S(1)} %get-tuple-element.33), channel_id=1, source_target_pairs={{0,1},{1,0},{2,3},{3,2},{4,5},{5,4},{6,7},{7,6},{8,9},{9,8},{10,11... | collective-permute-start | bytes 835592 | tf_op jit(solution)/shard_map/ppermute | solution.py:19
  10.7 0.2 columns.1
  10.9 0.9 %collective-permute-done.2 = f32[1,4,136,128]{3,2,1,0:T(8,128)S(1)} collective-permute-done((f32[1,4,136,128]{3,2,1,0:T(8,128)S(1)}, f32[1,4,136,128]{3,2,1,0:T(8,128)S(1)}, u32[]{:S(2)}, u32[]{:S(2)}) %collective-permute-start.2) | collective-permute-done | bytes 278560 | tf_op jit(solution)/shard_map/ppermute | solution.py:19
  11.9 1.4 %collective-permute-start.3 = (f32[144,128]{1,0:T(8,128)S(1)}, f32[144,128]{1,0:T(8,128)S(1)}, u32[]{:S(2)}, u32[]{:S(2)}) collective-permute-start(f32[144,128]{1,0:T(8,128)S(1)} %get-tuple-element.39), channel_id=1, source_target_pairs={{0,2},{2,0},{4,6},{6,4},{1,3},{3,1},{5,7},{7,5},{8,10},{10,8},{12,... | collective-permute-start | bytes 221192 | tf_op jit(solution)/shard_map/ppermute | solution.py:19
  13.3 1.2 %collective-permute-start.4 = (f32[144,128]{1,0:T(8,128)S(1)}, f32[144,128]{1,0:T(8,128)S(1)}, u32[]{:S(2)}, u32[]{:S(2)}) collective-permute-start(f32[144,128]{1,0:T(8,128)S(1)} %get-tuple-element.40), channel_id=1, source_target_pairs={{0,6},{2,4},{4,2},{6,0},{1,7},{3,5},{5,3},{7,1},{8,14},{10,12},{12... | collective-permute-start | bytes 221192 | tf_op jit(solution)/shard_map/ppermute | solution.py:19
  14.6 0.1 collective-permute-start.5
  14.6 1.7 %pole.1 = (f32[3,4,32,128]{3,2,1,0:T(8,128)}, f32[3,4,32,128]{3,2,1,0:T(8,128)S(1)}, f32[4,32,128]{2,1,0:T(8,128)S(1)}) custom-call(f32[3,4]{1,0:T(4,128)} %table_in.1, f32[3,4,32,128]{3,2,1,0:T(8,128)S(1)} %get-tuple-element.34.refs_0_.e.refs_4_, f32[3,4,32,128]{3,2,1,0:T(8,128)} %pole_in.1, s32[4,32,128]{2,1,0:T(8,128)} %material_in.1, ...), custom_call_target="tpu_custom_call" | custom-call | tf_op jit(solution)/shard_map/pole/pallas_call | solution.py:768
  16.4 3.4 %collective-permute-done.5.refs_3_ = f32[136,128]{1,0:T(8,128)S(1)} collective-permute-done((f32[136,128]{1,0:T(8,128)S(1)}, f32[136,128]{1,0:T(8,128)S(1)}, u32[]{:S(2)}, u32[]{:S(2)}) %collective-permute-start.5) | collective-permute-done | bytes 69664 | tf_op jit(solution)/shard_map/ppermute | solution.py:19
  19.8 0.0 collective-permute-done.3.refs_1_.refs_7_
  19.8 0.0 collective-permute-done.4.refs_2_.refs_8_
  19.8 3.4 %collective-permute-start.6 = (f32[96,128]{1,0:T(8,128)S(1)}, f32[96,128]{1,0:T(8,128)S(1)}, u32[]{:S(2)}, u32[]{:S(2)}) collective-permute-start(f32[96,128]{1,0:T(8,128)S(1)} %get-tuple-element.44), channel_id=1, source_target_pairs={{0,24},{8,16},{16,8},{24,0},{1,25},{9,17},{17,9},{25,1},{2,26},{10... | collective-permute-start | bytes 147464 | tf_op jit(solution)/shard_map/ppermute | solution.py:19
  23.2 1.5 %collective-permute-done.6.refs_9_ = f32[96,128]{1,0:T(8,128)S(1)} collective-permute-done((f32[96,128]{1,0:T(8,128)S(1)}, f32[96,128]{1,0:T(8,128)S(1)}, u32[]{:S(2)}, u32[]{:S(2)}) %collective-permute-start.6) | collective-permute-done | bytes 49184 | tf_op jit(solution)/shard_map/ppermute | solution.py:19
  24.7 1.9 %collective-permute-start.7 = (f32[72,128]{1,0:T(8,128)S(1)}, f32[72,128]{1,0:T(8,128)S(1)}, u32[]{:S(2)}, u32[]{:S(2)}) collective-permute-start(f32[72,128]{1,0:T(8,128)S(1)} %slice_add_fusion.refs_1_), channel_id=1, source_target_pairs={{0,1},{1,0},{2,3},{3,2},{4,5},{5,4},{6,7},{7,6},{8,9},{9,8},{10,11... | collective-permute-start | bytes 110600 | tf_op jit(solution)/shard_map/ppermute | solution.py:19
  26.6 0.6 %fields.1 = (f32[3,4,32,128]{3,2,1,0:T(8,128)S(1)}, f32[3,4,32,128]{3,2,1,0:T(8,128)S(1)}) custom-call(f32[3,4,32,128]{3,2,1,0:T(8,128)S(1)} %get-tuple-element.34.refs_0_.e.refs_4_, f32[3,4,32,128]{3,2,1,0:T(8,128)S(1)} %get-tuple-element.35.refs_1_.refs_5_, f32[3,4,32,128]{3,2,1,0:T(8,128)S(1)} %get-tuple-element.45.refs_2_, ...), custom_call_target="tpu_custom_call" | custom-call | tf_op jit(solution)/shard_map/fields/pallas_call | solution.py:856
  27.2 0.3 %collective-permute-done.7.refs_0_ = f32[72,128]{1,0:T(8,128)S(1)} collective-permute-done((f32[72,128]{1,0:T(8,128)S(1)}, f32[72,128]{1,0:T(8,128)S(1)}, u32[]{:S(2)}, u32[]{:S(2)}) %collective-permute-start.7) | collective-permute-done | bytes 36896 | tf_op jit(solution)/shard_map/ppermute | solution.py:19
  27.5 1.0 %inject.1 = (f32[3,4,32,128]{3,2,1,0:T(8,128)}, f32[3,4,32,128]{3,2,1,0:T(8,128)}) custom-call(f32[72,128]{1,0:T(8,128)S(1)} %collective-permute-done.7.refs_0_, f32[72,128]{1,0:T(8,128)S(1)} %slice_add_fusion.refs_1_, f32[3,4,32,128]{3,2,1,0:T(8,128)S(1)} %get-tuple-element.46.refs_2_, f32[3,4,32,128]{3,2,1,0:T(8,128)S(1)} %get-tuple-element.47.refs_3_, ...), custom_call_target="tpu_custom_call" | custom-call | tf_op jit(solution)/shard_map/inject/pallas_call | solution.py:870
  (3 shorter events, 0.1 us)
Async XLA Ops:
  1.6 5.6 %collective-permute-start.1 = (f32[6,32,128]{2,1,0:T(8,128)S(1)}, f32[6,32,128]{2,1,0:T(8,128)S(1)}, u32[]{:S(2)}, u32[]{:S(2)}) collective-permute-start(f32[6,32,128]{2,1,0:T(8,128)S(1)} %get-tuple-element.31), channel_id=1, source_target_pairs={{0,1},{1,0},{2,3},{3,2},{4,5},{5,4},{6,7},{7,6},{8,9},{9,8},{10,11... | collective-permute-start | bytes 294920 | tf_op jit(solution)/shard_map/ppermute | solution.py:19
  1.7 5.5 %collective-permute-start = (f32[20,8,128]{2,1,0:T(8,128)S(1)}, f32[20,8,128]{2,1,0:T(8,128)S(1)}, u32[]{:S(2)}, u32[]{:S(2)}) collective-permute-start(f32[20,8,128]{2,1,0:T(8,128)S(1)} %get-tuple-element.28.refs_1_), channel_id=1, source_target_pairs={{0,8},{8,0},{16,24},{24,16},{1,9},{9,1},{17,25},{25,17},{2,10},{10... | collective-permute-start | bytes 245768 | tf_op jit(solution)/shard_map/ppermute | solution.py:19
  10.0 1.9 %collective-permute-start.2 = (f32[1,4,136,128]{3,2,1,0:T(8,128)S(1)}, f32[1,4,136,128]{3,2,1,0:T(8,128)S(1)}, u32[]{:S(2)}, u32[]{:S(2)}) collective-permute-start(f32[1,4,136,128]{3,2,1,0:T(8,128)S(1)} %get-tuple-element.33), channel_id=1, source_target_pairs={{0,1},{1,0},{2,3},{3,2},{4,5},{5,4},{6,7},{7,6},{8,9},{9,8},{10,11... | collective-permute-start | bytes 835592 | tf_op jit(solution)/shard_map/ppermute | solution.py:19
  11.9 7.9 %collective-permute-start.3 = (f32[144,128]{1,0:T(8,128)S(1)}, f32[144,128]{1,0:T(8,128)S(1)}, u32[]{:S(2)}, u32[]{:S(2)}) collective-permute-start(f32[144,128]{1,0:T(8,128)S(1)} %get-tuple-element.39), channel_id=1, source_target_pairs={{0,2},{2,0},{4,6},{6,4},{1,3},{3,1},{5,7},{7,5},{8,10},{10,8},{12,... | collective-permute-start | bytes 221192 | tf_op jit(solution)/shard_map/ppermute | solution.py:19
  13.3 6.4 %collective-permute-start.4 = (f32[144,128]{1,0:T(8,128)S(1)}, f32[144,128]{1,0:T(8,128)S(1)}, u32[]{:S(2)}, u32[]{:S(2)}) collective-permute-start(f32[144,128]{1,0:T(8,128)S(1)} %get-tuple-element.40), channel_id=1, source_target_pairs={{0,6},{2,4},{4,2},{6,0},{1,7},{3,5},{5,3},{7,1},{8,14},{10,12},{12... | collective-permute-start | bytes 221192 | tf_op jit(solution)/shard_map/ppermute | solution.py:19
  14.6 5.2 %collective-permute-start.5 = (f32[136,128]{1,0:T(8,128)S(1)}, f32[136,128]{1,0:T(8,128)S(1)}, u32[]{:S(2)}, u32[]{:S(2)}) collective-permute-start(f32[136,128]{1,0:T(8,128)S(1)} %get-tuple-element.41), channel_id=1, source_target_pairs={{0,4},{2,6},{4,0},{6,2},{1,5},{3,7},{5,1},{7,3},{8,12},{10,14},{12... | collective-permute-start | bytes 208904 | tf_op jit(solution)/shard_map/ppermute | solution.py:19
  19.8 4.9 %collective-permute-start.6 = (f32[96,128]{1,0:T(8,128)S(1)}, f32[96,128]{1,0:T(8,128)S(1)}, u32[]{:S(2)}, u32[]{:S(2)}) collective-permute-start(f32[96,128]{1,0:T(8,128)S(1)} %get-tuple-element.44), channel_id=1, source_target_pairs={{0,24},{8,16},{16,8},{24,0},{1,25},{9,17},{17,9},{25,1},{2,26},{10... | collective-permute-start | bytes 147464 | tf_op jit(solution)/shard_map/ppermute | solution.py:19
  24.7 2.8 %collective-permute-start.7 = (f32[72,128]{1,0:T(8,128)S(1)}, f32[72,128]{1,0:T(8,128)S(1)}, u32[]{:S(2)}, u32[]{:S(2)}) collective-permute-start(f32[72,128]{1,0:T(8,128)S(1)} %slice_add_fusion.refs_1_), channel_id=1, source_target_pairs={{0,1},{1,0},{2,3},{3,2},{4,5},{5,4},{6,7},{7,6},{8,9},{9,8},{10,11... | collective-permute-start | bytes 110600 | tf_op jit(solution)/shard_map/ppermute | solution.py:19
